TPU v7x, 32 devices: a whole 2x2x4 slice. The times are simulated.
32 devices in a mesh: rep: 4 (over x, core), ctx: 8 (over z, y).
Axes of the slice: x: 2, y: 2, z: 4, core: 2. Of those that a mesh axis runs over, the one named last changes fastest.
Arguments:
- block_in: bfloat16 [2, 4, 1024, 1024], P(None, 'rep', 'ctx'), may hold values from -6 to 6
- lengths: int32 [2, 4], P(None, 'rep'), may hold values from 1024 to 1024, as said below
- norm_gains: bfloat16 [2, 1024], P(None, 'ctx'), may hold values from 0.5 to 1.5
- w_in: bfloat16 [1024, 6144], P('ctx'), may hold values from -0.1875 to 0.1875
- w_small: bfloat16 [1024, 24], P('ctx'), may hold values from -0.1875 to 0.1875
- conv_weight: bfloat16 [4, 5120], P(None, 'ctx'), may hold values from -3 to 3
- decay_log: float32 [8], replicated, may hold values from 0 to 2.7726
- decay_bias: float32 [8], replicated, may hold values from -6.9073 to -2.2521
- out_norm_gain: float32 [128], replicated, may hold values from 0.5 to 1.5
- w_out: bfloat16 [1024, 1024], P('ctx'), may hold values from -0.375 to 0.375
- gate_up_weight: bfloat16 [1024, 5632], P('ctx'), may hold values from -0.1875 to 0.1875
- w_down: bfloat16 [2816, 1024], P('ctx'), may hold values from -0.21875 to 0.21875
- out_cotangent: bfloat16 [2, 4, 1024, 1024], P(None, 'rep', 'ctx'), may hold values from -6 to 6
Outputs:
- block_out: bfloat16 [2, 4, 1024, 1024], P(None, 'rep', 'ctx')
- in_grad: bfloat16 [2, 4, 1024, 1024], P(None, 'rep', 'ctx')
- grad_norm_gains: float32 [2, 1024], P(None, 'ctx')
- grad_w_in: float32 [1024, 6144], P('ctx')
- grad_w_small: float32 [1024, 24], P('ctx')
- grad_conv_weight: float32 [4, 5120], P(None, 'ctx')
- grad_decay_log: float32 [8], replicated
- grad_decay_bias: float32 [8], replicated
- grad_out_norm_gain: float32 [128], replicated
- grad_w_out: float32 [1024, 1024], P('ctx')
- grad_w_gate_up: float32 [1024, 5632], P('ctx')
- grad_w_down: float32 [2816, 1024], P('ctx')
Inputs may be any that keep to these rules, and one draw needn't show every extreme that they name: `lengths`: in each micro-batch, one of its 4 sequences has length 1024 and another has length min(1024, 1024).
All inputs are finite; a program needn't handle non-finite values.
Results may differ from a plain program's by a relative error of at most 0.017.
Values may be sent and summed in bfloat16 or wider, within the bound.
A program may use at most 448 MiB of HBM per device.

v0:
```python
import jax
import jax.numpy as jnp
from jax import lax
from jax.sharding import PartitionSpec as P

STEPS = 2
CONV = 4
STRETCH = 64


EPS = 1e-06
HIGH_PRECISION = lax.Precision.HIGHEST


def from_behind(value, axis, steps):
    count = lax.axis_size(axis)
    first, last = (max(0, -steps), min(count, count - steps))
    return lax.ppermute(value, axis, [(source, source + steps) for source in range(first, last)])


def prefix(value, axis, join, neutral):
    count, mine = (lax.axis_size(axis), lax.axis_index(axis))
    pieces = jax.tree.map(lambda part: lax.all_gather(part, axis), value)
    running = jax.tree.map(
        lambda part, zero: jnp.full_like(part, 0) + jnp.asarray(zero, part.dtype), value, neutral
    )

    def prefix_turn(position, running):
        longer = join(running, jax.tree.map(lambda part: part[position], pieces))
        return jax.tree.map(lambda new, old: jnp.where(position < mine, new, old), longer, running)

    return lax.fori_loop(0, count - 1, prefix_turn, running)


def carried_in(array, axis, combine, identity):
    size, mine = (lax.axis_size(axis), lax.axis_index(axis))
    everything = jax.tree.map(
        lambda part, kind: lax.all_gather(part.astype(kind), axis),
        array,
        jax.tree.map(lambda a: jnp.bfloat16 if a.dtype == jnp.float32 else a.dtype, array),
    )
    start = jax.tree.map(
        lambda part, zero: jnp.broadcast_to(jnp.asarray(zero, part.dtype), part.shape),
        array,
        identity,
    )

    def carried_turn(k, before):
        at = size - 1 - k
        reached = at > mine
        new = combine(
            before, jax.tree.map(lambda part, own: part[at].astype(own.dtype), everything, array)
        )
        return jax.tree.map(lambda a, b: jnp.where(reached, a, b), new, before)

    return lax.fori_loop(0, size, carried_turn, start)


def matmul(left, right):
    return jnp.dot(left, right, preferred_element_type=jnp.float32)


def times_transposed(left, right):
    return lax.dot_general(
        left, right, (((1,), (1,)), ((), ())), preferred_element_type=jnp.float32
    )


def transposed_times(left, right):
    return lax.dot_general(
        left, right, (((0,), (0,)), ((), ())), preferred_element_type=jnp.float32
    )


def batched(form, left, right):
    return jnp.einsum(form, left, right, precision=HIGH_PRECISION)


def rms_gain(values, gain):
    return values * lax.rsqrt(jnp.mean(values * values, axis=-1, keepdims=True) + EPS) * gain


def swiglu(gate_up):
    half_width = gate_up.shape[-1] // 2
    return jax.nn.silu(gate_up[:, :half_width]) * gate_up[:, half_width:]


def prepare(extended, small_proj, conv_weight, decay_log, decay_bias):
    seq_count, padded_len, channels = extended.shape
    tokens = padded_len - CONV + 1
    head_count = decay_log.shape[0]
    model_width = channels // (1 + 2 * STEPS)
    head_dim = model_width // head_count
    convolved = conv_weight[0] * extended[:, 0:tokens]
    for offset in range(1, CONV):
        convolved = convolved + conv_weight[offset] * extended[:, offset : offset + tokens]
    activated = jax.nn.silu(convolved)
    query_rows = activated[..., :model_width].reshape(seq_count, tokens, 1, head_count, head_dim)
    key_matrix_rows = activated[..., model_width : (1 + STEPS) * model_width].reshape(
        seq_count, tokens, STEPS, head_count, head_dim
    )
    key_matrix_rows = key_matrix_rows * lax.rsqrt(
        jnp.sum(key_matrix_rows * key_matrix_rows, axis=-1, keepdims=True) + EPS
    )
    value_rows = activated[..., (1 + STEPS) * model_width :].reshape(
        seq_count, tokens, STEPS, head_count, head_dim
    )
    beta_rates = jax.nn.sigmoid(small_proj[..., : STEPS * head_count]).reshape(
        seq_count, tokens, STEPS, head_count
    )
    log_decay = -jnp.exp(decay_log) * jax.nn.softplus(
        small_proj[..., STEPS * head_count :] + decay_bias
    )
    query_sub = jnp.concatenate(
        [jnp.zeros((seq_count, tokens, STEPS - 1, head_count, head_dim), jnp.float32), query_rows],
        axis=2,
    )
    decay_sub = jnp.concatenate(
        [log_decay[:, :, None], jnp.zeros((seq_count, tokens, STEPS - 1, head_count), jnp.float32)],
        axis=2,
    )

    def steps_last(array):
        moved = jnp.moveaxis(array, 3, 1)
        return moved.reshape((seq_count, head_count, tokens * STEPS) + array.shape[4:])

    return (
        steps_last(query_sub),
        steps_last(key_matrix_rows),
        steps_last(value_rows),
        steps_last(beta_rates),
        steps_last(decay_sub),
    )


def run_stretches(recurrent_state, query_rows, key_matrix_rows, value_rows, beta_rates, log_decay):
    seq_count, head_count, substeps, head_dim = key_matrix_rows.shape
    state_width = value_rows.shape[-1]
    span_len = STEPS * STRETCH
    block_count = substeps // span_len

    def blocked(array):
        return array.reshape((seq_count, head_count, block_count, span_len) + array.shape[3:])

    query_rows, key_matrix_rows, value_rows, beta_rates, log_decay = [
        blocked(a) for a in (query_rows, key_matrix_rows, value_rows, beta_rates, log_decay)
    ]
    cumulative = jnp.cumsum(log_decay, axis=-1)
    row_index = lax.broadcasted_iota(jnp.int32, (span_len, span_len), 0)
    col_index = lax.broadcasted_iota(jnp.int32, (span_len, span_len), 1)
    lower_inclusive_mask = row_index >= col_index
    lower_strict = row_index > col_index
    decay_gaps = cumulative[..., :, None] - cumulative[..., None, :]
    decay_inside = jnp.where(
        lower_inclusive_mask, jnp.exp(jnp.where(lower_inclusive_mask, decay_gaps, 0.0)), 0.0
    )
    intersections = batched("...sk,...rk->...sr", key_matrix_rows, key_matrix_rows)
    system = jnp.where(
        lower_strict, beta_rates[..., :, None] * intersections * decay_inside, 0.0
    ) + jnp.eye(span_len, dtype=jnp.float32)
    scaled_keys = key_matrix_rows * jnp.exp(cumulative)[..., None]
    right_side = beta_rates[..., None] * jnp.concatenate([scaled_keys, value_rows], axis=-1)
    solved = jax.scipy.linalg.solve_triangular(system, right_side, lower=True, unit_diagonal=True)
    key_weights = solved[..., :head_dim]
    base_values = solved[..., head_dim:]
    scores = jnp.where(
        lower_inclusive_mask,
        batched("...sk,...rk->...sr", query_rows, key_matrix_rows) * decay_inside,
        0.0,
    )
    scaled_queries = query_rows * jnp.exp(cumulative)[..., None]
    to_end = key_matrix_rows * jnp.exp(cumulative[..., -1:] - cumulative)[..., None]
    carried = jnp.exp(cumulative[..., -1])
    outputs = []
    for block_index in range(block_count):
        fresh_values = base_values[:, :, block_index] - batched(
            "...sk,...kw->...sw", key_weights[:, :, block_index], recurrent_state
        )
        outputs.append(
            batched("...sk,...kw->...sw", scaled_queries[:, :, block_index], recurrent_state)
            + batched("...sr,...rw->...sw", scores[:, :, block_index], fresh_values)
        )
        recurrent_state = carried[:, :, block_index, None, None] * recurrent_state + batched(
            "...sk,...sw->...kw", to_end[:, :, block_index], fresh_values
        )
    return (
        jnp.stack(outputs, axis=2).reshape(seq_count, head_count, substeps, state_width),
        recurrent_state,
    )


def finish(sub_out, gate_z, out_gain):
    seq_count, head_count, substeps, head_dim = sub_out.shape
    tokens = substeps // STEPS
    last_sub = sub_out.reshape(seq_count, head_count, tokens, STEPS, head_dim)[:, :, :, STEPS - 1]
    last_sub = jnp.moveaxis(last_sub, 1, 2)
    gate_heads = gate_z.reshape(seq_count, tokens, head_count, head_dim)
    normed = (
        last_sub
        * lax.rsqrt(jnp.mean(last_sub * last_sub, axis=-1, keepdims=True) + EPS)
        * out_gain
        * jax.nn.silu(gate_heads)
    )
    return normed.reshape(seq_count, tokens, head_count * head_dim)


def chain_forward(earlier_part, later_part):
    return (
        batched("...ij,...jk->...ik", later_part[0], earlier_part[0]),
        batched("...ij,...jk->...ik", later_part[0], earlier_part[1]) + later_part[1],
    )


def chain_backward(earlier_part, later_part):
    return (
        batched("...ij,...jk->...ik", earlier_part[0], later_part[0]),
        batched("...ji,...jk->...ik", later_part[0], earlier_part[1]) + later_part[1],
    )


def per_device(
    block_in,
    lengths,
    norm_gains,
    w_in,
    w_small,
    conv_weight,
    decay_log,
    decay_bias,
    out_norm_gain,
    w_out,
    gate_up_weight,
    w_down,
    out_cotangent,
):
    micro_count, seq_count, tokens, model_width = block_in.shape
    head_count = decay_log.shape[0]
    head_dim = out_norm_gain.shape[0]
    channels = (1 + 2 * STEPS) * model_width
    rim_rows = CONV - 1
    flat_rows = seq_count * tokens
    places = lax.axis_index("ctx") * tokens + lax.broadcasted_iota(
        jnp.int32, (seq_count, tokens), 1
    )
    identity_state = jnp.broadcast_to(
        jnp.eye(head_dim, dtype=jnp.float32), (seq_count, head_count, head_dim, head_dim)
    )
    zero_state = jnp.zeros((seq_count, head_count, head_dim, head_dim), jnp.float32)
    results = []
    in_grads = []
    grad_sums = None
    small_sums = None
    for batch_index in range(micro_count):
        front_weights = (
            lax.all_gather(norm_gains, "ctx", axis=1, tiled=True),
            lax.all_gather(w_in, "ctx", axis=0, tiled=True),
            lax.all_gather(w_small, "ctx", axis=0, tiled=True),
            lax.all_gather(conv_weight, "ctx", axis=1, tiled=True),
            lax.all_gather(w_out, "ctx", axis=0, tiled=True),
            lax.all_gather(gate_up_weight, "ctx", axis=0, tiled=True),
            lax.all_gather(w_down, "ctx", axis=0, tiled=True),
        )
        gain_pair = front_weights[0].astype(jnp.float32)
        valid_rows = (
            (places < lengths[batch_index][:, None]).astype(jnp.float32).reshape(flat_rows, 1)
        )
        inputs = block_in[batch_index].astype(jnp.float32).reshape(flat_rows, model_width)
        first_norm, pull_first = jax.vjp(rms_gain, inputs, gain_pair[0])
        h_first = first_norm.astype(jnp.bfloat16)
        projected = matmul(h_first, front_weights[1]).reshape(seq_count, tokens, -1)
        small_proj = matmul(h_first, front_weights[2])
        edge_rows = from_behind(projected[:, tokens - rim_rows :, :channels], "ctx", 1)
        extended = jnp.concatenate([edge_rows, projected[:, :, :channels]], axis=1)
        prepared, pull_prep = jax.vjp(
            prepare,
            extended,
            small_proj.reshape(seq_count, tokens, -1),
            front_weights[3].astype(jnp.float32),
            decay_log,
            decay_bias,
        )
        query_rows, key_matrix_rows, value_rows, beta_rates, log_decay = prepared
        start_pair = jnp.concatenate([zero_state, identity_state], axis=-1)
        value_pair = jnp.concatenate([value_rows, jnp.zeros_like(value_rows)], axis=-1)
        end_states = run_stretches(
            start_pair, query_rows, key_matrix_rows, value_pair, beta_rates, log_decay
        )[1]
        offsets = end_states[..., :head_dim]
        transfers = end_states[..., head_dim:]
        prefix_states = prefix(
            (transfers, offsets), "ctx", chain_forward, (identity_state, zero_state)
        )
        incoming = prefix_states[1]
        stretch_result, pull_stretches = jax.vjp(
            run_stretches, incoming, query_rows, key_matrix_rows, value_rows, beta_rates, log_decay
        )
        mixed_out, pull_finish = jax.vjp(
            finish, stretch_result[0], projected[:, :, channels:], out_norm_gain
        )
        mixer = mixed_out.reshape(flat_rows, model_width).astype(jnp.bfloat16)
        resid = inputs + matmul(mixer, front_weights[4])
        second_norm, pull_second = jax.vjp(rms_gain, resid, gain_pair[1])
        h_second = second_norm.astype(jnp.bfloat16)
        gate_up = matmul(h_second, front_weights[5])
        hidden_full, pull_swiglu = jax.vjp(swiglu, gate_up)
        hidden = hidden_full.astype(jnp.bfloat16)
        result = resid + matmul(hidden, front_weights[6])
        results.append(
            (valid_rows * result).astype(jnp.bfloat16).reshape(seq_count, tokens, model_width)
        )
        back_weights = (
            lax.all_gather(norm_gains, "ctx", axis=1, tiled=True),
            lax.all_gather(w_in, "ctx", axis=0, tiled=True),
            lax.all_gather(w_small, "ctx", axis=0, tiled=True),
            lax.all_gather(conv_weight, "ctx", axis=1, tiled=True),
            lax.all_gather(w_out, "ctx", axis=0, tiled=True),
            lax.all_gather(gate_up_weight, "ctx", axis=0, tiled=True),
            lax.all_gather(w_down, "ctx", axis=0, tiled=True),
        )
        grad_out = (
            out_cotangent[batch_index].astype(jnp.float32).reshape(flat_rows, model_width)
            * valid_rows
        ).astype(jnp.bfloat16)
        grad_down = transposed_times(hidden, grad_out)
        d_hidden = times_transposed(grad_out, back_weights[6])
        d_gate_up = pull_swiglu(d_hidden)[0].astype(jnp.bfloat16)
        grad_gate_up = transposed_times(h_second, d_gate_up)
        d_second = times_transposed(d_gate_up, back_weights[5])
        d_resid_norm, grad_gain_second = pull_second(d_second)
        d_resid = grad_out.astype(jnp.float32) + d_resid_norm
        d_branch = d_resid.astype(jnp.bfloat16)
        grad_out_proj = transposed_times(mixer, d_branch)
        d_mixer = times_transposed(d_branch, back_weights[4])
        d_sub, d_gate_z, grad_out_gain = pull_finish(
            d_mixer.reshape(seq_count, tokens, model_width)
        )
        local_grad = pull_stretches((d_sub, jnp.zeros_like(incoming)))[0]
        later_states = carried_in(
            (transfers, local_grad), "ctx", chain_backward, (identity_state, zero_state)
        )
        stretch_grads = pull_stretches((d_sub, later_states[1]))
        d_ext, d_small, grad_conv, grad_decay_log, grad_decay_bias = pull_prep(
            tuple(stretch_grads[1:])
        )
        spill_rows = from_behind(d_ext[:, :rim_rows].astype(jnp.bfloat16), "ctx", -1).astype(
            jnp.float32
        )
        d_conv_part = d_ext[:, rim_rows:] + jnp.concatenate(
            [jnp.zeros((seq_count, tokens - rim_rows, channels), jnp.float32), spill_rows], axis=1
        )
        d_proj = (
            jnp.concatenate([d_conv_part, d_gate_z], axis=-1)
            .reshape(flat_rows, -1)
            .astype(jnp.bfloat16)
        )
        d_small_low = d_small.reshape(flat_rows, -1).astype(jnp.bfloat16)
        grad_in_proj = transposed_times(h_first, d_proj)
        grad_small_proj = transposed_times(h_first, d_small_low)
        d_first = times_transposed(d_proj, back_weights[1]) + times_transposed(
            d_small_low, back_weights[2]
        )
        d_inputs, grad_gain_first = pull_first(d_first)
        in_grads.append(
            (d_resid + d_inputs).astype(jnp.bfloat16).reshape(seq_count, tokens, model_width)
        )
        batch_terms = (
            jnp.stack([grad_gain_first, grad_gain_second]),
            grad_in_proj,
            grad_small_proj,
            grad_conv,
            grad_out_proj,
            grad_gate_up,
            grad_down,
        )
        small_terms = (grad_decay_log, grad_decay_bias, grad_out_gain)
        if batch_index == 0:
            grad_sums = batch_terms
            small_sums = small_terms
        else:
            grad_sums = tuple((left + right for left, right in zip(grad_sums, batch_terms)))
            small_sums = tuple((left + right for left, right in zip(small_sums, small_terms)))
    owned = (
        lax.psum_scatter(
            grad_sums[0].astype(jnp.bfloat16), "ctx", scatter_dimension=1, tiled=True
        ).astype(jnp.float32),
        lax.psum_scatter(
            grad_sums[1].astype(jnp.bfloat16), "ctx", scatter_dimension=0, tiled=True
        ).astype(jnp.float32),
        lax.psum_scatter(
            grad_sums[2].astype(jnp.bfloat16), "ctx", scatter_dimension=0, tiled=True
        ).astype(jnp.float32),
        lax.psum_scatter(
            grad_sums[3].astype(jnp.bfloat16), "ctx", scatter_dimension=1, tiled=True
        ).astype(jnp.float32),
        lax.psum_scatter(
            grad_sums[4].astype(jnp.bfloat16), "ctx", scatter_dimension=0, tiled=True
        ).astype(jnp.float32),
        lax.psum_scatter(
            grad_sums[5].astype(jnp.bfloat16), "ctx", scatter_dimension=0, tiled=True
        ).astype(jnp.float32),
        lax.psum_scatter(
            grad_sums[6].astype(jnp.bfloat16), "ctx", scatter_dimension=0, tiled=True
        ).astype(jnp.float32),
    )
    summed = (
        lax.psum(owned[0].astype(jnp.bfloat16), "rep").astype(jnp.float32),
        lax.psum(owned[1].astype(jnp.bfloat16), "rep").astype(jnp.float32),
        lax.psum(owned[2].astype(jnp.bfloat16), "rep").astype(jnp.float32),
        lax.psum(owned[3].astype(jnp.bfloat16), "rep").astype(jnp.float32),
        lax.psum(owned[4].astype(jnp.bfloat16), "rep").astype(jnp.float32),
        lax.psum(owned[5].astype(jnp.bfloat16), "rep").astype(jnp.float32),
        lax.psum(owned[6].astype(jnp.bfloat16), "rep").astype(jnp.float32),
    )
    shared = lax.psum((small_sums[0], small_sums[1], small_sums[2]), ("rep", "ctx"))
    return (
        jnp.stack(results),
        jnp.stack(in_grads),
        summed[0],
        summed[1],
        summed[2],
        summed[3],
        shared[0],
        shared[1],
        shared[2],
        summed[4],
        summed[5],
        summed[6],
    )


def solution(mesh):
    placed = (
        P(None, "rep", "ctx", None),
        P(None, "rep"),
        P(None, "ctx"),
        P("ctx", None),
        P("ctx", None),
        P(None, "ctx"),
        P(),
        P(),
        P(),
        P("ctx", None),
        P("ctx", None),
        P("ctx", None),
        P(None, "rep", "ctx", None),
    )
    return jax.shard_map(
        per_device,
        mesh=mesh,
        in_specs=placed,
        out_specs=(
            P(None, "rep", "ctx", None),
            P(None, "rep", "ctx", None),
            P(None, "ctx"),
            P("ctx", None),
            P("ctx", None),
            P(None, "ctx"),
            P(),
            P(),
            P(),
            P("ctx", None),
            P("ctx", None),
            P("ctx", None),
        ),
        check_vma=False,
    )
```

profile of v0, /device:TPU:8, one launch (start us, length us, event | category | flops | bytes accessed | tf_op | source)
XLA Modules:
  0.0 2219.2 jit_solution(16413604223705762989)
XLA Ops:
  8.0 18.1 all_gather.87
  26.1 28.5 %all_gather.89 = bf16[1024,24]{0,1:T(8,128)(2,1)S(1)} all-gather(bf16[128,24]{0,1:T(8,128)(2,1)} %param.34), channel_id=1, replica_groups=mesh['rep'=4,'ctx'=8] {'ctx'}, dimensions={0}, use_global_device_ids=true | all-gather | bytes 55296 | tf_op jit(solution)/shard_map/all_gather | solution.py:257
  60.5 29.5 %all_gather.86 = bf16[4,5120]{1,0:T(4,128)(2,1)S(1)} all-gather(bf16[4,640]{1,0:T(4,128)(2,1)S(1)} %copy-done.279), channel_id=1, replica_groups=mesh['rep'=4,'ctx'=8] {'ctx'}, dimensions={1}, use_global_device_ids=true | all-gather | bytes 46080 | tf_op jit(solution)/shard_map/all_gather | solution.py:258
  92.8 94.5 %all-gather.21.cloned.1.call-done = bf16[1024,6144]{1,0:T(8,128)(2,1)} async-done(((bf16[128,6144]{1,0:T(8,128)(2,1)}), bf16[1024,6144]{1,0:T(8,128)(2,1)}) %all-gather.21.cloned.1.call-update) | async-done | bytes 12582928 | tf_op jit(solution)/shard_map/all_gather | solution.py:256
  236.0 159.1 %custom-call.18 = f32[8,2,1,128,128]{3,4,2,1,0:T(8,128)} custom-call(f32[8,2,1,128,128]{4,3,2,1,0:T(8,128)} %get-tuple-element.827), custom_call_target="InvertDiagBlocksLowerTriangular" | custom-call | tf_op jit(solution)/shard_map/jit(_solve_triangular)/vmap(vmap())/triangular_solve | solution.py:163
  423.1 158.8 %custom-call.20 = f32[8,2,1,128,128]{3,4,2,1,0:T(8,128)} custom-call(f32[8,2,1,128,128]{4,3,2,1,0:T(8,128)} %get-tuple-element.828), custom_call_target="InvertDiagBlocksLowerTriangular" | custom-call | tf_op jit(solution)/shard_map/jit(_solve_triangular)/vmap(vmap())/triangular_solve | solution.py:163
  647.5 13.7 while.60
  681.5 73.7 %all-gather.35.cloned.1.call-done = f32[8,8,128,128]{3,2,1,0:T(8,128)} async-done(((f32[1,8,128,128]{3,2,1,0:T(8,128)}), f32[8,8,128,128]{3,2,1,0:T(8,128)}) %all-gather.35.cloned.1.call-update) | async-done | bytes 4194320 | tf_op jit(solution)/shard_map/all_gather | solution.py:23
  755.1 13.9 while.61
  790.1 15.2 all-gather.23.cloned.1.call-done
  808.3 159.6 %all-gather.25.cloned.1.call-done = bf16[1024,5632]{1,0:T(8,128)(2,1)} async-done(((bf16[128,5632]{1,0:T(8,128)(2,1)}), bf16[1024,5632]{1,0:T(8,128)(2,1)}) %all-gather.25.cloned.1.call-update) | async-done | bytes 11534352 | tf_op jit(solution)/shard_map/all_gather | solution.py:260
  980.0 81.5 %all-gather.27.cloned.1.call-done = bf16[2816,1024]{1,0:T(8,128)(2,1)} async-done(((bf16[352,1024]{1,0:T(8,128)(2,1)}), bf16[2816,1024]{1,0:T(8,128)(2,1)}) %all-gather.27.cloned.1.call-update) | async-done | bytes 5767184 | tf_op jit(solution)/shard_map/all_gather | solution.py:261
  1141.4 158.6 %custom-call.23 = f32[8,2,1,128,128]{3,4,2,1,0:T(8,128)} custom-call(f32[8,2,1,128,128]{4,3,2,1,0:T(8,128)} %get-tuple-element.826), custom_call_target="InvertDiagBlocksLowerTriangular" | custom-call | tf_op jit(solution)/shard_map/transpose(jvp(jit(_solve_triangular)))/vmap(vmap())/triangular_solve | solution.py:163
  1300.0 158.6 %custom-call.22 = f32[8,2,1,128,128]{3,4,2,1,0:T(8,128)} custom-call(f32[8,2,1,128,128]{4,3,2,1,0:T(8,128)} %get-tuple-element.825), custom_call_target="InvertDiagBlocksLowerTriangular" | custom-call | tf_op jit(solution)/shard_map/transpose(jvp(jit(_solve_triangular)))/vmap(vmap())/triangular_solve | solution.py:163
  1487.0 14.1 add_convert_fusion.1
  1501.2 13.1 while.63
  1524.9 13.2 while.62
  1700.7 14.8 add_convert_fusion
  1763.6 159.4 %reduce-scatter.14.cloned.1.call-done = bf16[128,6144]{1,0:T(8,128)(2,1)} async-done(((bf16[1024,6144]{1,0:T(8,128)(2,1)}), bf16[128,6144]{1,0:T(8,128)(2,1)}) %reduce-scatter.14.cloned.1.call-update) | async-done | bytes 1572880 | tf_op jit(solution)/shard_map/reduce_scatter | solution.py:386
  1931.4 41.0 %all-reduce.73 = (f32[8]{0:T(128)}, f32[8]{0:T(128)}, f32[128]{0:T(128)}) all-reduce(f32[8]{0:T(128)S(1)} %add_multiply_fusion, f32[8]{0:T(128)S(1)} %add.760, f32[128]{0:T(128)S(1)} %add.761), channel_id=1, replica_groups=mesh['rep'=4,'ctx'=8] {'rep','ctx'}, use_global_device_ids=true, to_apply=%region_70.75 | all-reduce | flops 144 | bytes 1152 | tf_op jit(solution)/shard_map/psum | solution.py:414
  1973.7 15.2 reduce-scatter.22.cloned.1.call-done
  1989.7 66.2 %reduce-scatter.26.cloned.1.call-done = bf16[640,4]{1,0:T(8,128)(2,1)} async-done(((bf16[5120,4]{1,0:T(8,128)(2,1)}), bf16[640,4]{1,0:T(8,128)(2,1)}) %reduce-scatter.26.cloned.1.call-update) | async-done | bytes 5136
  2056.9 63.2 %reduce-scatter.24.cloned.1.call-done = bf16[128,24]{1,0:T(8,128)(2,1)} async-done(((bf16[1024,24]{1,0:T(8,128)(2,1)}), bf16[128,24]{1,0:T(8,128)(2,1)}) %reduce-scatter.24.cloned.1.call-update) | async-done | bytes 6160
  2133.3 71.3 %all-reduce.78.cloned.1.call-done = (bf16[128,6144]{1,0:T(8,128)(2,1)}, bf16[128,1024]{1,0:T(8,128)(2,1)}, bf16[128,5632]{1,0:T(8,128)(2,1)}, bf16[352,1024]{1,0:T(8,128)(2,1)}) async-done(((bf16[128,6144]{1,0:T(8,128)(2,1)}, bf16[128,1024]{1,0:T(8,128)(2,1)}, bf16[128,5632]{1,0:T(8,128)(2,1)}, bf16[352,1024]{1,0:T(8,128)(2,1)}), (bf16[128,6144]{1,0:T(8,128)(2,1)}, bf16[128,1024]{1,0:T(8,128)(2,1)}, ...) | async-done | bytes 3997712 | tf_op jit(solution)/shard_map/psum | solution.py:407
  (1092 shorter events, 617.6 us)
Async XLA Ops:
  7.2 180.1 %all-gather.21.cloned.1.call-start = ((), (), s32[]{:S(2)}) async-start(), calls=%async_computation.7 | async-start | bytes 14155776 | tf_op jit(solution)/shard_map/all_gather | solution.py:256
  8.0 639.5 %all-gather.29.cloned.1.call-start = ((), (), s32[]{:S(2)}) async-start(), calls=%async_computation.15 | async-start | bytes 4718592 | tf_op jit(solution)/shard_map/all_gather | solution.py:23
  194.0 10.7 collective-permute-start
  198.6 7.3 collective-permute-start.1
  418.2 229.4 %all-gather.31.cloned.1.call-start = ((), (), s32[]{:S(2)}) async-start(), calls=%async_computation.16 | async-start | bytes 4718592 | tf_op jit(solution)/shard_map/all_gather | solution.py:23
  418.9 262.6 %all-gather.33.cloned.1.call-start = ((), (), s32[]{:S(2)}) async-start(), calls=%async_computation.17 | async-start | bytes 4718592 | tf_op jit(solution)/shard_map/all_gather | solution.py:23
  608.6 146.6 %all-gather.35.cloned.1.call-start = ((), (), s32[]{:S(2)}) async-start(), calls=%async_computation.18 | async-start | bytes 4718592 | tf_op jit(solution)/shard_map/all_gather | solution.py:23
  609.1 196.2 %all-gather.23.cloned.1.call-start = ((), (), s32[]{:S(2)}) async-start(), calls=%async_computation.8 | async-start | bytes 2359296 | tf_op jit(solution)/shard_map/all_gather | solution.py:259
  609.7 358.2 %all-gather.25.cloned.1.call-start = ((), (), s32[]{:S(2)}) async-start(), calls=%async_computation.9 | async-start | bytes 12976128 | tf_op jit(solution)/shard_map/all_gather | solution.py:260
  610.5 451.0 %all-gather.27.cloned.1.call-start = ((), (), s32[]{:S(2)}) async-start(), calls=%async_computation.10 | async-start | bytes 6488064 | tf_op jit(solution)/shard_map/all_gather | solution.py:261
  611.2 890.0 %all-gather.41.cloned.1.call-start = ((), (), s32[]{:S(2)}) async-start(), calls=%async_computation.21 | async-start | bytes 2359296 | tf_op jit(solution)/shard_map/all_gather | solution.py:38
  647.4 853.8 %all-gather.43.cloned.1.call-start = ((), (), s32[]{:S(2)}) async-start(), calls=%async_computation.22 | async-start | bytes 2359296 | tf_op jit(solution)/shard_map/all_gather | solution.py:38
  1111.7 413.2 %all-gather.37.cloned.1.call-start = ((), (), s32[]{:S(2)}) async-start(), calls=%async_computation.19 | async-start | bytes 2359296 | tf_op jit(solution)/shard_map/all_gather | solution.py:38
  1113.6 411.3 %all-gather.39.cloned.1.call-start = ((), (), s32[]{:S(2)}) async-start(), calls=%async_computation.20 | async-start | bytes 2359296 | tf_op jit(solution)/shard_map/all_gather | solution.py:38
  1129.1 634.4 %reduce-scatter.16.cloned.1.call-start = ((), (), s32[]{:S(2)}) async-start(), calls=%async_computation.12 | async-start | bytes 2359296 | tf_op jit(solution)/shard_map/reduce_scatter | solution.py:395
  1133.0 630.5 %reduce-scatter.20.cloned.1.call-start = ((), (), s32[]{:S(2)}) async-start(), calls=%async_computation.14 | async-start | bytes 6488064 | tf_op jit(solution)/shard_map/reduce_scatter | solution.py:401
  1141.1 622.4 %reduce-scatter.18.cloned.1.call-start = ((), (), s32[]{:S(2)}) async-start(), calls=%async_computation.13 | async-start | bytes 12976128 | tf_op jit(solution)/shard_map/reduce_scatter | solution.py:398
  1501.1 421.8 %reduce-scatter.14.cloned.1.call-start = ((), (), s32[]{:S(2)}) async-start(), calls=%async_computation.11 | async-start | bytes 14155776 | tf_op jit(solution)/shard_map/reduce_scatter | solution.py:386
  1679.3 8.2 collective-permute-start.3
  1684.2 5.9 collective-permute-start.2
  1715.6 273.3 %reduce-scatter.22.cloned.1.call-start = ((), (), s32[]{:S(2)}) async-start(), calls=%async_computation.23 | async-start | bytes 294912
  1760.2 295.7 %reduce-scatter.26.cloned.1.call-start = ((), (), s32[]{:S(2)}) async-start(), calls=%async_computation.25 | async-start | bytes 1474560
  1762.1 358.1 %reduce-scatter.24.cloned.1.call-start = ((), (), s32[]{:S(2)}) async-start(), calls=%async_computation.24 | async-start | bytes 294912
  1763.3 441.4 %all-reduce.78.cloned.1.call-start = ((), (), s32[]{:S(2)}) async-start(), calls=%async_computation.26 | async-start | bytes 7995392 | tf_op jit(solution)/shard_map/psum | solution.py:407
  (313 other events, 9944.7 us)
Sparse Core Ops, SparseCore 0:
  10.2 176.9 all-gather.20
  418.3 73.4 all-gather.28
  494.5 72.4 all-gather.30
  608.7 72.7 all-gather.32
  683.4 71.6 all-gather.34
  757.1 48.1 all-gather.22
  807.5 160.2 all-gather.24
  970.1 91.3 all-gather.26
  1063.6 48.7 all-gather.40
  1114.4 48.3 all-gather.42
  1164.9 48.2 all-gather.36
  1215.1 48.9 all-gather.38
  1267.7 66.4 reduce-scatter.15
  1337.7 109.5 reduce-scatter.19
  1501.2 192.3 reduce-scatter.17
  1715.7 207.1 reduce-scatter.13
  1926.7 62.1 reduce-scatter.21
  1992.7 63.1 reduce-scatter.25
  2059.8 60.3 reduce-scatter.23
  2122.6 81.9 all-reduce.77
where the time goes:
time: 2230 us; the launch traced here: 2220 us
  waiting for transfers between devices  818 us (37%)
  other arithmetic  752 us (34%)
  matrix products  354 us (16%)
  local copies, waits for them, and re-layouts  131 us (6%)
  blocking collectives  128 us (6%)
    another operation x9, other arithmetic, run_stretches(): jax.scipy.linalg.solve_triangular(system, right_side, lower=True, unit_di...  642 us
    dot_general x102, matrix products, batched(): return jnp.einsum(form, left, right, precision=HIGH_PRECISION)  178 us
    all_gather x1, waiting for transfers between devices, per_device(): lax.all_gather(gate_up_weight, 'ctx', axis=0, tiled=True)  160 us
    reduce_scatter x1, waiting for transfers between devices, per_device(): lax.psum_scatter(grad_sums[1].astype(jnp.bfloat16), 'ctx', scatter_dimens...  159 us
    unnamed x23, waiting for transfers between devices  149 us
    all_gather x1, waiting for transfers between devices, per_device(): lax.all_gather(w_in, 'ctx', axis=0, tiled=True)  94.5 us
    all_gather x4, waiting for transfers between devices, prefix(): pieces = jax.tree.map(lambda part: lax.all_gather(part, axis), value)  84.8 us
    all_gather x1, waiting for transfers between devices, per_device(): lax.all_gather(w_down, 'ctx', axis=0, tiled=True)  81.5 us
  transfers between devices with their start and end apart: 24, of which 13 were waited for; matrix products, arithmetic and copies ran while one was open for 45% of the time, Pallas kernels for 0%

commit v1 on v0

v1 whole, which is shorter than its diff:
```python
import functools
import jax
import jax.numpy as jnp
from jax import lax
from jax.experimental import pallas as pl
from jax.experimental.pallas import tpu as pltpu
from jax.sharding import PartitionSpec as P

STEPS = 2
CONV = 4
STRETCH = 64
HEADS = 8
EPS = 1e-06
WIDE = 2 * STRETCH


def low(a):
    return a.astype(jnp.bfloat16)


def halves(a):
    high = low(a)
    return high, low(a - high.astype(jnp.float32))


def dot(a, b, dims):
    return lax.dot_general(a, b, (dims, ((), ())), preferred_element_type=jnp.float32)


def fold(out):
    half = out.shape[1] // 2
    return out[:, :half] + out[:, half:]


def left_nn(parts):
    return jnp.concatenate(parts, axis=1)


def right_nn(parts):
    row = jnp.concatenate(parts, axis=1)
    return jnp.concatenate([row, row], axis=0)


def right_nt(parts):
    high, rest = parts
    return jnp.concatenate(
        [jnp.concatenate([high, high], axis=1), jnp.concatenate([rest, rest], axis=1)], axis=0
    )


def mul(a, b):
    return fold(dot(left_nn(halves(a)), right_nn(halves(b)), ((1,), (0,))))


def mul_nt(a, b):
    return fold(dot(left_nn(halves(a)), right_nt(halves(b)), ((1,), (1,))))


def mul_tn(a, b):
    left = jnp.concatenate(halves(a), axis=0)
    return fold(dot(left, right_nn(halves(b)), ((0,), (0,))))


def low_nn(a, b):
    return dot(low(a), low(b), ((1,), (0,)))


def low_nt(a, b):
    return dot(low(a), low(b), ((1,), (1,)))


def low_tn(a, b):
    return dot(low(a), low(b), ((0,), (0,)))


def iotas(rows, cols):
    return (
        lax.broadcasted_iota(jnp.int32, (rows, cols), 0),
        lax.broadcasted_iota(jnp.int32, (rows, cols), 1),
    )


def order(index):
    return STEPS * lax.rem(index, STRETCH) + lax.div(index, STRETCH)


def sigmoid(a):
    return 1.0 / (1.0 + jnp.exp(-a))


def softplus(a):
    return jnp.maximum(a, 0.0) + jnp.log1p(jnp.exp(-jnp.abs(a)))


def window(ref, halo, seq, base, columns):
    before = ref[seq, pl.ds(pl.multiple_of(jnp.maximum(base - 8, 0), 8), 8), columns]
    ahead = 0.0 if halo is None else halo[seq, :, columns]
    return jnp.concatenate(
        [jnp.where(base == 0, ahead, before), ref[seq, pl.ds(base, STRETCH), columns]], axis=0
    )


def stack(act, at, dim):
    return jnp.concatenate(
        [act[:, at * dim : (at + 1) * dim], act[:, (at + 1) * dim : (at + 2) * dim]], axis=0
    )


def convolve(rows, conv):
    total = None
    for tap in range(CONV):
        start = 8 - (CONV - 1) + tap
        term = conv[tap : tap + 1] * rows[start : start + STRETCH]
        total = term if total is None else total + term
    return total


def rates(small, decay):
    beta = jnp.concatenate([sigmoid(small[:, 0:1]), sigmoid(small[:, 1:2])], axis=0)
    gamma = -jnp.exp(decay[0:1]) * softplus(small + decay[1:2])
    row, col = iotas(STRETCH, STRETCH)
    tri = low(jnp.where(row >= col, 1.0, 0.0))
    high = low(gamma)
    rest = gamma - high.astype(jnp.float32)
    middle = low(rest)
    last = low(rest - middle.astype(jnp.float32))
    running = (
        dot(tri, high, ((1,), (0,))) + dot(tri, middle, ((1,), (0,))) + dot(tri, last, ((1,), (0,)))
    )
    return beta, running


def decays(running):
    column = running[:, 2:3]
    across = jnp.transpose(running)[2:3, :]
    row, col = iotas(STRETCH, STRETCH)
    gap = jnp.broadcast_to(column, (STRETCH, STRETCH)) - across
    upto = jnp.where(row >= col, jnp.exp(jnp.where(row >= col, gap, 0.0)), 0.0)
    before = jnp.where(row > col, upto, 0.0)
    strict = jnp.concatenate(
        [
            jnp.concatenate([before, before], axis=1),
            jnp.concatenate([upto, before], axis=1),
        ],
        axis=0,
    )
    return strict, jnp.concatenate([upto, upto], axis=1)


def level_masks():
    row, col = iotas(WIDE, WIDE)
    row, col = order(row), order(col)
    masks, size = [], 1
    while size < WIDE:
        inside = (lax.div(row, 2 * size) == lax.div(col, 2 * size)) & (
            lax.div(row, size) != lax.div(col, size)
        )
        masks.append(jnp.where(inside, 1.0, 0.0))
        size *= 2
    return [masks[0]] + [low(mask) for mask in masks[1:]]


def inverses(systems, masks):
    row, col = iotas(WIDE, WIDE)
    eye = jnp.where(row == col, 1.0, 0.0)
    solved = [eye - masks[0] * system for system in systems]
    split = [halves(system) for system in systems]
    for mask in masks[1:]:
        parts = [halves(a) for a in solved]
        steps = [
            fold(
                dot(
                    jnp.concatenate([high * mask, rest * mask], axis=1),
                    right_nn(part),
                    ((1,), (0,)),
                )
            )
            for (high, rest), part in zip(split, parts)
        ]
        solved = [
            a - fold(dot(left_nn(part), right_nn(halves(step)), ((1,), (0,))))
            for a, part, step in zip(solved, parts, steps)
        ]
    return solved


def unit_rows(stacked):
    return lax.rsqrt(jnp.sum(stacked * stacked, axis=1, keepdims=True) + EPS)


def twice(column):
    return jnp.concatenate([column, column], axis=0)


def forward_kernel(linked, *refs):
    if linked:
        proj, conv, decay, gain, halo, start, *refs = refs
        *refs, final, product, local, offset = refs
    else:
        proj, conv, decay, gain, *refs = refs
        halo, (*refs, local, offset) = None, refs
    mixer, out, fresh, inv, weights, trans, states = refs
    seqs, length, _ = proj.shape
    dim = gain.shape[1]
    blocks = length // STRETCH
    together = 2 if blocks % 2 == 0 else 1
    masks = level_masks()
    row, col = iotas(dim, dim)
    diagonal = row == col

    def spots(step):
        return [(seq, step * together + k) for k in range(together) for seq in range(seqs)]

    def first(step, _):
        units = spots(step)
        kept = []
        for seq, block in units:
            base = pl.multiple_of(block * STRETCH, STRETCH)
            rows = window(proj, halo, seq, base, pl.ds(0, 5 * dim))
            pre = convolve(rows, conv)
            act = pre * sigmoid(pre)
            raw = stack(act, 1, dim)
            key = raw * unit_rows(raw)
            beta, running = rates(proj[seq, pl.ds(base, STRETCH), pl.ds(6 * dim, dim)], decay)
            kept.append((act[:, :dim], key, stack(act, 3, dim), beta, running))
        systems = []
        for (seq, block), (query, key, value, beta, running) in zip(units, kept):
            at = seq * blocks + block
            strict, upto = decays(running)
            key_halves = halves(key)
            both = fold(
                dot(
                    jnp.concatenate([left_nn(key_halves), left_nn(halves(query))], axis=0),
                    right_nt(key_halves),
                    ((1,), (1,)),
                )
            )
            systems.append(beta * both[:WIDE] * strict)
            local[at] = both[WIDE:] * upto
            offset[at] = query * jnp.exp(running[:, 2:3])
        for (seq, block), (query, key, value, beta, running), solved in zip(
            units, kept, inverses(systems, masks)
        ):
            at = seq * blocks + block
            inv[at] = solved
            grown = twice(jnp.exp(running[:, 2:3]))
            end = running[STRETCH - 1 :, 2:3]
            solved_left = left_nn(halves(solved))
            weight = fold(dot(solved_left, right_nn(halves(beta * key * grown)), ((1,), (0,))))
            value = fold(dot(solved_left, right_nn(halves(beta * value)), ((1,), (0,))))
            weights[at] = weight
            fresh[at] = value
            to_end = jnp.concatenate(halves(key * twice(jnp.exp(end - running[:, 2:3]))), axis=0)
            trans[at] = jnp.where(diagonal, jnp.exp(end), 0.0) - fold(
                dot(to_end, right_nn(halves(weight)), ((0,), (0,)))
            )
            states[at] = fold(dot(to_end, right_nn(halves(value)), ((0,), (0,))))
        return 0

    lax.fori_loop(0, blocks // together, first, 0)

    def chain(block, carried):
        new = []
        for seq in range(seqs):
            at = seq * blocks + block
            state = carried[seq]
            added = states[at]
            states[at] = state
            new.append(mul(trans[at], state) + added)
            if linked:
                product[seq] = mul(trans[at], product[seq])
        return tuple(new)

    if linked:
        for seq in range(seqs):
            product[seq] = jnp.where(diagonal, 1.0, 0.0)
        begin = tuple(start[seq] for seq in range(seqs))
    else:
        begin = (jnp.zeros((dim, dim), jnp.float32),) * seqs
    ended = lax.fori_loop(0, blocks, chain, begin)
    if linked:
        for seq in range(seqs):
            final[seq] = ended[seq]

    def last(step, _):
        units = spots(step)
        reads = [
            mul(
                jnp.concatenate([weights[seq * blocks + block], offset[seq * blocks + block]], axis=0),
                states[seq * blocks + block],
            )
            for seq, block in units
        ]
        for (seq, block), read in zip(units, reads):
            at = seq * blocks + block
            base = pl.multiple_of(block * STRETCH, STRETCH)
            new = fresh[at] - read[:WIDE]
            fresh[at] = new
            result = read[WIDE:] + mul(local[at], new)
            out[seq, pl.ds(base, STRETCH)] = result
            gate = proj[seq, pl.ds(base, STRETCH), pl.ds(5 * dim, dim)]
            scale = lax.rsqrt(jnp.mean(result * result, axis=1, keepdims=True) + EPS)
            mixer[seq, pl.ds(base, STRETCH)] = low(
                result * scale * gain[...] * (gate * sigmoid(gate))
            )
        return 0

    lax.fori_loop(0, blocks // together, last, 0)


def mixer_forward(proj, conv, decay, gain, link=()):
    seqs, length, _ = proj.shape
    dim = gain.shape[1]
    units = seqs * (length // STRETCH)
    square = jax.ShapeDtypeStruct((units, WIDE, dim), jnp.float32)
    state = jax.ShapeDtypeStruct((seqs, dim, dim), jnp.float32)
    shapes = (
        jax.ShapeDtypeStruct((seqs, length, dim), jnp.bfloat16),
        jax.ShapeDtypeStruct((seqs, length, dim), jnp.float32),
        square,
        square,
        square,
        square,
        square,
    )
    if link:
        shapes += (state, state)
    return pl.pallas_call(
        functools.partial(forward_kernel, bool(link)),
        out_shape=shapes,
        in_specs=[pl.BlockSpec(memory_space=pltpu.VMEM)] * (4 + len(link)),
        out_specs=[pl.BlockSpec(memory_space=pltpu.VMEM)] * len(shapes),
        scratch_shapes=[
            pltpu.VMEM((units, STRETCH, WIDE), jnp.float32),
            pltpu.VMEM((units, STRETCH, dim), jnp.float32),
        ],
        compiler_params=pltpu.CompilerParams(vmem_limit_bytes=56 * 2**20),
        cost_estimate=pl.CostEstimate(
            flops=units * 60 * WIDE * WIDE * WIDE,
            bytes_accessed=units * WIDE * WIDE * 30,
            transcendentals=units * WIDE * WIDE * 8,
        ),
        name="mixer_forward",
    )(proj, conv, decay, gain, *link)


def backward_kernel(linked, *refs):
    proj, conv, decay, gain, out, fresh, inv, weights, trans, states, d_mixer, *refs = refs
    if linked:
        halo, end_state, *refs = refs
        d_proj, d_conv, d_small_sums, d_gain, d_start, d_first, *refs = refs
    else:
        halo = None
        d_proj, d_conv, d_small_sums, d_gain, *refs = refs
    d_out, chained = refs
    seqs, length, _ = proj.shape
    dim = gain.shape[1]
    blocks = length // STRETCH
    together = 2 if blocks % 2 == 0 else 1
    all_conv = pl.ds(0, 5 * dim)

    def spots(step):
        return [(seq, blocks - 1 - step * together - k) for k in range(together) for seq in range(seqs)]

    def first(step, gain_sum):
        units = spots(step)
        kept = []
        for seq, block in units:
            at = seq * blocks + block
            base = pl.multiple_of(block * STRETCH, STRETCH)
            result = out[seq, pl.ds(base, STRETCH)]
            gate = proj[seq, pl.ds(base, STRETCH), pl.ds(5 * dim, dim)]
            given = d_mixer[seq, pl.ds(base, STRETCH)].astype(jnp.float32)
            scale = lax.rsqrt(jnp.mean(result * result, axis=1, keepdims=True) + EPS)
            normal = result * scale
            open_ = sigmoid(gate)
            silu = gate * open_
            gain_sum = gain_sum + jnp.sum(given * normal * silu, axis=0, keepdims=True)
            d_proj[seq, pl.ds(base, STRETCH), pl.ds(5 * dim, dim)] = low(
                given * normal * gain[...] * (open_ * (1.0 + gate * (1.0 - open_)))
            )
            inner = given * gain[...] * silu
            d_result = scale * (inner - normal * jnp.mean(inner * normal, axis=1, keepdims=True))
            d_out[at] = d_result
            pre = convolve(window(proj, halo, seq, base, pl.ds(0, 3 * dim)), conv[:, : 3 * dim])
            act = pre * sigmoid(pre)
            raw = stack(act, 1, dim)
            _, running = rates(proj[seq, pl.ds(base, STRETCH), pl.ds(6 * dim, dim)], decay)
            kept.append((act[:, :dim], raw * unit_rows(raw), running, d_result))
        scores = [
            mul_nt(query, key) * decays(running)[1] for query, key, running, _ in kept
        ]
        d_freshes = [mul_tn(score, unit[3]) for score, unit in zip(scores, kept)]
        for (seq, block), (query, _, running, d_result), d_fresh in zip(units, kept, d_freshes):
            at = seq * blocks + block
            chained[at] = mul_tn(
                jnp.concatenate([query * jnp.exp(running[:, 2:3]), -weights[at]], axis=0),
                jnp.concatenate([d_result, d_fresh], axis=0),
            )
        return gain_sum

    d_gain[...] = lax.fori_loop(0, blocks // together, first, jnp.zeros((1, dim), jnp.float32))

    def chain(step, carried):
        block = blocks - 1 - step
        new = []
        for seq in range(seqs):
            at = seq * blocks + block
            later = carried[seq]
            added = chained[at]
            chained[at] = later
            new.append(mul_tn(trans[at], later) + added)
        return tuple(new)

    if linked:
        begin = tuple(end_state[seq] for seq in range(seqs))
    else:
        begin = (jnp.zeros((dim, dim), jnp.float32),) * seqs
    ended = lax.fori_loop(0, blocks, chain, begin)
    if linked:
        for seq in range(seqs):
            d_start[seq] = ended[seq]

    def last(step, sums):
        conv_sum, small_sum, *rims = sums
        units = spots(step)
        ats = [seq * blocks + block for seq, block in units]
        bases = [pl.multiple_of(block * STRETCH, STRETCH) for _, block in units]
        acts, keys, rate_sets = [], [], []
        for (seq, _), base in zip(units, bases):
            pre = convolve(window(proj, halo, seq, base, all_conv), conv)
            gate = sigmoid(pre)
            act = pre * gate
            raw = stack(act, 1, dim)
            unit = unit_rows(raw)
            acts.append((act, gate * (1.0 + pre * (1.0 - gate)), unit))
            keys.append(raw * unit)
            rate_sets.append(rates(proj[seq, pl.ds(base, STRETCH), pl.ds(6 * dim, dim)], decay))
        nears = [
            mul_nt(jnp.concatenate([key, act[:, :dim]], axis=0), key)
            for (act, _, _), key in zip(acts, keys)
        ]
        masks = [decays(running) for _, running in rate_sets]
        d_freshes = [
            mul_tn(near[WIDE:] * upto, d_out[at])
            + mul(key * twice(jnp.exp(running[STRETCH - 1 :, 2:3] - running[:, 2:3])), chained[at])
            for near, (_, upto), at, key, (_, running) in zip(nears, masks, ats, keys, rate_sets)
        ]
        backs = [mul_tn(inv[at], d_fresh) for at, d_fresh in zip(ats, d_freshes)]
        reads = [
            stack(act, 3, dim) - mul(key * twice(jnp.exp(running[:, 2:3])), states[at])
            for (act, _, _), key, (_, running), at in zip(acts, keys, rate_sets, ats)
        ]
        to_state = [
            mul_nt(jnp.concatenate([beta * back, d_out[at]], axis=0), states[at])
            for (beta, _), back, at in zip(rate_sets, backs, ats)
        ]
        to_new = [
            mul_nt(jnp.concatenate([back, d_out[at]], axis=0), fresh[at])
            for back, at in zip(backs, ats)
        ]
        d_ends = [mul_nt(fresh[at], chained[at]) for at in ats]
        shaped = [-cross[:WIDE] * strict for cross, (strict, _) in zip(to_new, masks)]
        insides = [beta * a for (beta, _), a in zip(rate_sets, shaped)]
        d_nears = [cross[WIDE:] * upto for cross, (_, upto) in zip(to_new, masks)]
        towards = [
            mul(jnp.concatenate([inside, d_near], axis=0), key)
            for inside, d_near, key in zip(insides, d_nears, keys)
        ]
        away = [
            mul_tn(
                jnp.concatenate([inside, d_near], axis=0),
                jnp.concatenate([key, act[:, :dim]], axis=0),
            )
            for inside, d_near, key, (act, _, _) in zip(insides, d_nears, keys, acts)
        ]
        d_heres = []
        for k, ((seq, _), at, base) in enumerate(zip(units, ats, bases)):
            act, slope, unit = acts[k]
            query, key = act[:, :dim], keys[k]
            beta, running = rate_sets[k]
            small = proj[seq, pl.ds(base, STRETCH), pl.ds(6 * dim, dim)]
            g = running[:, 2:3]
            end = g[STRETCH - 1 :]
            grown, to_go = jnp.exp(g), jnp.exp(end - g)
            back = backs[k]
            d_scaled, d_query_scaled = -to_state[k][:WIDE], to_state[k][WIDE:]
            with_inside = shaped[k] * nears[k][:WIDE]
            d_beta = jnp.sum(back * reads[k] + with_inside, axis=1, keepdims=True)
            gaps = beta * with_inside
            score_gaps = d_nears[k] * nears[k][WIDE:]
            d_query = towards[k][WIDE:] + d_query_scaled * grown
            from_start, from_end = d_scaled * twice(grown), d_ends[k] * twice(to_go)
            d_key = towards[k][:WIDE] + away[k] + from_start + from_end
            ended = jnp.sum(from_end * key, axis=1, keepdims=True)
            row_terms = jnp.sum(gaps + from_start * key, axis=1, keepdims=True) - ended
            col_terms = jnp.sum(gaps, axis=0, keepdims=True) + jnp.sum(
                score_gaps, axis=0, keepdims=True
            )
            col_terms = jnp.transpose(jnp.broadcast_to(col_terms, (8, WIDE)))[:, 0:1]
            row_terms = row_terms - col_terms
            d_g = (
                row_terms[:STRETCH]
                + row_terms[STRETCH:]
                + jnp.sum(score_gaps + d_query_scaled * grown * query, axis=1, keepdims=True)
            )
            d_end = jnp.sum(ended, axis=0, keepdims=True) + jnp.exp(end) * jnp.sum(
                jnp.sum(states[at] * chained[at], axis=0, keepdims=True), axis=1, keepdims=True
            )
            row, col = iotas(STRETCH, STRETCH)
            across = jnp.transpose(jnp.broadcast_to(d_g, (STRETCH, WIDE)))[:STRETCH]
            d_gamma = jnp.sum(jnp.where(row <= col, across, 0.0), axis=1, keepdims=True) + d_end
            lane = iotas(STRETCH, dim)[1]
            shifted = small + decay[1:2]
            d_soft = -jnp.exp(decay[0:1]) * d_gamma
            d_logit = d_soft * sigmoid(shifted)
            d_rate = jnp.where(lane == 0, d_beta[:STRETCH], d_beta[STRETCH:])
            open_beta = sigmoid(small)
            d_small = jnp.where(
                lane < 2,
                d_rate * open_beta * (1.0 - open_beta),
                jnp.where(lane == 2, d_logit, 0.0),
            )
            d_proj[seq, pl.ds(base, STRETCH), pl.ds(6 * dim, dim)] = low(d_small)
            small_sum = small_sum + jnp.concatenate(
                [
                    jnp.sum(d_soft * softplus(shifted), axis=0, keepdims=True),
                    jnp.sum(d_logit, axis=0, keepdims=True),
                ],
                axis=0,
            )
            d_raw = unit * (d_key - key * jnp.sum(d_key * key, axis=1, keepdims=True))
            d_value = beta * back
            d_act = jnp.concatenate(
                [d_query, d_raw[:STRETCH], d_raw[STRETCH:], d_value[:STRETCH], d_value[STRETCH:]],
                axis=1,
            )
            d_heres.append(d_act * slope)
        for (seq, _), base, d_here in zip(units, bases, d_heres):
            rows = window(proj, halo, seq, base, all_conv)
            first_row = 8 - (CONV - 1)
            conv_sum = conv_sum + jnp.concatenate(
                [
                    jnp.sum(
                        d_here * rows[first_row + tap : first_row + tap + STRETCH],
                        axis=0,
                        keepdims=True,
                    )
                    for tap in range(CONV)
                ],
                axis=0,
            )
            ahead = jnp.concatenate([d_here, rims[seq]], axis=0)
            rims[seq] = d_here[:8]
            total = None
            for tap in range(CONV):
                start = CONV - 1 - tap
                term = conv[tap : tap + 1] * ahead[start : start + STRETCH]
                total = term if total is None else total + term
            d_proj[seq, pl.ds(base, STRETCH), all_conv] = low(total)
        return conv_sum, small_sum, *rims

    conv_sum, small_sum, *rims = lax.fori_loop(
        0,
        blocks // together,
        last,
        (jnp.zeros((CONV, 5 * dim), jnp.float32), jnp.zeros((2, dim), jnp.float32))
        + (jnp.zeros((8, 5 * dim), jnp.float32),) * seqs,
    )
    if linked:
        for seq in range(seqs):
            d_first[seq] = rims[seq]
    d_conv[...] = conv_sum
    d_small_sums[...] = small_sum


def mixer_backward(proj, conv, decay, gain, kept, d_mixer, link=()):
    seqs, length, width = proj.shape
    dim = gain.shape[1]
    units = seqs * (length // STRETCH)
    shapes = (
        jax.ShapeDtypeStruct((seqs, length, width), jnp.bfloat16),
        jax.ShapeDtypeStruct((CONV, 5 * dim), jnp.float32),
        jax.ShapeDtypeStruct((2, dim), jnp.float32),
        jax.ShapeDtypeStruct((1, dim), jnp.float32),
    )
    if link:
        shapes += (
            jax.ShapeDtypeStruct((seqs, dim, dim), jnp.float32),
            jax.ShapeDtypeStruct((seqs, 8, 5 * dim), jnp.float32),
        )
    return pl.pallas_call(
        functools.partial(backward_kernel, bool(link)),
        out_shape=shapes,
        in_specs=[pl.BlockSpec(memory_space=pltpu.VMEM)] * (11 + len(link)),
        out_specs=[pl.BlockSpec(memory_space=pltpu.VMEM)] * len(shapes),
        scratch_shapes=[
            pltpu.VMEM((units, STRETCH, dim), jnp.float32),
            pltpu.VMEM((units, dim, dim), jnp.float32),
        ],
        compiler_params=pltpu.CompilerParams(vmem_limit_bytes=60 * 2**20),
        cost_estimate=pl.CostEstimate(
            flops=units * 60 * WIDE * WIDE * WIDE,
            bytes_accessed=units * WIDE * WIDE * 30,
            transcendentals=units * WIDE * WIDE * 8,
        ),
        name="mixer_backward",
    )(proj, conv, decay, gain, *kept, d_mixer, *link)


def matmul(left, right):
    return jnp.dot(left, right, preferred_element_type=jnp.float32)


def times_transposed(left, right):
    return lax.dot_general(
        left, right, (((1,), (1,)), ((), ())), preferred_element_type=jnp.float32
    )


def transposed_times(left, right):
    return lax.dot_general(
        left, right, (((0,), (0,)), ((), ())), preferred_element_type=jnp.float32
    )


def batched(left, right):
    return jnp.einsum("sij,sjk->sik", left, right, precision=lax.Precision.HIGHEST)


def norm_scale(values):
    return lax.rsqrt(jnp.mean(values * values, axis=-1, keepdims=True) + EPS)


def norm_back(values, gain, given):
    scale = norm_scale(values)
    normal = values * scale
    inner = given * gain
    return scale * (inner - normal * jnp.mean(inner * normal, axis=-1, keepdims=True)), (
        given * normal
    )


def per_device(
    block_in,
    lengths,
    norm_gains,
    w_in,
    w_small,
    conv_weight,
    decay_log,
    decay_bias,
    out_norm_gain,
    w_out,
    gate_up_weight,
    w_down,
    out_cotangent,
):
    micro, seq_count, tokens, width = block_in.shape
    seqs = micro * seq_count
    count = lax.axis_size("ctx")
    groups = lax.axis_size("rep")
    place = lax.axis_index("ctx")
    group = lax.axis_index("rep")
    teams = count // HEADS
    head = lax.rem(place, HEADS)
    team = lax.div(place, HEADS)
    mates = peers = None
    if teams > 1:
        mates = [[t * HEADS + h for h in range(HEADS)] for t in range(teams)]
        peers = [[t * HEADS + h for t in range(teams)] for h in range(HEADS)]
    dim = width // HEADS
    length = HEADS * tokens
    rows = seqs * tokens
    kinds = 2 + 2 * STEPS
    rates_of = STEPS + 1
    f32, bf16 = jnp.float32, jnp.bfloat16

    own = width // count
    small_block = jnp.concatenate(
        [norm_gains.reshape(-1), w_small.reshape(-1), conv_weight.reshape(-1)]
    )
    small_block = jnp.pad(small_block, (0, -small_block.size % 128)).reshape(-1, 128)
    smalls = lax.all_gather(small_block, "ctx", axis=0).reshape(count, -1)
    gains = smalls[:, : 2 * own].reshape(count, 2, own).transpose(1, 0, 2).reshape(2, width)
    gains = gains.astype(f32)
    small_all = smalls[:, 2 * own : (2 + HEADS * rates_of) * own].reshape(width, rates_of, HEADS)
    small_head = lax.dynamic_index_in_dim(small_all, head, 2, keepdims=False)
    taps_at = (2 + HEADS * rates_of) * own
    conv_all = smalls[:, taps_at : taps_at + conv_weight.size].reshape(count, CONV, -1)
    conv_all = conv_all.transpose(1, 0, 2).reshape(CONV, kinds - 1, HEADS, dim)
    conv_head = lax.dynamic_index_in_dim(conv_all, head, 2, keepdims=False)
    conv_head = conv_head.reshape(CONV, -1).astype(f32)
    sequence = lax.all_gather(
        block_in.reshape(seqs, tokens, width), "ctx", axis=1, tiled=True, axis_index_groups=mates
    )
    w_head = w_in.reshape(own, kinds, HEADS, dim).transpose(2, 0, 1, 3)
    w_head = lax.all_to_all(w_head, "ctx", 0, 0, tiled=True, axis_index_groups=mates)
    w_head = w_head.reshape(HEADS * own, kinds * dim)
    if teams > 1:
        w_head = lax.all_gather(w_head, "ctx", axis=0, tiled=True, axis_index_groups=peers)
    w_head = jnp.concatenate(
        [w_head, small_head, jnp.zeros((width, dim - rates_of), bf16)], axis=1
    )
    w_out_full = lax.all_gather(w_out, "ctx", axis=0, tiled=True)
    hidden_own = w_down.shape[0] // groups
    gate_up_part = lax.dynamic_index_in_dim(
        gate_up_weight.reshape(own, 2, count, groups, hidden_own), group, 3, keepdims=False
    )
    gate_up_part = lax.all_gather(gate_up_part.reshape(own, -1), "ctx", axis=0, tiled=True)
    down_part = lax.dynamic_index_in_dim(
        w_down.reshape(groups, hidden_own, width), group, 0, keepdims=False
    )
    down_part = lax.all_gather(down_part, "ctx", axis=0, tiled=True)
    hidden_units = count * hidden_own

    inputs_all = sequence.astype(f32)
    h_first = (inputs_all * norm_scale(inputs_all) * gains[0]).astype(bf16)
    proj = matmul(h_first.reshape(seqs * length, width), w_head).reshape(seqs, length, -1)
    decay = jnp.stack(
        [
            jnp.broadcast_to(lax.dynamic_index_in_dim(decay_log, head, 0), (dim,)),
            jnp.broadcast_to(lax.dynamic_index_in_dim(decay_bias, head, 0), (dim,)),
        ]
    )
    gain = out_norm_gain.reshape(1, dim)
    halo = None
    if teams > 1:
        onward = [(c, c + HEADS) for c in range(count - HEADS)]
        halo = lax.ppermute(proj[:, length - 8 :], "ctx", onward)
        start = jnp.zeros((seqs, dim, dim), f32)
        *_, offset, transfer = mixer_forward(proj, conv_head, decay, gain, (halo, start))
        spans = lax.all_gather((transfer, offset), "ctx", axis_index_groups=peers)
        for turn in range(teams - 1):
            start = jnp.where(turn < team, batched(spans[0][turn], start) + spans[1][turn], start)
        mixer_head, *kept = mixer_forward(proj, conv_head, decay, gain, (halo, start))[:-2]
    else:
        mixer_head, *kept = mixer_forward(proj, conv_head, decay, gain)

    def to_tokens(array):
        split = array.reshape(seqs, HEADS, tokens, dim).transpose(1, 0, 2, 3)
        moved = lax.all_to_all(
            split.reshape(HEADS, rows, dim), "ctx", 0, 0, tiled=True, axis_index_groups=mates
        )
        return moved.transpose(1, 0, 2).reshape(rows, width)

    def to_heads(array):
        split = array.reshape(rows, HEADS, dim).transpose(1, 0, 2)
        moved = lax.all_to_all(split, "ctx", 0, 0, tiled=True, axis_index_groups=mates)
        return moved.reshape(HEADS, seqs, tokens, dim).transpose(1, 0, 2, 3).reshape(
            seqs, length, dim
        )

    mixer = to_tokens(mixer_head)
    inputs = block_in.reshape(rows, width).astype(f32)
    resid = inputs + matmul(mixer, w_out_full)

    h_second = (resid * norm_scale(resid) * gains[1]).astype(bf16)
    places = place * tokens + lax.broadcasted_iota(jnp.int32, (seqs, tokens), 1)
    valid = (places < lengths.reshape(seqs, 1)).astype(f32).reshape(rows, 1)
    grad_out = (out_cotangent.reshape(rows, width).astype(f32) * valid).astype(bf16)
    grad_all = lax.all_gather(grad_out, "rep", axis=0, tiled=True)
    h_all = lax.all_gather(h_second, "rep", axis=0, tiled=True)
    gate_up = matmul(h_all, gate_up_part)
    gate, up = gate_up[:, :hidden_units], gate_up[:, hidden_units:]
    open_gate = jax.nn.sigmoid(gate)
    silu = gate * open_gate
    hidden = (silu * up).astype(bf16)
    down = lax.psum_scatter(
        matmul(hidden, down_part).astype(bf16), "rep", scatter_dimension=0, tiled=True
    )
    result = (valid * (resid + down.astype(f32))).astype(bf16)

    d_hidden = times_transposed(grad_all, down_part)
    d_gate_up = jnp.concatenate(
        [d_hidden * up * (open_gate * (1.0 + gate * (1.0 - open_gate))), d_hidden * silu], axis=1
    ).astype(bf16)
    d_second = lax.psum_scatter(
        times_transposed(d_gate_up, gate_up_part).astype(bf16),
        "rep",
        scatter_dimension=0,
        tiled=True,
    ).astype(f32)
    grad_down = transposed_times(hidden, grad_all)
    grad_gate_up = transposed_times(h_all, d_gate_up)
    d_norm, gain_terms_second = norm_back(resid, gains[1], d_second)
    d_resid = grad_out.astype(f32) + d_norm
    d_branch = d_resid.astype(bf16)
    grad_out_proj = transposed_times(mixer, d_branch)
    d_mixer = times_transposed(d_branch, w_out_full)

    d_mixer = to_heads(d_mixer.astype(bf16))
    if teams > 1:
        later = jnp.zeros((seqs, dim, dim), f32)
        local = mixer_backward(proj, conv_head, decay, gain, kept, d_mixer, (halo, later))[4]
        locals_ = lax.all_gather(local, "ctx", axis_index_groups=peers)
        for turn in range(teams - 1, 0, -1):
            later = jnp.where(
                turn > team,
                batched(spans[0][turn].transpose(0, 2, 1), later) + locals_[turn],
                later,
            )
        d_proj, grad_conv, small_sums, grad_gain, _, rim = mixer_backward(
            proj, conv_head, decay, gain, kept, d_mixer, (halo, later)
        )
        rim = lax.ppermute(rim, "ctx", [(c, c - HEADS) for c in range(HEADS, count)])
        spill = jnp.zeros((seqs, CONV - 1, kinds * dim - dim), f32)
        for ahead in range(1, CONV):
            spill = spill.at[:, CONV - 1 - ahead :].add(
                conv_head[CONV - 1 - ahead] * rim[:, :ahead]
            )
        last = d_proj[:, length - CONV + 1 :, : (kinds - 1) * dim]
        d_proj = d_proj.at[:, length - CONV + 1 :, : (kinds - 1) * dim].set(
            (last.astype(f32) + spill).astype(bf16)
        )
    else:
        d_proj, grad_conv, small_sums, grad_gain = mixer_backward(
            proj, conv_head, decay, gain, kept, d_mixer
        )
    d_proj = d_proj.reshape(seqs * length, -1)
    grad_head = transposed_times(h_first.reshape(seqs * length, width), d_proj)
    d_first = times_transposed(d_proj, w_head).astype(bf16)
    d_first = d_first.reshape(seqs, HEADS, tokens, width).transpose(1, 0, 2, 3)
    d_first = lax.psum_scatter(
        d_first.reshape(HEADS * rows, width),
        "ctx",
        scatter_dimension=0,
        tiled=True,
        axis_index_groups=mates,
    ).astype(f32)
    d_inputs, gain_terms_first = norm_back(inputs, gains[0], d_first)
    in_grad = (d_resid + d_inputs).astype(bf16)

    grad_gate_up = lax.psum_scatter(
        grad_gate_up.astype(bf16), "ctx", scatter_dimension=0, tiled=True
    )
    grad_gate_up = lax.all_gather(
        grad_gate_up.reshape(own, 2, count, hidden_own), "rep", axis=3
    ).reshape(own, -1)
    grad_down = lax.psum_scatter(grad_down.astype(bf16), "ctx", scatter_dimension=0, tiled=True)
    grad_down = lax.all_gather(grad_down, "rep", axis=0, tiled=True)
    grad_out_proj = lax.psum_scatter(
        grad_out_proj.astype(bf16), "ctx", scatter_dimension=0, tiled=True
    )
    grad_in = grad_head[:, : kinds * dim].astype(bf16)
    if teams > 1:
        grad_in = lax.psum_scatter(
            grad_in, "ctx", scatter_dimension=0, tiled=True, axis_index_groups=peers
        )
    grad_in = lax.all_to_all(
        grad_in.reshape(HEADS, own, kinds * dim), "ctx", 0, 0, tiled=True, axis_index_groups=mates
    )
    grad_in = grad_in.reshape(HEADS, own, kinds, dim).transpose(1, 2, 0, 3).reshape(own, -1)
    grad_in, grad_out_proj = lax.psum((grad_in, grad_out_proj), "rep")

    gain_terms = jnp.stack([gain_terms_first.sum(axis=0), gain_terms_second.sum(axis=0)])
    here = jnp.arange(HEADS, dtype=jnp.int32) == head
    grad_small = grad_head[:, kinds * dim : kinds * dim + rates_of]
    packed = jnp.concatenate(
        [
            gain_terms.reshape(-1),
            jnp.where(here[None, None, :], grad_small[:, :, None], 0.0).reshape(-1),
            jnp.where(
                here[None, None, :, None], grad_conv.reshape(CONV, kinds - 1, 1, dim), 0.0
            ).reshape(-1),
            grad_gain.reshape(-1),
            jnp.pad(
                jnp.where(here[None, :], small_sums[:, STEPS : STEPS + 1], 0.0).reshape(-1),
                (0, dim - 2 * HEADS),
            ),
        ]
    ).reshape(-1, 128)
    packed = lax.psum(packed, ("rep", "ctx")).reshape(-1)

    def take(size):
        nonlocal packed
        part, packed = packed[:size], packed[size:]
        return part

    def mine(array, axis, size):
        return lax.dynamic_slice_in_dim(array, place * size, size, axis)

    grad_gains = mine(take(2 * width).reshape(2, width), 1, own)
    grad_small = mine(take(width * rates_of * HEADS).reshape(width, -1), 0, own)
    taps = (kinds - 1) * width
    grad_conv = mine(take(CONV * taps).reshape(CONV, taps), 1, taps // count)
    grad_gain = take(dim)
    decays_sum = take(2 * HEADS).reshape(2, HEADS)
    return (
        result.reshape(block_in.shape),
        in_grad.reshape(block_in.shape),
        grad_gains,
        grad_in.astype(f32),
        grad_small,
        grad_conv,
        decays_sum[0],
        decays_sum[1],
        grad_gain,
        grad_out_proj.astype(f32),
        grad_gate_up.astype(f32),
        grad_down.astype(f32),
    )


def solution(mesh):
    placed = (
        P(None, "rep", "ctx", None),
        P(None, "rep"),
        P(None, "ctx"),
        P("ctx", None),
        P("ctx", None),
        P(None, "ctx"),
        P(),
        P(),
        P(),
        P("ctx", None),
        P("ctx", None),
        P("ctx", None),
        P(None, "rep", "ctx", None),
    )
    return jax.shard_map(
        per_device,
        mesh=mesh,
        in_specs=placed,
        out_specs=(
            P(None, "rep", "ctx", None),
            P(None, "rep", "ctx", None),
            P(None, "ctx"),
            P("ctx", None),
            P("ctx", None),
            P(None, "ctx"),
            P(),
            P(),
            P(),
            P("ctx", None),
            P("ctx", None),
            P("ctx", None),
        ),
        check_vma=False,
    )
```

time: 2230 us -> 953 us (0.43)
  other arithmetic: 752 us -> 19.6 us
  waiting for transfers between devices: 818 us -> 532 us
  matrix products: 354 us -> 68.4 us
  Pallas kernels: 0 us -> 107 us
  local copies, waits for them, and re-layouts: 131 us -> 53 us
    another operation x20 -> x1, other arithmetic: 652 us -> 0.01 us  [per_device(): smalls = lax.all_gather(small_block, 'ctx', axis=0).reshape(count, -1)]
    all_gather x12 -> x7, waiting for transfers between devices: 436 us -> 123 us  [the longest x1 37.4 us: per_device(): down_part = lax.all_gather(down_part, 'ctx', axis=0, tiled=True)]
    dot_general x104 -> x0, matrix products: 184 us -> none  [the longest x102 178 us: batched(): return jnp.einsum(form, left, right, precision=HIGH_PRECISION)]
    unnamed x23 -> x15, waiting for transfers between devices: 149 us -> 1.59 us
    pallas_call x0 -> x2, Pallas kernels: none -> 107 us  [the longest x1 58.8 us: mixer_backward(): pl.pallas_call(functools.partial(backward_kernel, bool(link)), out_shape=...]
    psum x1 -> x2, waiting for transfers between devices: 71.3 us -> 169 us  [the longest x1 126 us: per_device(): packed = lax.psum(packed, ('rep', 'ctx')).reshape(-1)]
    all_to_all x0 -> x2, blocking collectives: none -> 56.1 us  [the longest x1 30.6 us: to_heads(): lax.all_to_all(split, 'ctx', 0, 0, tiled=True, axis_index_groups=mates)]
    psum x2 -> x0, blocking collectives: 51.6 us -> none  [the longest x1 41 us: per_device(): lax.psum((small_sums[0], small_sums[1], small_sums[2]), ('rep', 'ctx'))]
  transfers between devices with their start and end apart: 24 -> 17, of which waited for: 13 -> 14; matrix products, arithmetic and copies ran while one was open for 45% -> 12% of each run, Pallas kernels for 0% -> 11%
where the time goes in v1:
time: 953 us; the launch traced here: 944 us
  waiting for transfers between devices  532 us (56%)
  blocking collectives  134 us (14%)
  Pallas kernels  107 us (11%)
  matrix products  68.4 us (7%)
  local copies, waits for them, and re-layouts  53 us (6%)
  other arithmetic  19.6 us (2%)
  starting transfers between devices  14.8 us (2%)
  between operations  14.7 us (2%)
    psum x1, waiting for transfers between devices, per_device(): packed = lax.psum(packed, ('rep', 'ctx')).reshape(-1)  126 us
    reduce_scatter x1, waiting for transfers between devices, per_device(): lax.psum_scatter(d_first.reshape(HEADS * rows, width), 'ctx', scatter_dim...  87.9 us
    all_gather x1, blocking collectives, per_device(): smalls = lax.all_gather(small_block, 'ctx', axis=0).reshape(count, -1)  69.8 us
    pallas_call x1, Pallas kernels, mixer_backward(): pl.pallas_call(functools.partial(backward_kernel, bool(link)), out_shape=...  58.8 us
    reduce_scatter x1, waiting for transfers between devices, per_device(): lax.psum_scatter(grad_down.astype(bf16), 'ctx', scatter_dimension=0, tile...  57.8 us
    pallas_call x1, Pallas kernels, mixer_forward(): pl.pallas_call(functools.partial(forward_kernel, bool(link)), out_shape=s...  48.5 us
    psum x1, waiting for transfers between devices, per_device(): grad_in, grad_out_proj = lax.psum((grad_in, grad_out_proj), 'rep')  43.1 us
    all_gather x1, waiting for transfers between devices, per_device(): down_part = lax.all_gather(down_part, 'ctx', axis=0, tiled=True)  37.4 us
  transfers between devices with their start and end apart: 17, of which 14 were waited for; matrix products, arithmetic and copies ran while one was open for 12% of the time, Pallas kernels for 11%

profile of v1, /device:TPU:8, one launch (start us, length us, event | category | flops | bytes accessed | tf_op | source)
XLA Modules:
  0.0 944.1 jit_solution(13112481093450454496)
XLA Ops:
  21.3 69.8 %all_gather.28 = bf16[8,46,128]{2,1,0:T(8,128)(2,1)S(1)} all-gather(bf16[1,46,128]{2,1,0:T(8,128)(2,1)S(1)} %maximum_bitcast_fusion), channel_id=1, replica_groups=mesh['rep'=4,'ctx'=8] {'ctx'}, dimensions={0}, use_global_device_ids=true | all-gather | bytes 105984 | tf_op jit(solution)/shard_map/all_gather | solution.py:684
  101.5 7.3 all-gather.20.cloned.1.call-done
  112.3 8.1 fusion.5.refs_0_
  121.1 48.5 %mixer_forward.1 = (bf16[2,1024,128]{2,1,0:T(8,128)(2,1)}, f32[2,1024,128]{2,1,0:T(8,128)}, f32[32,128,128]{2,1,0:T(8,128)}, f32[32,128,128]{2,1,0:T(8,128)}, f3...) custom-call(f32[2,1024,896]{2,1,0:T(8,128)} %fusion.5.refs_0_, f32[4,640]{1,0:T(4,128)} %bitcast.177, ...), custom_call_target="tpu_custom_call" | custom-call | flops 4026531840 | bytes 15728640 | tf_op jit(solution)/shard_map/mixer_forward/pallas_call | solution.py:328
  170.7 25.6 %all_to_all.20 = bf16[8,256,128]{2,1,0:T(8,128)(2,1)S(1)} all-to-all(bf16[8,256,128]{2,1,0:T(8,128)(2,1)S(1)} %bitcast.158), channel_id=1, replica_groups=mesh['rep'=4,'ctx'=8] {'ctx'}, dimensions={0} | all-to-all | bytes 1048576 | tf_op jit(solution)/shard_map/all_to_all | solution.py:742
  202.1 24.7 %all-gather.14.cloned.1.call-done = bf16[1024,1408]{0,1:T(8,128)(2,1)} async-done(((bf16[128,1408]{0,1:T(8,128)(2,1)}), bf16[1024,1408]{0,1:T(8,128)(2,1)}) %all-gather.14.cloned.1.call-update) | async-done | bytes 2883600 | tf_op jit(solution)/shard_map/all_gather | solution.py:710
  226.8 24.6 %all-gather.12.cloned.1.call-done = bf16[1024,1024]{1,0:T(8,128)(2,1)} async-done(((bf16[256,1024]{1,0:T(8,128)(2,1)}), bf16[1024,1024]{1,0:T(8,128)(2,1)}) %all-gather.12.cloned.1.call-update) | async-done | bytes 2097168 | tf_op jit(solution)/shard_map/all_gather | solution.py:763
  251.5 8.4 fusion.39
  259.9 37.4 %all-gather.22.cloned.1.call-done = bf16[1,704,1024]{2,1,0:T(8,128)(2,1)} async-done(((bf16[1,88,1024]{2,1,0:T(8,128)(2,1)}), bf16[1,704,1024]{2,1,0:T(8,128)(2,1)}) %all-gather.22.cloned.1.call-update) | async-done | bytes 1441808 | tf_op jit(solution)/shard_map/all_gather | solution.py:714
  297.3 23.0 %all-gather.16.cloned.1.call-done = bf16[1024,1024]{1,0:T(8,128)(2,1)} async-done(((bf16[256,1024]{1,0:T(8,128)(2,1)}), bf16[1024,1024]{1,0:T(8,128)(2,1)}) %all-gather.16.cloned.1.call-update) | async-done | bytes 2097168 | tf_op jit(solution)/shard_map/all_gather | solution.py:762
  320.3 7.7 multiply_convert_fusion.1
  340.0 7.8 convolution_convert_fusion
  347.9 18.1 %reduce-scatter.9.cloned.1.call-done = bf16[256,1024]{1,0:T(8,128)(2,1)} async-done(((bf16[1024,1024]{1,0:T(8,128)(2,1)}), bf16[256,1024]{1,0:T(8,128)(2,1)}) %reduce-scatter.9.cloned.1.call-update) | async-done | bytes 524304 | tf_op jit(solution)/shard_map/reduce_scatter | solution.py:778
  367.5 32.7 %reduce-scatter.7.cloned.1.call-done = bf16[256,1024]{1,0:T(8,128)(2,1)} async-done(((bf16[1024,1024]{1,0:T(8,128)(2,1)}), bf16[256,1024]{1,0:T(8,128)(2,1)}) %reduce-scatter.7.cloned.1.call-update) | async-done | bytes 524304 | tf_op jit(solution)/shard_map/reduce_scatter | solution.py:769
  412.2 30.6 %all_to_all.21 = bf16[8,256,128]{2,1,0:T(8,128)(2,1)S(1)} all-to-all(bf16[8,256,128]{2,1,0:T(8,128)(2,1)S(1)} %bitcast.160), channel_id=1, replica_groups=mesh['rep'=4,'ctx'=8] {'ctx'}, dimensions={0} | all-to-all | bytes 1048576 | tf_op jit(solution)/shard_map/all_to_all | solution.py:749
  443.6 58.8 %mixer_backward.1 = (bf16[2,1024,896]{2,1,0:T(8,128)(2,1)}, f32[4,640]{1,0:T(4,128)}, f32[2,128]{1,0:T(2,128)}, f32[1,128]{1,0:T(1,128)}) custom-call(f32[2,1024,896]{2,1,0:T(8,128)} %fusion.5.refs_0_, f32[4,640]{1,0:T(4,128)} %bitcast.178, f32[2,128]{1,0:T(2,128)} %stack.15.refs_2_, f32[1,128]{1,0:T(1,128)} %bitcast.183, ...), custom_call_target="tpu_custom_call" | custom-call | flops 4026531840 | bytes 15728640 | tf_op jit(solution)/shard_map/mixer_backward/pallas_call | solution.py:592
  502.5 7.6 fusion.8
  525.1 31.4 %all-to-all-done.3 = bf16[8,128,768]{1,2,0:T(8,128)(2,1)} async-done(((bf16[8,128,768]{1,2,0:T(8,128)(2,1)}), bf16[8,128,768]{1,2,0:T(8,128)(2,1)}, u32[]{:S(2)}, u32[]{:S(2)}) %all-to-all-start.3) | async-done | bytes 1572896 | tf_op jit(solution)/shard_map/all_to_all | solution.py:850
  559.2 10.4 %reduce-scatter.13.cloned.1.call-done = bf16[128,1024]{1,0:T(8,128)(2,1)} async-done(((bf16[1024,1024]{1,0:T(8,128)(2,1)}), bf16[128,1024]{1,0:T(8,128)(2,1)}) %reduce-scatter.13.cloned.1.call-update) | async-done | bytes 262160 | tf_op jit(solution)/shard_map/reduce_scatter | solution.py:842
  579.7 57.8 %reduce-scatter.17.cloned.1.call-done = bf16[88,1024]{1,0:T(8,128)(2,1)} async-done(((bf16[704,1024]{1,0:T(8,128)(2,1)}), bf16[88,1024]{1,0:T(8,128)(2,1)}) %reduce-scatter.17.cloned.1.call-update) | async-done | bytes 180240 | tf_op jit(solution)/shard_map/reduce_scatter | solution.py:840
  637.5 8.4 all_gather.35
  664.5 43.1 %all-reduce.8.cloned.1.call-done = (bf16[128,6144]{0,1:T(8,128)(2,1)}, bf16[128,1024]{1,0:T(8,128)(2,1)}) async-done(((bf16[128,6144]{0,1:T(8,128)(2,1)}, bf16[128,1024]{1,0:T(8,128)(2,1)}), (bf16[128,6144]{0,1:T(8,128)(2,1)}, bf16[128,1024]{1,0:T(8,128)(2,1)})) %all-reduce.8.cloned.1.call-update) | async-done | bytes 1835024 | tf_op jit(solution)/shard_map/psum | solution.py:854
  711.6 87.9 %reduce-scatter.11.cloned.1.call-done = bf16[256,1024]{1,0:T(8,128)(2,1)} async-done(((bf16[2048,1024]{1,0:T(8,128)(2,1)}), bf16[256,1024]{1,0:T(8,128)(2,1)}) %reduce-scatter.11.cloned.1.call-update) | async-done | bytes 524304 | tf_op jit(solution)/shard_map/reduce_scatter | solution.py:824
  803.9 126.2 %all-reduce.6.cloned.1.call-done = f32[370,128]{1,0:T(8,128)} async-done(((f32[370,128]{1,0:T(8,128)}), f32[370,128]{1,0:T(8,128)}) %all-reduce.6.cloned.1.call-update) | async-done | bytes 189456 | tf_op jit(solution)/shard_map/psum | solution.py:873
  (178 shorter events, 123.4 us)
Async XLA Ops:
  7.2 193.0 %copy-start = (bf16[352,1024]{1,0:T(8,128)(2,1)S(1)}, bf16[352,1024]{1,0:T(8,128)(2,1)}, u32[]{:S(2)}) copy-start(bf16[352,1024]{1,0:T(8,128)(2,1)} %param.24) | copy-start | bytes 2162692
  7.2 101.7 %all-gather.20.cloned.1.call-start = ((), (), s32[]{:S(2)}) async-start(), calls=%async_computation.22 | async-start | bytes 4718592 | tf_op jit(solution)/shard_map/all_gather | solution.py:694
  7.9 188.6 %all-gather.10.cloned.1.call-start = ((), (), s32[]{:S(2)}) async-start(), calls=%async_computation.10 | async-start | bytes 2359296 | tf_op jit(solution)/shard_map/all_gather | solution.py:705
  11.8 85.2 %all-to-all-start = ((bf16[8,128,6,128]{1,3,2,0:T(8,128)(2,1)}), bf16[8,128,6,128]{1,3,2,0:T(8,128)(2,1)}, u32[]{:S(2)}, u32[]{:S(2)}) async-start(bf16[8,128,6,128]{1,3,2,0:T(8,128)(2,1)} %copy.101), calls=%async_computation | async-start | bytes 3145728 | tf_op jit(solution)/shard_map/all_to_all | solution.py:698
  18.3 73.0 %copy-start.19 = (f32[8]{0:T(128)S(1)}, f32[8]{0:T(128)}, u32[]{:S(2)}) copy-start(f32[8]{0:T(128)} %param.20) | copy-start | bytes 100
  18.3 73.6 %copy-start.20 = (f32[8]{0:T(128)S(1)}, f32[8]{0:T(128)}, u32[]{:S(2)}) copy-start(f32[8]{0:T(128)} %param.19) | copy-start | bytes 100
  18.3 208.6 %all-gather.14.cloned.1.call-start = ((), (), s32[]{:S(2)}) async-start(), calls=%async_computation.12 | async-start | bytes 3244032 | tf_op jit(solution)/shard_map/all_gather | solution.py:710
  21.0 230.5 %all-gather.12.cloned.1.call-start = ((), (), s32[]{:S(2)}) async-start(), calls=%async_computation.11 | async-start | bytes 2621440 | tf_op jit(solution)/shard_map/all_gather | solution.py:763
  200.2 97.1 %all-gather.22.cloned.1.call-start = ((), (), s32[]{:S(2)}) async-start(), calls=%async_computation.23 | async-start | bytes 1622016 | tf_op jit(solution)/shard_map/all_gather | solution.py:714
  200.9 119.4 %all-gather.16.cloned.1.call-start = ((), (), s32[]{:S(2)}) async-start(), calls=%async_computation.14 | async-start | bytes 2621440 | tf_op jit(solution)/shard_map/all_gather | solution.py:762
  202.1 164.0 %reduce-scatter.9.cloned.1.call-start = ((), (), s32[]{:S(2)}) async-start(), calls=%async_computation.15 | async-start | bytes 2621440 | tf_op jit(solution)/shard_map/reduce_scatter | solution.py:778
  334.4 65.8 %reduce-scatter.7.cloned.1.call-start = ((), (), s32[]{:S(2)}) async-start(), calls=%async_computation.13 | async-start | bytes 2621440 | tf_op jit(solution)/shard_map/reduce_scatter | solution.py:769
  339.5 183.5 %reduce-scatter.15.cloned.1.call-start = ((), (), s32[]{:S(2)}) async-start(), calls=%async_computation.19 | async-start | bytes 3244032 | tf_op jit(solution)/shard_map/reduce_scatter | solution.py:834
  347.8 55.0 %copy-start.4 = (bf16[256,8,128]{0,2,1:T(8,128)(2,1)S(1)}, bf16[256,8,128]{0,2,1:T(8,128)(2,1)}, u32[]{:S(2)}) copy-start(bf16[256,8,128]{0,2,1:T(8,128)(2,1)} %copy-done.3) | copy-start | bytes 1572868
  347.8 221.8 %reduce-scatter.13.cloned.1.call-start = ((), (), s32[]{:S(2)}) async-start(), calls=%async_computation.18 | async-start | bytes 2359296 | tf_op jit(solution)/shard_map/reduce_scatter | solution.py:842
  404.9 232.7 %reduce-scatter.17.cloned.1.call-start = ((), (), s32[]{:S(2)}) async-start(), calls=%async_computation.21 | async-start | bytes 1622016 | tf_op jit(solution)/shard_map/reduce_scatter | solution.py:840
  515.8 40.6 %all-to-all-start.3 = ((bf16[8,128,768]{1,2,0:T(8,128)(2,1)}), bf16[8,128,768]{1,2,0:T(8,128)(2,1)}, u32[]{:S(2)}, u32[]{:S(2)}) async-start(bf16[8,128,768]{1,2,0:T(8,128)(2,1)} %copy.115), calls=%async_computation.6 | async-start | bytes 3145728 | tf_op jit(solution)/shard_map/all_to_all | solution.py:850
  523.0 134.7 %all-gather.18.cloned.1.call-start = ((), (), s32[]{:S(2)}) async-start(), calls=%async_computation.20 | async-start | bytes 1802240 | tf_op jit(solution)/shard_map/all_gather | solution.py:837
  525.0 182.6 %all-reduce.8.cloned.1.call-start = ((), (), s32[]{:S(2)}) async-start(), calls=%async_computation.24 | async-start | bytes 3670016 | tf_op jit(solution)/shard_map/psum | solution.py:854
  569.7 229.8 %reduce-scatter.11.cloned.1.call-start = ((), (), s32[]{:S(2)}) async-start(), calls=%async_computation.16 | async-start | bytes 4718592 | tf_op jit(solution)/shard_map/reduce_scatter | solution.py:824
  579.5 67.7 %slice-start = ((f32[1024,896]{1,0:T(8,128)}), f32[1024,3]{1,0:T(8,128)S(1)}, s32[]{:S(2)}) async-start(f32[1024,896]{1,0:T(8,128)} %copy-done.7), calls=%async_computation.25 | async-start | bytes 1048576 | tf_op jit(solution)/shard_map/slice | solution.py:858
  579.5 350.6 %all-reduce.6.cloned.1.call-start = ((), (), s32[]{:S(2)}) async-start(), calls=%async_computation.17 | async-start | bytes 385024 | tf_op jit(solution)/shard_map/psum | solution.py:873
  707.6 93.4 %copy-start.21 = (f32[1,128]{1,0:T(1,128)S(1)}, f32[1,128]{1,0:T(1,128)}, u32[]{:S(2)}) copy-start(f32[1,128]{1,0:T(1,128)} %get-tuple-element.32) | copy-start | bytes 1540
  710.7 226.6 %copy-start.1 = (bf16[352,1024]{1,0:T(8,128)(2,1)S(1)}, bf16[352,1024]{1,0:T(8,128)(2,1)}, u32[]{:S(2)}) copy-start(bf16[352,1024]{1,0:T(8,128)(2,1)} %param.24) | copy-start | bytes 2162692
  (18 other events, 162.1 us)
Sparse Core Ops, SparseCore 0:
  10.2 98.6 all-gather.19
  111.0 48.6 all-gather.9
  162.4 64.4 all-gather.13
  228.8 22.6 all-gather.11
  254.1 43.1 all-gather.21
  299.3 20.9 all-gather.15
  334.5 31.4 reduce-scatter.8
  368.7 31.4 reduce-scatter.6
  404.3 82.0 reduce-scatter.14
  489.7 79.8 reduce-scatter.12
  573.6 63.8 reduce-scatter.16
  639.5 18.2 all-gather.17
  660.3 47.3 all-reduce.7
  711.1 88.3 reduce-scatter.10
  805.7 124.2 all-reduce.5

commit v2 on v1

--- a/solution.py
+++ b/solution.py
@@ -12,6 +12,557 @@
 HEADS = 8
 EPS = 1e-06
 WIDE = 2 * STRETCH
+
+
+MESH = pl.DeviceIdType.MESH
+ROWS = 2
+COLS = HEADS // ROWS
+
+
+class Spot:
+    def __init__(self, groups):
+        place = lax.axis_index("ctx")
+        self.mate = lax.rem(place, HEADS)
+        self.base = place - self.mate
+        self.col = lax.div(self.mate, ROWS)
+        self.row = lax.rem(self.mate, ROWS)
+        self.groups = groups
+        self.group = lax.axis_index("rep")
+        self.side = lax.rem(self.group, 2)
+        self.pair = lax.div(self.group, 2)
+        self.twin = self.group + 1 - 2 * self.side
+
+    def to_mate(self, mate):
+        return {"ctx": self.base + mate}
+
+    def to_group(self, group):
+        return {"rep": group}
+
+    def mate_off(self, k):
+        return lax.rem(self.mate + k, HEADS)
+
+    def group_off(self, k):
+        return lax.rem(self.group + 2 * k, self.groups)
+
+    def barrier(self, team=True, copies=True):
+        sem = pltpu.get_barrier_semaphore()
+        others = []
+        if team:
+            others += [self.to_mate(self.mate_off(k)) for k in range(1, HEADS)]
+        if copies:
+            others += [self.to_group(self.twin)]
+            others += [self.to_group(self.group_off(k)) for k in range(1, self.groups // 2)]
+        for other in others:
+            pl.semaphore_signal(sem, inc=1, device_id=other, device_id_type=MESH)
+        pl.semaphore_wait(sem, len(others))
+
+
+def remote(src, dst, send, recv, where):
+    return pltpu.make_async_remote_copy(
+        src_ref=src,
+        dst_ref=dst,
+        send_sem=send,
+        recv_sem=recv,
+        device_id=where,
+        device_id_type=MESH,
+    )
+
+
+TEAM_SEMS = 3 * COLS + 1
+
+
+def team_gather(spot, src, out, send, recv, own):
+    mate, col = spot.mate, spot.col
+    up, down = spot.to_mate(mate + ROWS), spot.to_mate(mate - ROWS)
+    across = spot.to_mate(mate + 1 - 2 * spot.row)
+    other = mate + 1 - 2 * spot.row
+    local = pltpu.make_async_copy(src, out(mate), own)
+
+    def hop(block, origin, slot, where):
+        return remote(block, out(origin), send.at[slot], recv.at[slot], where)
+
+    rise, fall, cross_low, cross_high = 0, COLS - 1, 2 * COLS - 2, 3 * COLS - 3
+    last = COLS - 1
+    local.start()
+
+    @pl.when(col < last)
+    def _():
+        hop(src, mate, rise, up).start()
+
+    @pl.when(col > 0)
+    def _():
+        hop(src, mate, fall, down).start()
+
+    hop(src, mate, cross_low, across).start()
+    yield
+    for k in range(1, COLS):
+        below, above = mate - ROWS * k, mate + ROWS * k
+
+        @pl.when(col >= k)
+        def _():
+            hop(out(below), below, rise + k - 1, up).wait_recv()
+            if k < last:
+
+                @pl.when(col < last)
+                def _():
+                    hop(out(below), below, rise + k, up).start()
+
+            hop(out(below), below, cross_low + k, across).start()
+
+        @pl.when(col + k <= last)
+        def _():
+            hop(out(above), above, fall + k - 1, down).wait_recv()
+            if k < last:
+
+                @pl.when(col > 0)
+                def _():
+                    hop(out(above), above, fall + k, down).start()
+
+            hop(out(above), above, cross_high + k, across).start()
+
+        yield
+    hop(src, other, cross_low, across).wait_recv()
+    for k in range(1, COLS):
+
+        @pl.when(col >= k)
+        def _():
+            hop(src, other - ROWS * k, cross_low + k, across).wait_recv()
+
+        @pl.when(col + k <= last)
+        def _():
+            hop(src, other + ROWS * k, cross_high + k, across).wait_recv()
+
+    @pl.when(col < last)
+    def _():
+        hop(src, mate, rise, up).wait_send()
+
+    @pl.when(col > 0)
+    def _():
+        hop(src, mate, fall, down).wait_send()
+
+    hop(src, mate, cross_low, across).wait_send()
+    for k in range(1, COLS):
+
+        @pl.when(col >= k)
+        def _():
+            if k < last:
+
+                @pl.when(col < last)
+                def _():
+                    hop(src, mate, rise + k, up).wait_send()
+
+            hop(src, mate, cross_low + k, across).wait_send()
+
+        @pl.when(col + k <= last)
+        def _():
+            if k < last:
+
+                @pl.when(col > 0)
+                def _():
+                    hop(src, mate, fall + k, down).wait_send()
+
+            hop(src, mate, cross_high + k, across).wait_send()
+
+    local.wait()
+    yield
+
+
+def rep_gather(spot, src, out, send, recv, own):
+    group, twin, half = spot.group, spot.twin, spot.groups // 2
+    local = None
+    if own is not None:
+        local = pltpu.make_async_copy(src, out(group), own)
+        local.start()
+
+    def hop(block, origin, slot, where):
+        return remote(block, out(origin), send.at[slot], recv.at[slot], spot.to_group(where))
+
+    hop(src, group, 0, twin).start()
+    for k in range(1, half):
+        hop(src, group, k, spot.group_off(k)).start()
+    yield
+    for k in range(1, half):
+        origin = spot.group_off(half - k)
+        hop(out(origin), origin, k, twin).wait_recv()
+        hop(out(origin), origin, half + k, twin).start()
+    yield
+    hop(src, twin, 0, twin).wait_recv()
+    for k in range(1, half):
+        origin = lax.rem(twin + 2 * (half - k), spot.groups)
+        hop(src, origin, half + k, twin).wait_recv()
+    hop(src, group, 0, twin).wait_send()
+    for k in range(1, half):
+        hop(src, group, k, twin).wait_send()
+        hop(src, group, half + k, twin).wait_send()
+    if local is not None:
+        local.wait()
+    yield
+
+
+def team_exchange(spot, src, dst, send, recv, own):
+    local = pltpu.make_async_copy(src(spot.mate), dst(spot.mate), own)
+    local.start()
+
+    def hop(k):
+        to = spot.mate_off(k)
+        return remote(src(to), dst(spot.mate), send.at[k], recv.at[k], spot.to_mate(to))
+
+    for k in range(1, HEADS):
+        hop(k).start()
+    yield
+    for k in range(1, HEADS):
+        hop(k).wait_recv()
+    for k in range(1, HEADS):
+        hop(k).wait_send()
+    local.wait()
+    yield
+
+
+def dma(*shape):
+    return pltpu.SemaphoreType.DMA(shape)
+
+
+ANY = pl.BlockSpec(memory_space=pl.ANY)
+IN_VMEM = pl.BlockSpec(memory_space=pltpu.VMEM)
+
+
+def finish(*steps):
+    for step in steps:
+        for _ in step:
+            pass
+
+
+def prologue_kernel(groups, tokens_in, pieces, smalls, given, sequence, w_head, smalls_all, given_all, *sems):
+    (ex_send, ex_recv, sm_send, sm_recv, tok_send, tok_recv, rep_send, rep_recv, w_send, w_recv, own) = sems
+    spot = Spot(groups)
+    span = tokens_in.shape[1]
+    spot.barrier()
+    small = team_exchange(
+        spot, lambda m: smalls, lambda m: smalls_all.at[m], sm_send, sm_recv, own.at[0]
+    )
+    exchange = team_exchange(
+        spot,
+        lambda m: pieces.at[m, spot.group],
+        lambda m: w_head.at[m, spot.group],
+        ex_send,
+        ex_recv,
+        own.at[1],
+    )
+    gathers = [
+        team_gather(
+            spot,
+            tokens_in.at[seq],
+            lambda m, seq=seq: sequence.at[seq, pl.ds(pl.multiple_of(m * span, span), span)],
+            tok_send.at[seq],
+            tok_recv.at[seq],
+            own.at[4 + seq],
+        )
+        for seq in range(tokens_in.shape[0])
+    ]
+    copies = rep_gather(spot, given, lambda g: given_all.at[g], rep_send, rep_recv, own.at[2])
+    next(exchange)
+    next(small)
+    for gather in gathers:
+        next(gather)
+    next(copies)
+    finish(exchange)
+    weights = rep_gather(
+        spot, w_head.at[:, spot.group], lambda g: w_head.at[:, g], w_send, w_recv, None
+    )
+    next(weights)
+    for _ in range(1, COLS):
+        for gather in gathers:
+            next(gather)
+    next(weights)
+    finish(weights, copies, small, *gathers)
+
+
+def prologue(tokens_in, pieces, smalls, given, groups):
+    seqs, span, width = tokens_in.shape
+    return pl.pallas_call(
+        functools.partial(prologue_kernel, groups),
+        out_shape=(
+            jax.ShapeDtypeStruct((seqs, HEADS * span, width), tokens_in.dtype),
+            jax.ShapeDtypeStruct(pieces.shape, pieces.dtype),
+            jax.ShapeDtypeStruct((HEADS,) + smalls.shape, smalls.dtype),
+            jax.ShapeDtypeStruct((groups,) + given.shape, given.dtype),
+        ),
+        in_specs=[ANY] * 4,
+        out_specs=[ANY] * 4,
+        scratch_shapes=[
+            dma(HEADS), dma(HEADS), dma(HEADS), dma(HEADS),
+            dma(seqs, TEAM_SEMS), dma(seqs, TEAM_SEMS),
+            dma(groups), dma(groups), dma(groups), dma(groups), dma(4 + seqs),
+        ],
+        compiler_params=pltpu.CompilerParams(collective_id=1, has_side_effects=True),
+        name="prologue",
+    )(tokens_in, pieces, smalls, given)
+
+
+def copies_kernel(groups, block, out, send, recv, own):
+    spot = Spot(groups)
+    spot.barrier(team=False)
+    finish(rep_gather(spot, block, lambda g: out.at[g], send, recv, own.at[0]))
+
+
+def gather_copies(block, groups, number):
+    return pl.pallas_call(
+        functools.partial(copies_kernel, groups),
+        out_shape=jax.ShapeDtypeStruct((groups,) + block.shape, block.dtype),
+        in_specs=[ANY],
+        out_specs=ANY,
+        scratch_shapes=[dma(groups), dma(groups), dma(1)],
+        compiler_params=pltpu.CompilerParams(collective_id=number, has_side_effects=True),
+        name="gather_copies",
+    )(block)
+
+
+def rep_reduce(spot, part, pairs, sums, others, send, recv):
+    half, side = spot.groups // 2, spot.side
+
+    def to_twin(k):
+        return remote(
+            part(2 * k + 1 - side), pairs.at[k], send.at[k], recv.at[k], spot.to_group(spot.twin)
+        )
+
+    def onward(k):
+        slot = half + k
+        return remote(
+            sums.at[k], others.at[k], send.at[slot], recv.at[slot], spot.to_group(spot.group_off(k))
+        )
+
+    for k in range(half):
+        to_twin(k).start()
+    yield
+    for k in range(half):
+        to_twin(k).wait_recv()
+
+    def both(pair):
+        return part(2 * pair + side)[...].astype(jnp.float32) + pairs[pair].astype(jnp.float32)
+
+    for k in range(1, half):
+        sums[k] = both(lax.rem(spot.pair + k, half)).astype(sums.dtype)
+        onward(k).start()
+    yield
+    total = both(spot.pair)
+    for k in range(1, half):
+        onward(k).wait_recv()
+        total = total + others[k].astype(jnp.float32)
+    for k in range(half):
+        to_twin(k).wait_send()
+    for k in range(1, half):
+        onward(k).wait_send()
+    yield total
+
+
+def reduce_kernel(groups, parts, out, pairs, sums, others, send, recv):
+    spot = Spot(groups)
+    spot.barrier(team=False)
+    *_, total = rep_reduce(spot, lambda g: parts.at[g], pairs, sums, others, send, recv)
+    out[...] = total
+
+
+def reduce_copies(parts, number):
+    groups = parts.shape[0]
+    block = (groups // 2,) + parts.shape[1:]
+    return pl.pallas_call(
+        functools.partial(reduce_kernel, groups),
+        out_shape=jax.ShapeDtypeStruct(parts.shape[1:], jnp.float32),
+        in_specs=[IN_VMEM],
+        out_specs=IN_VMEM,
+        scratch_shapes=[pltpu.VMEM(block, parts.dtype)] * 3 + [dma(groups), dma(groups)],
+        compiler_params=pltpu.CompilerParams(
+            collective_id=number, has_side_effects=True, vmem_limit_bytes=40 * 2**20
+        ),
+        name="reduce_copies",
+    )(parts)
+
+
+def team_reduce(spot, part, seqs, across_in, sums, rising, falling, total, send, recv):
+    mate, col, row = spot.mate, spot.col, spot.row
+    up, down = spot.to_mate(mate + ROWS), spot.to_mate(mate - ROWS)
+    across = spot.to_mate(mate + 1 - 2 * row)
+    last = COLS - 1
+    f32 = jnp.float32
+
+    def cross(seq, d):
+        return remote(
+            part(ROWS * d + 1 - row, seq),
+            across_in.at[seq, d],
+            send.at[0, seq, d],
+            recv.at[0, seq, d],
+            across,
+        )
+
+    def rise(seq, d):
+        return remote(
+            sums.at[seq, d], rising.at[seq, d], send.at[1, seq, d], recv.at[1, seq, d], up
+        )
+
+    def fall(seq, d):
+        return remote(
+            sums.at[seq, d], falling.at[seq, d], send.at[2, seq, d], recv.at[2, seq, d], down
+        )
+
+    order_out = [d for pair in zip(range(last, -1, -1), range(COLS)) for d in pair][:COLS]
+    for d in order_out:
+        for seq in range(seqs):
+            cross(seq, d).start()
+    yield
+    for d in order_out:
+        for seq in range(seqs):
+            cross(seq, d).wait_recv()
+
+            def both(seq=seq, d=d):
+                own = part(ROWS * d + row, seq)[...].astype(f32)
+                return own + across_in[seq, d].astype(f32)
+
+            @pl.when(col == d)
+            def _():
+                total[seq] = both()
+
+            if d > 0:
+
+                @pl.when(col == 0)
+                def _():
+                    sums[seq, d] = both().astype(sums.dtype)
+
+                @pl.when((col < d) & (col > 0))
+                def _():
+                    rise(seq, d).wait_recv()
+                    sums[seq, d] = (both() + rising[seq, d].astype(f32)).astype(sums.dtype)
+
+                @pl.when(col < d)
+                def _():
+                    rise(seq, d).start()
+
+            if d < last:
+
+                @pl.when(col == last)
+                def _():
+                    sums[seq, d] = both().astype(sums.dtype)
+
+                @pl.when((col > d) & (col < last))
+                def _():
+                    fall(seq, d).wait_recv()
+                    sums[seq, d] = (both() + falling[seq, d].astype(f32)).astype(sums.dtype)
+
+                @pl.when(col > d)
+                def _():
+                    fall(seq, d).start()
+
+        yield
+    for d in range(COLS):
+        for seq in range(seqs):
+            if d > 0:
+
+                @pl.when(col == d)
+                def _():
+                    rise(seq, d).wait_recv()
+                    total[seq] += rising[seq, d].astype(f32)
+
+            if d < last:
+
+                @pl.when(col == d)
+                def _():
+                    fall(seq, d).wait_recv()
+                    total[seq] += falling[seq, d].astype(f32)
+
+    for d in range(COLS):
+        for seq in range(seqs):
+            cross(seq, d).wait_send()
+
+            @pl.when(col < d)
+            def _():
+                rise(seq, d).wait_send()
+
+            @pl.when(col > d)
+            def _():
+                fall(seq, d).wait_send()
+
+    yield
+
+
+def epilogue_kernel(groups, d_first, grads, smalls, *refs):
+    (d_own, grads_all, smalls_all, across_in, sums, rising, falling,
+     pairs, pair_sums, others, quarter, copies, small_sum,
+     t_send, t_recv, r_send, r_recv, e_send, e_recv, g_send, g_recv,
+     s_send, s_recv, x_send, x_recv, own) = refs
+    spot = Spot(groups)
+    seqs, length, _ = d_first.shape
+    span = length // HEADS
+    spot.barrier()
+    tokens = team_reduce(
+        spot,
+        lambda m, seq: d_first.at[seq, pl.ds(pl.multiple_of(m * span, span), span)],
+        seqs, across_in, sums, rising, falling, d_own, t_send, t_recv,
+    )
+    weights = rep_reduce(
+        spot, lambda g: grads.at[:, g], pairs, pair_sums, others, r_send, r_recv
+    )
+    small = rep_gather(spot, smalls, lambda g: copies.at[g], s_send, s_recv, own.at[0])
+    next(weights)
+    next(small)
+    next(tokens)
+    next(weights)
+    next(small)
+    next(tokens)
+    quarter[...] = next(weights).astype(quarter.dtype)
+    exchange = team_exchange(
+        spot,
+        lambda m: quarter.at[m],
+        lambda m: grads_all.at[spot.group, m],
+        e_send, e_recv, own.at[1],
+    )
+    next(exchange)
+    finish(small)
+    small_sum[...] = sum(copies[g] for g in range(groups))
+    spread = team_exchange(
+        spot, lambda m: small_sum, lambda m: smalls_all.at[m], x_send, x_recv, own.at[2]
+    )
+    next(spread)
+    next(tokens)
+    finish(exchange)
+    gathered = rep_gather(
+        spot, grads_all.at[spot.group], lambda g: grads_all.at[g], g_send, g_recv, None
+    )
+    next(gathered)
+    next(tokens)
+    next(gathered)
+    finish(tokens, gathered, spread)
+
+
+def epilogue(d_first, grads, smalls):
+    seqs, length, width = d_first.shape
+    _, groups, piece, cols = grads.shape
+    half = groups // 2
+    low_, f32 = d_first.dtype, jnp.float32
+    span = length // HEADS
+    block = pltpu.VMEM((seqs, COLS, span, width), low_)
+    part = pltpu.VMEM((half, HEADS, piece, cols), low_)
+    return pl.pallas_call(
+        functools.partial(epilogue_kernel, groups),
+        out_shape=(
+            jax.ShapeDtypeStruct((seqs, span, width), f32),
+            jax.ShapeDtypeStruct((groups, HEADS, piece, cols), low_),
+            jax.ShapeDtypeStruct((HEADS,) + smalls.shape, f32),
+        ),
+        in_specs=[IN_VMEM] * 3,
+        out_specs=[IN_VMEM] * 3,
+        scratch_shapes=[
+            block, block, block, block, part, part, part,
+            pltpu.VMEM((HEADS, piece, cols), low_),
+            pltpu.VMEM((groups,) + smalls.shape, f32),
+            pltpu.VMEM(smalls.shape, f32),
+            dma(3, seqs, COLS), dma(3, seqs, COLS),
+            dma(groups), dma(groups), dma(HEADS), dma(HEADS), dma(groups), dma(groups),
+            dma(groups), dma(groups), dma(HEADS), dma(HEADS), dma(3),
+        ],
+        compiler_params=pltpu.CompilerParams(
+            collective_id=6, has_side_effects=True, vmem_limit_bytes=50 * 2**20
+        ),
+        name="epilogue",
+    )(d_first, grads, smalls)
 
 
 def low(a):
@@ -192,18 +743,50 @@
     return jnp.concatenate([column, column], axis=0)
 
 
-def forward_kernel(linked, *refs):
+def forward_kernel(linked, groups, *refs):
+    proj, conv, decay, gain, *refs = refs
+    halo = None
     if linked:
-        proj, conv, decay, gain, halo, start, *refs = refs
-        *refs, final, product, local, offset = refs
-    else:
-        proj, conv, decay, gain, *refs = refs
-        halo, (*refs, local, offset) = None, refs
-    mixer, out, fresh, inv, weights, trans, states = refs
+        halo, start, *refs = refs
+    if groups:
+        *parts, refs = refs[0], refs[1], refs[2], refs[3:]
+    out, fresh, inv, weights, trans, states, *refs = refs
+    if linked:
+        final, product, *refs = refs
+    if groups:
+        mixed, *wholes, refs = refs[0], refs[1], refs[2], refs[3], refs[4:]
+    local, offset, mixer, *sems = refs
     seqs, length, _ = proj.shape
     dim = gain.shape[1]
     blocks = length // STRETCH
-    together = 2 if blocks % 2 == 0 else 1
+    span = length // HEADS
+    together = span // STRETCH
+    turns = blocks // together
+    plan = {}
+    if groups:
+        sends, recvs, c_send, c_recv, x_send, x_recv, own = sems
+        spot = Spot(groups)
+        spot.barrier()
+        first_part = team_gather(
+            spot, parts[0], lambda m: wholes[0].at[m, spot.group],
+            sends.at[0], recvs.at[0], own.at[0],
+        )
+        gathers = [
+            team_gather(
+                spot, parts[k], lambda m, k=k: wholes[k].at[m], sends.at[k], recvs.at[k], own.at[k]
+            )
+            for k in (1, 2)
+        ]
+        copies = rep_gather(
+            spot, wholes[0].at[:, spot.group], lambda g: wholes[0].at[:, g], c_send, c_recv, None
+        )
+        next(first_part)
+        for gather in gathers:
+            next(gather)
+        plan = {
+            2: [first_part], 3: gathers, 4: [first_part], 5: gathers, 6: [first_part],
+            7: gathers,
+        }
     masks = level_masks()
     row, col = iotas(dim, dim)
     diagonal = row == col
@@ -257,7 +840,16 @@
             states[at] = fold(dot(to_end, right_nn(halves(value)), ((0,), (0,))))
         return 0
 
-    lax.fori_loop(0, blocks // together, first, 0)
+    reached = 0
+    for turn in sorted(plan):
+        lax.fori_loop(reached, turn, first, 0)
+        reached = turn
+        for step in plan[turn]:
+            next(step)
+    lax.fori_loop(reached, turns, first, 0)
+    if groups:
+        finish(first_part)
+        next(copies)
 
     def chain(block, carried):
         new = []
@@ -281,6 +873,25 @@
     if linked:
         for seq in range(seqs):
             final[seq] = ended[seq]
+    if groups:
+        next(copies)
+
+    def block_of(ref, mate):
+        return ref.at[:, pl.ds(pl.multiple_of(mate * span, span), span)]
+
+    def columns_of(ref, mate):
+        return ref.at[:, :, pl.ds(pl.multiple_of(mate * dim, dim), dim)]
+
+    def to_mate(mate, slot):
+        return remote(
+            block_of(mixer, mate), columns_of(mixed, spot.mate),
+            x_send.at[slot], x_recv.at[slot], spot.to_mate(mate),
+        )
+
+    def to_self():
+        return pltpu.make_async_copy(
+            block_of(mixer, spot.mate), columns_of(mixed, spot.mate), own.at[3]
+        )
 
     def last(step, _):
         units = spots(step)
@@ -303,48 +914,76 @@
             mixer[seq, pl.ds(base, STRETCH)] = low(
                 result * scale * gain[...] * (gate * sigmoid(gate))
             )
+        if groups:
+            slot = lax.rem(step - spot.mate + HEADS, HEADS)
+
+            @pl.when(slot == 0)
+            def _():
+                to_self().start()
+
+            @pl.when(slot != 0)
+            def _():
+                to_mate(step, slot).start()
+
         return 0
 
-    lax.fori_loop(0, blocks // together, last, 0)
-
-
-def mixer_forward(proj, conv, decay, gain, link=()):
+    lax.fori_loop(0, turns, last, 0)
+    if groups:
+        finish(copies, *gathers)
+        for k in range(1, HEADS):
+            to_mate(spot.mate_off(k), k).wait_recv()
+        for k in range(1, HEADS):
+            to_mate(spot.mate_off(k), k).wait_send()
+        to_self().wait()
+
+
+def mixer_forward(proj, conv, decay, gain, parts=(), groups=0, link=()):
     seqs, length, _ = proj.shape
     dim = gain.shape[1]
     units = seqs * (length // STRETCH)
     square = jax.ShapeDtypeStruct((units, WIDE, dim), jnp.float32)
     state = jax.ShapeDtypeStruct((seqs, dim, dim), jnp.float32)
-    shapes = (
-        jax.ShapeDtypeStruct((seqs, length, dim), jnp.bfloat16),
-        jax.ShapeDtypeStruct((seqs, length, dim), jnp.float32),
-        square,
-        square,
-        square,
-        square,
-        square,
-    )
+    shapes = (jax.ShapeDtypeStruct((seqs, length, dim), jnp.float32),) + (square,) * 5
     if link:
         shapes += (state, state)
+    specs = [IN_VMEM] * len(shapes)
+    scratch = [
+        pltpu.VMEM((units, STRETCH, WIDE), jnp.float32),
+        pltpu.VMEM((units, STRETCH, dim), jnp.float32),
+        pltpu.VMEM((seqs, length, dim), jnp.bfloat16),
+    ]
+    if groups:
+        low_ = jnp.bfloat16
+        shapes += (
+            jax.ShapeDtypeStruct((seqs, length // HEADS, HEADS * dim), low_),
+            jax.ShapeDtypeStruct((HEADS, groups) + parts[0].shape, low_),
+            jax.ShapeDtypeStruct((HEADS,) + parts[1].shape, low_),
+            jax.ShapeDtypeStruct((HEADS,) + parts[2].shape, low_),
+        )
+        specs += [ANY] * 4
+        scratch += [dma(3, TEAM_SEMS), dma(3, TEAM_SEMS), dma(groups), dma(groups)]
+        scratch += [dma(HEADS), dma(HEADS), dma(4)]
     return pl.pallas_call(
-        functools.partial(forward_kernel, bool(link)),
+        functools.partial(forward_kernel, bool(link), groups),
         out_shape=shapes,
-        in_specs=[pl.BlockSpec(memory_space=pltpu.VMEM)] * (4 + len(link)),
-        out_specs=[pl.BlockSpec(memory_space=pltpu.VMEM)] * len(shapes),
-        scratch_shapes=[
-            pltpu.VMEM((units, STRETCH, WIDE), jnp.float32),
-            pltpu.VMEM((units, STRETCH, dim), jnp.float32),
-        ],
-        compiler_params=pltpu.CompilerParams(vmem_limit_bytes=56 * 2**20),
+        in_specs=[IN_VMEM] * (4 + len(link)) + [ANY] * len(parts),
+        out_specs=specs,
+        scratch_shapes=scratch,
+        compiler_params=pltpu.CompilerParams(
+            vmem_limit_bytes=56 * 2**20,
+            collective_id=2 if groups else None,
+            has_side_effects=bool(groups),
+        ),
         cost_estimate=pl.CostEstimate(
             flops=units * 60 * WIDE * WIDE * WIDE,
             bytes_accessed=units * WIDE * WIDE * 30,
             transcendentals=units * WIDE * WIDE * 8,
         ),
         name="mixer_forward",
-    )(proj, conv, decay, gain, *link)
-
-
-def backward_kernel(linked, *refs):
+    )(proj, conv, decay, gain, *link, *parts)
+
+
+def backward_kernel(linked, groups, *refs):
     proj, conv, decay, gain, out, fresh, inv, weights, trans, states, d_mixer, *refs = refs
     if linked:
         halo, end_state, *refs = refs
@@ -352,11 +991,37 @@
     else:
         halo = None
         d_proj, d_conv, d_small_sums, d_gain, *refs = refs
-    d_out, chained = refs
+    d_out, chained, *refs = refs
     seqs, length, _ = proj.shape
     dim = gain.shape[1]
     blocks = length // STRETCH
-    together = 2 if blocks % 2 == 0 else 1
+    span = length // HEADS
+    together = span // STRETCH
+    if groups:
+        d_tokens = d_mixer
+        d_mixer, x_send, x_recv, own = refs
+        spot = Spot(groups)
+        spot.barrier(copies=False)
+
+        def block_of(mate):
+            return d_mixer.at[:, pl.ds(pl.multiple_of(mate * span, span), span)]
+
+        def columns_of(mate):
+            return d_tokens.at[:, :, pl.ds(pl.multiple_of(mate * dim, dim), dim)]
+
+        def from_mate(mate, slot):
+            return remote(
+                columns_of(mate), block_of(mate), x_send.at[slot], x_recv.at[slot],
+                spot.to_mate(mate),
+            )
+
+        def from_self():
+            return pltpu.make_async_copy(columns_of(spot.mate), block_of(spot.mate), own.at[0])
+
+        exchange = team_exchange(
+            spot, columns_of, block_of, x_send, x_recv, own.at[0]
+        )
+        next(exchange)
     all_conv = pl.ds(0, 5 * dim)
 
     def spots(step):
@@ -365,6 +1030,18 @@
     def first(step, gain_sum):
         units = spots(step)
         kept = []
+        if groups:
+            origin = HEADS - 1 - step
+            slot = lax.rem(spot.mate - origin + HEADS, HEADS)
+
+            @pl.when(slot == 0)
+            def _():
+                from_self().wait()
+
+            @pl.when(slot != 0)
+            def _():
+                from_mate(origin, slot).wait_recv()
+
         for seq, block in units:
             at = seq * blocks + block
             base = pl.multiple_of(block * STRETCH, STRETCH)
@@ -572,9 +1249,12 @@
             d_first[seq] = rims[seq]
     d_conv[...] = conv_sum
     d_small_sums[...] = small_sum
-
-
-def mixer_backward(proj, conv, decay, gain, kept, d_mixer, link=()):
+    if groups:
+        for k in range(1, HEADS):
+            from_mate(spot.mate_off(k), k).wait_send()
+
+
+def mixer_backward(proj, conv, decay, gain, kept, d_mixer, groups=0, link=()):
     seqs, length, width = proj.shape
     dim = gain.shape[1]
     units = seqs * (length // STRETCH)
@@ -590,15 +1270,24 @@
             jax.ShapeDtypeStruct((seqs, 8, 5 * dim), jnp.float32),
         )
     return pl.pallas_call(
-        functools.partial(backward_kernel, bool(link)),
+        functools.partial(backward_kernel, bool(link), groups),
         out_shape=shapes,
-        in_specs=[pl.BlockSpec(memory_space=pltpu.VMEM)] * (11 + len(link)),
-        out_specs=[pl.BlockSpec(memory_space=pltpu.VMEM)] * len(shapes),
+        in_specs=[IN_VMEM] * (11 + len(link)),
+        out_specs=[IN_VMEM] * len(shapes),
         scratch_shapes=[
             pltpu.VMEM((units, STRETCH, dim), jnp.float32),
             pltpu.VMEM((units, dim, dim), jnp.float32),
-        ],
-        compiler_params=pltpu.CompilerParams(vmem_limit_bytes=60 * 2**20),
+        ]
+        + (
+            [pltpu.VMEM((seqs, length, dim), jnp.bfloat16), dma(HEADS), dma(HEADS), dma(1)]
+            if groups
+            else []
+        ),
+        compiler_params=pltpu.CompilerParams(
+            vmem_limit_bytes=60 * 2**20,
+            collective_id=5 if groups else None,
+            has_side_effects=bool(groups),
+        ),
         cost_estimate=pl.CostEstimate(
             flops=units * 60 * WIDE * WIDE * WIDE,
             bytes_accessed=units * WIDE * WIDE * 30,
@@ -676,12 +1365,31 @@
     rates_of = STEPS + 1
     f32, bf16 = jnp.float32, jnp.bfloat16
 
+    def over_teams(array):
+        if teams == 1:
+            return array
+        return lax.all_gather(array, "ctx", axis=0, tiled=True, axis_index_groups=peers)
+
+    places = place * tokens + lax.broadcasted_iota(jnp.int32, (seqs, tokens), 1)
+    valid = (places < lengths.reshape(seqs, 1)).astype(f32).reshape(rows, 1)
+    grad_out = (out_cotangent.reshape(rows, width).astype(f32) * valid).astype(bf16)
+
     own = width // count
     small_block = jnp.concatenate(
         [norm_gains.reshape(-1), w_small.reshape(-1), conv_weight.reshape(-1)]
     )
     small_block = jnp.pad(small_block, (0, -small_block.size % 128)).reshape(-1, 128)
-    smalls = lax.all_gather(small_block, "ctx", axis=0).reshape(count, -1)
+    piece = own // groups
+    pieces = w_in.reshape(groups, piece, kinds, HEADS, dim).transpose(3, 0, 1, 2, 4)
+    sequence, w_head, smalls, grad_all = prologue(
+        block_in.reshape(seqs, tokens, width),
+        pieces.reshape(HEADS, groups, piece, kinds * dim),
+        small_block,
+        grad_out,
+        groups,
+    )
+    grad_all = grad_all.reshape(groups * rows, width)
+    smalls = over_teams(smalls).reshape(count, -1)
     gains = smalls[:, : 2 * own].reshape(count, 2, own).transpose(1, 0, 2).reshape(2, width)
     gains = gains.astype(f32)
     small_all = smalls[:, 2 * own : (2 + HEADS * rates_of) * own].reshape(width, rates_of, HEADS)
@@ -691,28 +1399,26 @@
     conv_all = conv_all.transpose(1, 0, 2).reshape(CONV, kinds - 1, HEADS, dim)
     conv_head = lax.dynamic_index_in_dim(conv_all, head, 2, keepdims=False)
     conv_head = conv_head.reshape(CONV, -1).astype(f32)
-    sequence = lax.all_gather(
-        block_in.reshape(seqs, tokens, width), "ctx", axis=1, tiled=True, axis_index_groups=mates
-    )
-    w_head = w_in.reshape(own, kinds, HEADS, dim).transpose(2, 0, 1, 3)
-    w_head = lax.all_to_all(w_head, "ctx", 0, 0, tiled=True, axis_index_groups=mates)
-    w_head = w_head.reshape(HEADS * own, kinds * dim)
-    if teams > 1:
-        w_head = lax.all_gather(w_head, "ctx", axis=0, tiled=True, axis_index_groups=peers)
     w_head = jnp.concatenate(
-        [w_head, small_head, jnp.zeros((width, dim - rates_of), bf16)], axis=1
-    )
-    w_out_full = lax.all_gather(w_out, "ctx", axis=0, tiled=True)
+        [
+            over_teams(w_head).reshape(width, kinds * dim),
+            small_head,
+            jnp.zeros((width, dim - rates_of), bf16),
+        ],
+        axis=1,
+    )
     hidden_own = w_down.shape[0] // groups
+    hidden_units = count * hidden_own
+    out_piece = lax.dynamic_index_in_dim(
+        w_out.reshape(groups, piece, width), group, 0, keepdims=False
+    )
     gate_up_part = lax.dynamic_index_in_dim(
         gate_up_weight.reshape(own, 2, count, groups, hidden_own), group, 3, keepdims=False
-    )
-    gate_up_part = lax.all_gather(gate_up_part.reshape(own, -1), "ctx", axis=0, tiled=True)
+    ).reshape(own, -1)
     down_part = lax.dynamic_index_in_dim(
         w_down.reshape(groups, hidden_own, width), group, 0, keepdims=False
     )
-    down_part = lax.all_gather(down_part, "ctx", axis=0, tiled=True)
-    hidden_units = count * hidden_own
+    parts = (out_piece, gate_up_part, down_part)
 
     inputs_all = sequence.astype(f32)
     h_first = (inputs_all * norm_scale(inputs_all) * gains[0]).astype(bf16)
@@ -729,38 +1435,29 @@
         onward = [(c, c + HEADS) for c in range(count - HEADS)]
         halo = lax.ppermute(proj[:, length - 8 :], "ctx", onward)
         start = jnp.zeros((seqs, dim, dim), f32)
-        *_, offset, transfer = mixer_forward(proj, conv_head, decay, gain, (halo, start))
+        *_, offset, transfer = mixer_forward(
+            proj, conv_head, decay, gain, link=(halo, start)
+        )
         spans = lax.all_gather((transfer, offset), "ctx", axis_index_groups=peers)
         for turn in range(teams - 1):
             start = jnp.where(turn < team, batched(spans[0][turn], start) + spans[1][turn], start)
-        mixer_head, *kept = mixer_forward(proj, conv_head, decay, gain, (halo, start))[:-2]
+        link = (halo, start)
     else:
-        mixer_head, *kept = mixer_forward(proj, conv_head, decay, gain)
-
-    def to_tokens(array):
-        split = array.reshape(seqs, HEADS, tokens, dim).transpose(1, 0, 2, 3)
-        moved = lax.all_to_all(
-            split.reshape(HEADS, rows, dim), "ctx", 0, 0, tiled=True, axis_index_groups=mates
-        )
-        return moved.transpose(1, 0, 2).reshape(rows, width)
-
-    def to_heads(array):
-        split = array.reshape(rows, HEADS, dim).transpose(1, 0, 2)
-        moved = lax.all_to_all(split, "ctx", 0, 0, tiled=True, axis_index_groups=mates)
-        return moved.reshape(HEADS, seqs, tokens, dim).transpose(1, 0, 2, 3).reshape(
-            seqs, length, dim
-        )
-
-    mixer = to_tokens(mixer_head)
+        link = ()
+    *kept, mixer, w_out_full, gate_up_part, down_part = mixer_forward(
+        proj, conv_head, decay, gain, parts, groups, link
+    )
+    kept = kept[:6]
+    mixer = mixer.reshape(rows, width)
+    w_out_full = over_teams(w_out_full).reshape(width, width)
+    gate_up_part = over_teams(gate_up_part).reshape(width, 2 * hidden_units)
+    down_part = over_teams(down_part).reshape(hidden_units, width)
+
     inputs = block_in.reshape(rows, width).astype(f32)
     resid = inputs + matmul(mixer, w_out_full)
 
     h_second = (resid * norm_scale(resid) * gains[1]).astype(bf16)
-    places = place * tokens + lax.broadcasted_iota(jnp.int32, (seqs, tokens), 1)
-    valid = (places < lengths.reshape(seqs, 1)).astype(f32).reshape(rows, 1)
-    grad_out = (out_cotangent.reshape(rows, width).astype(f32) * valid).astype(bf16)
-    grad_all = lax.all_gather(grad_out, "rep", axis=0, tiled=True)
-    h_all = lax.all_gather(h_second, "rep", axis=0, tiled=True)
+    h_all = gather_copies(h_second, groups, 3).reshape(groups * rows, width)
     gate_up = matmul(h_all, gate_up_part)
     gate, up = gate_up[:, :hidden_units], gate_up[:, hidden_units:]
     open_gate = jax.nn.sigmoid(gate)
@@ -775,12 +1472,9 @@
     d_gate_up = jnp.concatenate(
         [d_hidden * up * (open_gate * (1.0 + gate * (1.0 - open_gate))), d_hidden * silu], axis=1
     ).astype(bf16)
-    d_second = lax.psum_scatter(
-        times_transposed(d_gate_up, gate_up_part).astype(bf16),
-        "rep",
-        scatter_dimension=0,
-        tiled=True,
-    ).astype(f32)
+    d_second = reduce_copies(
+        times_transposed(d_gate_up, gate_up_part).astype(bf16).reshape(groups, rows, width), 4
+    )
     grad_down = transposed_times(hidden, grad_all)
     grad_gate_up = transposed_times(h_all, d_gate_up)
     d_norm, gain_terms_second = norm_back(resid, gains[1], d_second)
@@ -789,10 +1483,18 @@
     grad_out_proj = transposed_times(mixer, d_branch)
     d_mixer = times_transposed(d_branch, w_out_full)
 
-    d_mixer = to_heads(d_mixer.astype(bf16))
+    d_mixer = d_mixer.astype(bf16)
     if teams > 1:
+        def to_heads(array):
+            split = array.reshape(rows, HEADS, dim).transpose(1, 0, 2)
+            moved = lax.all_to_all(split, "ctx", 0, 0, tiled=True, axis_index_groups=mates)
+            return moved.reshape(HEADS, seqs, tokens, dim).transpose(1, 0, 2, 3).reshape(
+                seqs, length, dim
+            )
+
+        d_mixer = to_heads(d_mixer)
         later = jnp.zeros((seqs, dim, dim), f32)
-        local = mixer_backward(proj, conv_head, decay, gain, kept, d_mixer, (halo, later))[4]
+        local = mixer_backward(proj, conv_head, decay, gain, kept, d_mixer, link=(halo, later))[4]
         locals_ = lax.all_gather(local, "ctx", axis_index_groups=peers)
         for turn in range(teams - 1, 0, -1):
             later = jnp.where(
@@ -801,7 +1503,7 @@
                 later,
             )
         d_proj, grad_conv, small_sums, grad_gain, _, rim = mixer_backward(
-            proj, conv_head, decay, gain, kept, d_mixer, (halo, later)
+            proj, conv_head, decay, gain, kept, d_mixer, link=(halo, later)
         )
         rim = lax.ppermute(rim, "ctx", [(c, c - HEADS) for c in range(HEADS, count)])
         spill = jnp.zeros((seqs, CONV - 1, kinds * dim - dim), f32)
@@ -815,21 +1517,41 @@
         )
     else:
         d_proj, grad_conv, small_sums, grad_gain = mixer_backward(
-            proj, conv_head, decay, gain, kept, d_mixer
+            proj, conv_head, decay, gain, kept, d_mixer.reshape(seqs, tokens, width), groups
         )
     d_proj = d_proj.reshape(seqs * length, -1)
-    grad_head = transposed_times(h_first.reshape(seqs * length, width), d_proj)
-    d_first = times_transposed(d_proj, w_head).astype(bf16)
-    d_first = d_first.reshape(seqs, HEADS, tokens, width).transpose(1, 0, 2, 3)
-    d_first = lax.psum_scatter(
-        d_first.reshape(HEADS * rows, width),
-        "ctx",
-        scatter_dimension=0,
-        tiled=True,
-        axis_index_groups=mates,
-    ).astype(f32)
-    d_inputs, gain_terms_first = norm_back(inputs, gains[0], d_first)
+    h_flat = h_first.reshape(seqs * length, width)
+    grad_head = transposed_times(h_flat, d_proj[:, : kinds * dim]).astype(bf16)
+    grad_small = transposed_times(d_proj[:, kinds * dim : kinds * dim + 8], h_flat)
+    d_first = times_transposed(d_proj, w_head)
+    normal_all = (inputs_all * norm_scale(inputs_all)).reshape(seqs * length, width)
+    grad_gains = jnp.stack(
+        [(d_first * normal_all).sum(axis=0), gain_terms_second.sum(axis=0)]
+    )
+    packed = jnp.concatenate(
+        [
+            grad_gains.reshape(-1, dim),
+            grad_small[:rates_of].reshape(-1, dim),
+            grad_conv.reshape(-1, dim),
+            grad_gain,
+            small_sums[:, STEPS : STEPS + 1] + jnp.zeros((1, dim), f32),
+        ]
+    )
+    packed = jnp.pad(packed, ((0, -packed.shape[0] % 8), (0, 0)))
+    if teams > 1:
+        grad_head = lax.psum_scatter(
+            grad_head, "ctx", scatter_dimension=0, tiled=True, axis_index_groups=peers
+        )
+        packed = lax.psum(packed, "ctx", axis_index_groups=peers)
+    d_first, grad_in, packed = epilogue(
+        d_first.astype(bf16).reshape(seqs, length, width),
+        grad_head.reshape(HEADS, groups, piece, kinds * dim),
+        packed,
+    )
+    d_inputs, _ = norm_back(inputs, gains[0], d_first.reshape(rows, width))
     in_grad = (d_resid + d_inputs).astype(bf16)
+    grad_in = grad_in.reshape(groups, HEADS, piece, kinds, dim).transpose(0, 2, 3, 1, 4)
+    grad_in = grad_in.reshape(own, -1)
 
     grad_gate_up = lax.psum_scatter(
         grad_gate_up.astype(bf16), "ctx", scatter_dimension=0, tiled=True
@@ -842,50 +1564,27 @@
     grad_out_proj = lax.psum_scatter(
         grad_out_proj.astype(bf16), "ctx", scatter_dimension=0, tiled=True
     )
-    grad_in = grad_head[:, : kinds * dim].astype(bf16)
-    if teams > 1:
-        grad_in = lax.psum_scatter(
-            grad_in, "ctx", scatter_dimension=0, tiled=True, axis_index_groups=peers
-        )
-    grad_in = lax.all_to_all(
-        grad_in.reshape(HEADS, own, kinds * dim), "ctx", 0, 0, tiled=True, axis_index_groups=mates
-    )
-    grad_in = grad_in.reshape(HEADS, own, kinds, dim).transpose(1, 2, 0, 3).reshape(own, -1)
-    grad_in, grad_out_proj = lax.psum((grad_in, grad_out_proj), "rep")
-
-    gain_terms = jnp.stack([gain_terms_first.sum(axis=0), gain_terms_second.sum(axis=0)])
-    here = jnp.arange(HEADS, dtype=jnp.int32) == head
-    grad_small = grad_head[:, kinds * dim : kinds * dim + rates_of]
-    packed = jnp.concatenate(
-        [
-            gain_terms.reshape(-1),
-            jnp.where(here[None, None, :], grad_small[:, :, None], 0.0).reshape(-1),
-            jnp.where(
-                here[None, None, :, None], grad_conv.reshape(CONV, kinds - 1, 1, dim), 0.0
-            ).reshape(-1),
-            grad_gain.reshape(-1),
-            jnp.pad(
-                jnp.where(here[None, :], small_sums[:, STEPS : STEPS + 1], 0.0).reshape(-1),
-                (0, dim - 2 * HEADS),
-            ),
-        ]
-    ).reshape(-1, 128)
-    packed = lax.psum(packed, ("rep", "ctx")).reshape(-1)
+    grad_out_proj = lax.psum(grad_out_proj, "rep")
 
     def take(size):
         nonlocal packed
-        part, packed = packed[:size], packed[size:]
+        part, packed = packed[:, :size], packed[:, size:]
         return part
+
+    grad_gains = take(2 * HEADS).sum(axis=0).reshape(2, width)
+    grad_small = take(rates_of * HEADS).reshape(HEADS, rates_of, width)
+    grad_small = grad_small.transpose(2, 1, 0).reshape(width, rates_of * HEADS)
+    grad_conv = take(CONV * (kinds - 1)).reshape(HEADS, CONV, kinds - 1, dim)
+    grad_conv = grad_conv.transpose(1, 2, 0, 3).reshape(CONV, (kinds - 1) * width)
+    grad_gain = take(1).sum(axis=0).reshape(dim)
+    decays_sum = take(2)[:, :, 0].transpose(1, 0)
 
     def mine(array, axis, size):
         return lax.dynamic_slice_in_dim(array, place * size, size, axis)
 
-    grad_gains = mine(take(2 * width).reshape(2, width), 1, own)
-    grad_small = mine(take(width * rates_of * HEADS).reshape(width, -1), 0, own)
-    taps = (kinds - 1) * width
-    grad_conv = mine(take(CONV * taps).reshape(CONV, taps), 1, taps // count)
-    grad_gain = take(dim)
-    decays_sum = take(2 * HEADS).reshape(2, HEADS)
+    grad_gains = mine(grad_gains, 1, own)
+    grad_small = mine(grad_small, 0, own)
+    grad_conv = mine(grad_conv, 1, conv_weight.shape[1])
     return (
         result.reshape(block_in.shape),
         in_grad.reshape(block_in.shape),

time: 953 us -> 649 us (0.68)
  waiting for transfers between devices: 532 us -> 154 us
  Pallas kernels: 107 us -> 327 us
  blocking collectives: 134 us -> 8.44 us
  starting transfers between devices: 14.8 us -> 0.25 us
  local copies, waits for them, and re-layouts: 53 us -> 41.9 us
    pallas_call x2 -> x6, Pallas kernels: 107 us -> 327 us  [the longest x1 89.9 us: epilogue(): pl.pallas_call(functools.partial(epilogue_kernel, groups), out_shape=(jax...]
    psum x2 -> x1, waiting for transfers between devices: 169 us -> 25.2 us  [per_device(): grad_out_proj = lax.psum(grad_out_proj, 'rep')]
    all_gather x6 -> x0, waiting for transfers between devices: 117 us -> none  [the longest x1 37.4 us: per_device(): down_part = lax.all_gather(down_part, 'ctx', axis=0, tiled=True)]
    reduce_scatter x2 -> x0, waiting for transfers between devices: 106 us -> none  [the longest x1 87.9 us: per_device(): lax.psum_scatter(d_first.reshape(HEADS * rows, width), 'ctx', scatter_dim...]
    all_gather x1 -> x0, blocking collectives: 69.8 us -> none  [per_device(): smalls = lax.all_gather(small_block, 'ctx', axis=0).reshape(count, -1)]
    reduce_scatter x1, waiting for transfers between devices: 0.01 us -> 64.9 us  [per_device(): lax.psum_scatter(grad_gate_up.astype(bf16), 'ctx', scatter_dimension=0, t...]
    all_to_all x2 -> x0, blocking collectives: 56.1 us -> none  [the longest x1 30.6 us: to_heads(): lax.all_to_all(split, 'ctx', 0, 0, tiled=True, axis_index_groups=mates)]
    all_to_all x2 -> x0, waiting for transfers between devices: 31.4 us -> none  [the longest x1 31.4 us: per_device(): lax.all_to_all(grad_in.reshape(HEADS, own, kinds * dim), 'ctx', 0, 0, til...]
  transfers between devices with their start and end apart: 17 -> 6, of which waited for: 14 -> 4; matrix products, arithmetic and copies ran while one was open for 12% -> 12% of each run, Pallas kernels for 11% -> 28%
where the time goes in v2:
time: 649 us; the launch traced here: 638 us
  Pallas kernels  327 us (50%)
  waiting for transfers between devices  154 us (24%)
  matrix products  66.3 us (10%)
  local copies, waits for them, and re-layouts  41.9 us (6%)
  other arithmetic  24.8 us (4%)
  between operations  15.1 us (2%)
  blocking collectives  8.44 us (1%)
    pallas_call x1, Pallas kernels, epilogue(): pl.pallas_call(functools.partial(epilogue_kernel, groups), out_shape=(jax...  89.9 us
    pallas_call x1, Pallas kernels, mixer_forward(): pl.pallas_call(functools.partial(forward_kernel, bool(link), groups), out...  77.5 us
    pallas_call x1, Pallas kernels, mixer_backward(): pl.pallas_call(functools.partial(backward_kernel, bool(link), groups), ou...  69.8 us
    reduce_scatter x1, waiting for transfers between devices, per_device(): lax.psum_scatter(grad_gate_up.astype(bf16), 'ctx', scatter_dimension=0, t...  64.9 us
    pallas_call x1, Pallas kernels, prologue(): pl.pallas_call(functools.partial(prologue_kernel, groups), out_shape=(jax...  56 us
    reduce_scatter x1, waiting for transfers between devices, per_device(): lax.psum_scatter(grad_down.astype(bf16), 'ctx', scatter_dimension=0, tile...  39.6 us
    psum x1, waiting for transfers between devices, per_device(): grad_out_proj = lax.psum(grad_out_proj, 'rep')  25.2 us
    reduce_scatter x1, waiting for transfers between devices, per_device(): lax.psum_scatter(matmul(hidden, down_part).astype(bf16), 'rep', scatter_d...  24.2 us
  transfers between devices with their start and end apart: 6, of which 4 were waited for; matrix products, arithmetic and copies ran while one was open for 12% of the time, Pallas kernels for 28%

profile of v2, /device:TPU:8, one launch (start us, length us, event | category | flops | bytes accessed | tf_op | source)
XLA Modules:
  0.0 638.4 jit_solution(17578307613450942483)
XLA Ops:
  14.3 56.0 %prologue.1 = (bf16[2,1024,1024]{2,1,0:T(8,128)(2,1)}, bf16[8,4,32,768]{3,2,1,0:T(8,128)(2,1)}, bf16[8,46,128]{2,1,0:T(8,128)(2,1)}, bf16[4,256,1024]{2,1,0:T(8,128)(2,1)}) custom-call(bf16[2,128,1024]{2,1,0:T(8,128)(2,1)} %bitcast.152, bf16[8,4,32,768]{3,2,1,0:T(8,128)(2,1)} %reshape.272.pieces, bf16[46,128]{1,0:T(8,128)(2,1)} %maximum_bitcast_fusion.smalls, ...), custom_call_target="tpu_custom_call" | custom-call | tf_op jit(solution)/shard_map/prologue/pallas_call | solution.py:282
  85.0 5.5 convert_multiply_fusion
  90.6 6.5 %fusion.5.refs_0_ = f32[2,1024,896]{2,1,0:T(8,128)} fusion(bf16[2,1024,1024]{2,1,0:T(8,128)(2,1)S(1)} %get-tuple-element.110, bf16[1024,3]{1,0:T(8,128)(2,1)S(1)} %copy.70, bf16[1024,768]{1,0:T(8,128)(2,1)S(1)} %bitcast.197, bf16[896]{0:T(1024)(128)(2,1)S(1)} %pad.12.clone), kind=kOutput, calls=%fused_computation.20 | convolution fusion | flops 3763601408 | bytes 13115136 | tf_op jit(solution)/shard_map/dot_general | solution.py:1301
  97.7 77.5 %mixer_forward.1 = (f32[2,1024,128]{2,1,0:T(8,128)}, f32[32,128,128]{2,1,0:T(8,128)}, f32[32,128,128]{2,1,0:T(8,128)}, f32[32,128,128]{2,1,0:T(8,128)}, f32[32,1...) custom-call(f32[2,1024,896]{2,1,0:T(8,128)} %fusion.5.refs_0_, ...), custom_call_target="tpu_custom_call" | custom-call | flops 4026531840 | bytes 15728640 | tf_op jit(solution)/shard_map/mixer_forward/pallas_call | solution.py:966
  175.3 3.5 multiply_reduce_fusion.4
  180.9 17.1 %gather_copies.1 = bf16[4,256,1024]{2,1,0:T(8,128)(2,1)} custom-call(bf16[256,1024]{1,0:T(8,128)(2,1)} %multiply_convert_fusion.5.block), custom_call_target="tpu_custom_call" | custom-call | tf_op jit(solution)/shard_map/gather_copies/pallas_call | solution.py:309
  198.0 6.0 fusion.29
  204.1 4.0 multiply_convert_fusion.2
  209.7 5.1 convolution_convert_fusion
  214.9 4.2 convolution_convert_fusion.4
  219.2 4.9 convolution_convert_fusion.3
  224.2 64.9 %reduce-scatter.9.cloned.1.call-done = bf16[128,1408]{1,0:T(8,128)(2,1)} async-done(((bf16[1024,1408]{1,0:T(8,128)(2,1)}), bf16[128,1408]{1,0:T(8,128)(2,1)}) %reduce-scatter.9.cloned.1.call-update) | async-done | bytes 360464 | tf_op jit(solution)/shard_map/reduce_scatter | solution.py:1556
  291.1 6.2 convolution_convert_fusion.2
  297.3 17.2 %reduce_copies.1 = f32[256,1024]{1,0:T(8,128)S(1)} custom-call(bf16[4,256,1024]{2,1,0:T(8,128)(2,1)S(1)} %bitcast.148), custom_call_target="tpu_custom_call" | custom-call | tf_op jit(solution)/shard_map/reduce_copies/pallas_call | solution.py:368
  317.4 39.6 %reduce-scatter.11.cloned.1.call-done = bf16[88,1024]{1,0:T(8,128)(2,1)} async-done(((bf16[704,1024]{1,0:T(8,128)(2,1)}), bf16[88,1024]{1,0:T(8,128)(2,1)}) %reduce-scatter.11.cloned.1.call-update) | async-done | bytes 180240 | tf_op jit(solution)/shard_map/reduce_scatter | solution.py:1562
  357.1 8.4 %all_gather.7 = bf16[352,1024]{1,0:T(8,128)(2,1)S(1)} all-gather(bf16[88,1024]{1,0:T(8,128)(2,1)} %reduce-scatter.11.cloned.1.call-done), channel_id=1, replica_groups=mesh['rep'=4,'ctx'=8] {'rep'}, dimensions={0}, use_global_device_ids=true | all-gather | bytes 901120 | tf_op jit(solution)/shard_map/all_gather | solution.py:1563
  366.8 24.2 %reduce-scatter.5.cloned.1.call-done = bf16[256,1024]{1,0:T(8,128)(2,1)} async-done(((bf16[1024,1024]{1,0:T(8,128)(2,1)}), bf16[256,1024]{1,0:T(8,128)(2,1)}) %reduce-scatter.5.cloned.1.call-update) | async-done | bytes 524304 | tf_op jit(solution)/shard_map/reduce_scatter | solution.py:1466
  398.9 69.8 %mixer_backward.1 = (bf16[2,1024,896]{2,1,0:T(8,128)(2,1)}, f32[4,640]{1,0:T(4,128)}, f32[2,128]{1,0:T(2,128)}, f32[1,128]{1,0:T(1,128)}) custom-call(f32[2,1024,896]{2,1,0:T(8,128)} %fusion.5.refs_0_, f32[4,640]{1,0:T(4,128)} %bitcast.185, f32[2,128]{1,0:T(2,128)} %stack.15.refs_2_, f32[1,128]{1,0:T(1,128)} %bitcast.192, ...), custom_call_target="tpu_custom_call" | custom-call | flops 4026531840 | bytes 15728640 | tf_op jit(solution)/shard_map/mixer_backward/pallas_call | solution.py:1272
  472.1 9.5 %fusion.1 = (f32[1024]{0:T(1024)S(1)}, bf16[2048,1024]{1,0:T(8,128)(2,1)}) fusion(f32[2,1024,1024]{2,1,0:T(8,128)} %get-tuple-element.109, bf16[2048,896]{1,0:T(8,128)(2,1)} %bitcast.181, bf16[1024,3]{1,0:T(8,128)(2,1)S(1)} %copy.70, bf16[1024,768]{1,0:T(8,128)(2,1)S(1)} %bitcast.198, bf16[896]{0:T(1024)(128)(2,1)S(1)} %pad.12.clone), kind=kOutput, calls=%fused_computation.4 | convolution fusion | flops 3769891840 | bytes 17837824 | tf_op jit(solution)/shard_map/dot_general | solution.py:1305
  482.0 7.9 %fusion.7 = bf16[1024,768]{1,0:T(8,128)(2,1)} fusion(bf16[2048,1024]{1,0:T(8,128)(2,1)} %bitcast.151, bf16[2048,896]{1,0:T(8,128)(2,1)} %bitcast.182), kind=kOutput, calls=%fused_computation.22 | convolution fusion | flops 3222011904 | bytes 8912896 | tf_op jit(solution)/shard_map/dot_general | solution.py:1311
  489.8 89.9 %epilogue.1 = (f32[2,128,1024]{2,1,0:T(8,128)S(1)}, bf16[4,8,32,768]{3,2,1,0:T(8,128)(2,1)S(1)}, f32[8,64,128]{2,1,0:T(8,128)S(1)}) custom-call(bf16[2,1024,1024]{2,1,0:T(8,128)(2,1)} %bitcast.158, bf16[8,4,32,768]{3,2,1,0:T(8,128)(2,1)} %bitcast.166, f32[64,128]{1,0:T(8,128)S(1)} %pad.5.smalls), custom_call_target="tpu_custom_call" | custom-call | tf_op jit(solution)/shard_map/epilogue/pallas_call | solution.py:543
  582.7 5.7 copy.75
  588.4 4.4 reshape.315
  604.1 25.2 %all-reduce.4.cloned.1.call-done = bf16[128,1024]{1,0:T(8,128)(2,1)} async-done(((bf16[128,1024]{1,0:T(8,128)(2,1)}), bf16[128,1024]{1,0:T(8,128)(2,1)}) %all-reduce.4.cloned.1.call-update) | async-done | bytes 262160 | tf_op jit(solution)/shard_map/psum | solution.py:1567
  (144 shorter events, 60.1 us)
Async XLA Ops:
  7.2 74.4 %copy-start = (bf16[352,1024]{1,0:T(8,128)(2,1)S(1)}, bf16[352,1024]{1,0:T(8,128)(2,1)}, u32[]{:S(2)}) copy-start(bf16[352,1024]{1,0:T(8,128)(2,1)} %param.24) | copy-start | bytes 2162692
  7.2 281.9 %reduce-scatter.9.cloned.1.call-start = ((), (), s32[]{:S(2)}) async-start(), calls=%async_computation.7 | async-start | bytes 3244032 | tf_op jit(solution)/shard_map/reduce_scatter | solution.py:1556
  12.4 58.9 %copy-start.21 = (f32[8]{0:T(128)S(1)}, f32[8]{0:T(128)}, u32[]{:S(2)}) copy-start(f32[8]{0:T(128)} %param.20) | copy-start | bytes 100
  12.4 59.5 %copy-start.22 = (f32[8]{0:T(128)S(1)}, f32[8]{0:T(128)}, u32[]{:S(2)}) copy-start(f32[8]{0:T(128)} %param.19) | copy-start | bytes 100
  85.0 5.6 copy-start.18
  90.5 6.6 %copy-start.4 = (bf16[2,1024,1024]{2,1,0:T(8,128)(2,1)}, bf16[2,1024,1024]{2,1,0:T(8,128)(2,1)S(1)}, u32[]{:S(2)}) copy-start(bf16[2,1024,1024]{2,1,0:T(8,128)(2,1)S(1)} %get-tuple-element.110) | copy-start | bytes 12582916
  97.7 77.5 %copy-start.5 = (bf16[2,1,128,1024]{3,2,1,0:T(8,128)(2,1)S(1)}, bf16[2,1,128,1024]{3,2,1,0:T(8,128)(2,1)}, u32[]{:S(2)}) copy-start(bf16[2,1,128,1024]{3,2,1,0:T(8,128)(2,1)} %param.13) | copy-start | bytes 1572868
  198.0 6.0 copy-start.17
  198.0 6.0 copy-start.23
  204.0 5.6 copy-start.8
  214.9 142.2 %reduce-scatter.11.cloned.1.call-start = ((), (), s32[]{:S(2)}) async-start(), calls=%async_computation.9 | async-start | bytes 1622016 | tf_op jit(solution)/shard_map/reduce_scatter | solution.py:1562
  219.1 171.8 %reduce-scatter.5.cloned.1.call-start = ((), (), s32[]{:S(2)}) async-start(), calls=%async_computation.4 | async-start | bytes 2621440 | tf_op jit(solution)/shard_map/reduce_scatter | solution.py:1466
  224.2 373.1 %all-gather.2.cloned.1.call-start = ((), (), s32[]{:S(2)}) async-start(), calls=%async_computation.8 | async-start | bytes 1802240 | tf_op jit(solution)/shard_map/all_gather | solution.py:1559
  291.0 307.8 %reduce-scatter.7.cloned.1.call-start = ((), (), s32[]{:S(2)}) async-start(), calls=%async_computation.5 | async-start | bytes 2359296 | tf_op jit(solution)/shard_map/reduce_scatter | solution.py:1564
  314.5 76.5 %copy-start.10 = (bf16[2,1,128,1024]{3,2,1,0:T(8,128)(2,1)S(1)}, bf16[2,1,128,1024]{3,2,1,0:T(8,128)(2,1)}, u32[]{:S(2)}) copy-start(bf16[2,1,128,1024]{3,2,1,0:T(8,128)(2,1)} %param.25) | copy-start | bytes 1572868
  366.8 26.8 %copy-start.7 = (bf16[2,128,1024]{2,1,0:T(8,128)(2,1)S(1)}, bf16[2,128,1024]{2,1,0:T(8,128)(2,1)}, u32[]{:S(2)}) copy-start(bf16[2,128,1024]{2,1,0:T(8,128)(2,1)} %get-tuple-element.36) | copy-start | bytes 1572868
  393.6 5.2 copy-start.2
  398.8 230.5 %all-reduce.4.cloned.1.call-start = ((), (), s32[]{:S(2)}) async-start(), calls=%async_computation.6 | async-start | bytes 524288 | tf_op jit(solution)/shard_map/psum | solution.py:1567
  472.1 9.6 %copy-start.11 = (f32[4,640]{1,0:T(4,128)S(1)}, f32[4,640]{1,0:T(4,128)}, u32[]{:S(2)}) copy-start(f32[4,640]{1,0:T(4,128)} %get-tuple-element.48) | copy-start | bytes 30724
  472.1 9.6 %copy-start.20 = (f32[2,128]{1,0:T(2,128)S(1)}, f32[2,128]{1,0:T(2,128)}, u32[]{:S(2)}) copy-start(f32[2,128]{1,0:T(2,128)} %get-tuple-element.50) | copy-start | bytes 3076
  472.1 9.9 %copy-start.14 = (f32[1,128]{1,0:T(1,128)S(1)}, f32[1,128]{1,0:T(1,128)}, u32[]{:S(2)}) copy-start(f32[1,128]{1,0:T(1,128)} %get-tuple-element.49) | copy-start | bytes 1540
  588.4 7.0 %copy-start.6 = (bf16[2,1,128,1024]{3,2,1,0:T(8,128)(2,1)S(1)}, bf16[2,1,128,1024]{3,2,1,0:T(8,128)(2,1)}, u32[]{:S(2)}) copy-start(bf16[2,1,128,1024]{3,2,1,0:T(8,128)(2,1)} %param.13) | copy-start | bytes 1572868
  588.4 7.8 %copy-start.3 = (f32[256,1024]{1,0:T(8,128)S(1)}, f32[256,1024]{1,0:T(8,128)}, u32[]{:S(2)}) copy-start(f32[256,1024]{1,0:T(8,128)} %copy-done.2) | copy-start | bytes 3145732
  598.9 32.3 %copy-start.1 = (bf16[352,1024]{1,0:T(8,128)(2,1)S(1)}, bf16[352,1024]{1,0:T(8,128)(2,1)}, u32[]{:S(2)}) copy-start(bf16[352,1024]{1,0:T(8,128)(2,1)} %param.24) | copy-start | bytes 2162692
  (8 other events, 24.3 us)
Sparse Core Ops, SparseCore 0:
  215.0 74.0 reduce-scatter.8
  293.0 63.9 reduce-scatter.10
  360.2 30.7 reduce-scatter.4
  392.5 18.9 all-gather.1
  415.8 67.2 reduce-scatter.6
  599.0 30.3 all-reduce.3

commit v3 on v2

--- a/solution.py
+++ b/solution.py
@@ -317,18 +317,18 @@
     )(block)
 
 
-def rep_reduce(spot, part, pairs, sums, others, send, recv):
+def rep_reduce(spot, part, sums, others, send, recv):
     half, side = spot.groups // 2, spot.side
 
     def to_twin(k):
         return remote(
-            part(2 * k + 1 - side), pairs.at[k], send.at[k], recv.at[k], spot.to_group(spot.twin)
+            part(2 * k + 1 - side), sums.at[k], send.at[k], recv.at[k], spot.to_group(spot.twin)
         )
 
     def onward(k):
         slot = half + k
         return remote(
-            sums.at[k], others.at[k], send.at[slot], recv.at[slot], spot.to_group(spot.group_off(k))
+            sums.at[lax.rem(spot.pair + k, half)], others.at[k], send.at[slot], recv.at[slot], spot.to_group(spot.group_off(k))
         )
 
     for k in range(half):
@@ -338,10 +338,11 @@
         to_twin(k).wait_recv()
 
     def both(pair):
-        return part(2 * pair + side)[...].astype(jnp.float32) + pairs[pair].astype(jnp.float32)
+        return part(2 * pair + side)[...].astype(jnp.float32) + sums[pair].astype(jnp.float32)
 
     for k in range(1, half):
-        sums[k] = both(lax.rem(spot.pair + k, half)).astype(sums.dtype)
+        pair = lax.rem(spot.pair + k, half)
+        sums[pair] = both(pair).astype(sums.dtype)
         onward(k).start()
     yield
     total = both(spot.pair)
@@ -355,10 +356,10 @@
     yield total
 
 
-def reduce_kernel(groups, parts, out, pairs, sums, others, send, recv):
+def reduce_kernel(groups, parts, out, sums, others, send, recv):
     spot = Spot(groups)
     spot.barrier(team=False)
-    *_, total = rep_reduce(spot, lambda g: parts.at[g], pairs, sums, others, send, recv)
+    *_, total = rep_reduce(spot, lambda g: parts.at[g], sums, others, send, recv)
     out[...] = total
 
 
@@ -370,7 +371,7 @@
         out_shape=jax.ShapeDtypeStruct(parts.shape[1:], jnp.float32),
         in_specs=[IN_VMEM],
         out_specs=IN_VMEM,
-        scratch_shapes=[pltpu.VMEM(block, parts.dtype)] * 3 + [dma(groups), dma(groups)],
+        scratch_shapes=[pltpu.VMEM(block, parts.dtype)] * 2 + [dma(groups), dma(groups)],
         compiler_params=pltpu.CompilerParams(
             collective_id=number, has_side_effects=True, vmem_limit_bytes=40 * 2**20
         ),
@@ -378,7 +379,7 @@
     )(parts)
 
 
-def team_reduce(spot, part, seqs, across_in, sums, rising, falling, total, send, recv):
+def team_reduce(spot, part, seqs, sums, passing, total, send, recv):
     mate, col, row = spot.mate, spot.col, spot.row
     up, down = spot.to_mate(mate + ROWS), spot.to_mate(mate - ROWS)
     across = spot.to_mate(mate + 1 - 2 * row)
@@ -388,7 +389,7 @@
     def cross(seq, d):
         return remote(
             part(ROWS * d + 1 - row, seq),
-            across_in.at[seq, d],
+            sums.at[seq, d],
             send.at[0, seq, d],
             recv.at[0, seq, d],
             across,
@@ -396,12 +397,12 @@
 
     def rise(seq, d):
         return remote(
-            sums.at[seq, d], rising.at[seq, d], send.at[1, seq, d], recv.at[1, seq, d], up
+            sums.at[seq, d], passing.at[seq, d + 1], send.at[1, seq, d], recv.at[1, seq, d], up
         )
 
     def fall(seq, d):
         return remote(
-            sums.at[seq, d], falling.at[seq, d], send.at[2, seq, d], recv.at[2, seq, d], down
+            sums.at[seq, d], passing.at[seq, d], send.at[2, seq, d], recv.at[2, seq, d], down
         )
 
     order_out = [d for pair in zip(range(last, -1, -1), range(COLS)) for d in pair][:COLS]
@@ -415,7 +416,7 @@
 
             def both(seq=seq, d=d):
                 own = part(ROWS * d + row, seq)[...].astype(f32)
-                return own + across_in[seq, d].astype(f32)
+                return own + sums[seq, d].astype(f32)
 
             @pl.when(col == d)
             def _():
@@ -430,7 +431,7 @@
                 @pl.when((col < d) & (col > 0))
                 def _():
                     rise(seq, d).wait_recv()
-                    sums[seq, d] = (both() + rising[seq, d].astype(f32)).astype(sums.dtype)
+                    sums[seq, d] = (both() + passing[seq, d + 1].astype(f32)).astype(sums.dtype)
 
                 @pl.when(col < d)
                 def _():
@@ -445,7 +446,7 @@
                 @pl.when((col > d) & (col < last))
                 def _():
                     fall(seq, d).wait_recv()
-                    sums[seq, d] = (both() + falling[seq, d].astype(f32)).astype(sums.dtype)
+                    sums[seq, d] = (both() + passing[seq, d].astype(f32)).astype(sums.dtype)
 
                 @pl.when(col > d)
                 def _():
@@ -459,14 +460,14 @@
                 @pl.when(col == d)
                 def _():
                     rise(seq, d).wait_recv()
-                    total[seq] += rising[seq, d].astype(f32)
+                    total[seq] += passing[seq, d + 1].astype(f32)
 
             if d < last:
 
                 @pl.when(col == d)
                 def _():
                     fall(seq, d).wait_recv()
-                    total[seq] += falling[seq, d].astype(f32)
+                    total[seq] += passing[seq, d].astype(f32)
 
     for d in range(COLS):
         for seq in range(seqs):
@@ -483,11 +484,11 @@
     yield
 
 
-def epilogue_kernel(groups, d_first, grads, smalls, *refs):
-    (d_own, grads_all, smalls_all, across_in, sums, rising, falling,
-     pairs, pair_sums, others, quarter, copies, small_sum,
+def epilogue_kernel(groups, d_first, grads, smalls, gate_up, down, *refs):
+    (d_own, grads_all, smalls_all, gate_up_all, down_all, sums, passing,
+     pair_sums, others, quarter, copies, small_sum,
      t_send, t_recv, r_send, r_recv, e_send, e_recv, g_send, g_recv,
-     s_send, s_recv, x_send, x_recv, own) = refs
+     s_send, s_recv, x_send, x_recv, f_send, f_recv, own) = refs
     spot = Spot(groups)
     seqs, length, _ = d_first.shape
     span = length // HEADS
@@ -495,17 +496,23 @@
     tokens = team_reduce(
         spot,
         lambda m, seq: d_first.at[seq, pl.ds(pl.multiple_of(m * span, span), span)],
-        seqs, across_in, sums, rising, falling, d_own, t_send, t_recv,
+        seqs, sums, passing, d_own, t_send, t_recv,
     )
     weights = rep_reduce(
-        spot, lambda g: grads.at[:, g], pairs, pair_sums, others, r_send, r_recv
+        spot, lambda g: grads.at[:, g], pair_sums, others, r_send, r_recv
     )
     small = rep_gather(spot, smalls, lambda g: copies.at[g], s_send, s_recv, own.at[0])
+    ready = [
+        rep_gather(spot, gate_up, lambda g: gate_up_all.at[g], f_send.at[0], f_recv.at[0], own.at[3]),
+        rep_gather(spot, down, lambda g: down_all.at[g], f_send.at[1], f_recv.at[1], own.at[4]),
+    ]
     next(weights)
     next(small)
     next(tokens)
     next(weights)
     next(small)
+    for step in ready:
+        next(step)
     next(tokens)
     quarter[...] = next(weights).astype(quarter.dtype)
     exchange = team_exchange(
@@ -527,18 +534,19 @@
         spot, grads_all.at[spot.group], lambda g: grads_all.at[g], g_send, g_recv, None
     )
     next(gathered)
+    for step in ready:
+        next(step)
     next(tokens)
     next(gathered)
-    finish(tokens, gathered, spread)
-
-
-def epilogue(d_first, grads, smalls):
+    finish(tokens, gathered, spread, *ready)
+
+
+def epilogue(d_first, grads, smalls, gate_up, down):
     seqs, length, width = d_first.shape
     _, groups, piece, cols = grads.shape
     half = groups // 2
     low_, f32 = d_first.dtype, jnp.float32
     span = length // HEADS
-    block = pltpu.VMEM((seqs, COLS, span, width), low_)
     part = pltpu.VMEM((half, HEADS, piece, cols), low_)
     return pl.pallas_call(
         functools.partial(epilogue_kernel, groups),
@@ -546,23 +554,27 @@
             jax.ShapeDtypeStruct((seqs, span, width), f32),
             jax.ShapeDtypeStruct((groups, HEADS, piece, cols), low_),
             jax.ShapeDtypeStruct((HEADS,) + smalls.shape, f32),
+            jax.ShapeDtypeStruct((groups,) + gate_up.shape, low_),
+            jax.ShapeDtypeStruct((groups,) + down.shape, low_),
         ),
-        in_specs=[IN_VMEM] * 3,
-        out_specs=[IN_VMEM] * 3,
+        in_specs=[IN_VMEM] * 5,
+        out_specs=[IN_VMEM] * 5,
         scratch_shapes=[
-            block, block, block, block, part, part, part,
+            pltpu.VMEM((seqs, COLS, span, width), low_),
+            pltpu.VMEM((seqs, COLS + 1, span, width), low_),
+            part, part,
             pltpu.VMEM((HEADS, piece, cols), low_),
             pltpu.VMEM((groups,) + smalls.shape, f32),
             pltpu.VMEM(smalls.shape, f32),
             dma(3, seqs, COLS), dma(3, seqs, COLS),
             dma(groups), dma(groups), dma(HEADS), dma(HEADS), dma(groups), dma(groups),
-            dma(groups), dma(groups), dma(HEADS), dma(HEADS), dma(3),
+            dma(groups), dma(groups), dma(HEADS), dma(HEADS), dma(2, groups), dma(2, groups), dma(5),
         ],
         compiler_params=pltpu.CompilerParams(
             collective_id=6, has_side_effects=True, vmem_limit_bytes=50 * 2**20
         ),
         name="epilogue",
-    )(d_first, grads, smalls)
+    )(d_first, grads, smalls, gate_up, down)
 
 
 def low(a):
@@ -985,23 +997,34 @@
 
 def backward_kernel(linked, groups, *refs):
     proj, conv, decay, gain, out, fresh, inv, weights, trans, states, d_mixer, *refs = refs
+    halo = None
     if linked:
         halo, end_state, *refs = refs
-        d_proj, d_conv, d_small_sums, d_gain, d_start, d_first, *refs = refs
-    else:
-        halo = None
-        d_proj, d_conv, d_small_sums, d_gain, *refs = refs
+    if groups:
+        parts, refs = refs[:4], refs[4:]
+    d_proj, d_conv, d_small_sums, d_gain, *refs = refs
+    if linked:
+        d_start, d_first, *refs = refs
+    if groups:
+        results, refs = refs[:4], refs[4:]
     d_out, chained, *refs = refs
     seqs, length, _ = proj.shape
     dim = gain.shape[1]
     blocks = length // STRETCH
     span = length // HEADS
     together = span // STRETCH
+    plan = {}
     if groups:
         d_tokens = d_mixer
-        d_mixer, x_send, x_recv, own = refs
+        (d_mixer, x_send, x_recv, own,
+         g_sums, g_passing, g_total, g_send, g_recv,
+         w_sums, w_passing, w_total, w_send, w_recv,
+         o_sums, o_others, o_send, o_recv, o_quarter, o_from, o_own, oe_send, oe_recv,
+         oc_send, oc_recv, p_sums, p_others, p_send, p_recv) = refs
+        gate_up_grad, down_grad, out_grad, down_parts = parts
+        gate_up_own, down_own, out_all, down_sum = results
         spot = Spot(groups)
-        spot.barrier(copies=False)
+        spot.barrier()
 
         def block_of(mate):
             return d_mixer.at[:, pl.ds(pl.multiple_of(mate * span, span), span)]
@@ -1022,6 +1045,66 @@
             spot, columns_of, block_of, x_send, x_recv, own.at[0]
         )
         next(exchange)
+        reduces = [
+            team_reduce(
+                spot, lambda mate, seq: gate_up_grad.at[mate], 1,
+                g_sums, g_passing, g_total, g_send, g_recv,
+            ),
+            team_reduce(
+                spot, lambda mate, seq: down_grad.at[mate], 1,
+                w_sums, w_passing, w_total, w_send, w_recv,
+            ),
+        ]
+        out_reduce = rep_reduce(
+            spot, lambda g: out_grad.at[:, g], o_sums, o_others, o_send, o_recv
+        )
+        out_exchange = team_exchange(
+            spot, lambda mate: o_quarter.at[mate], lambda mate: o_from.at[mate],
+            oe_send, oe_recv, own.at[1],
+        )
+        out_copies = rep_gather(
+            spot, o_own, lambda g: out_all.at[g], oc_send, oc_recv, own.at[2]
+        )
+        down_reduce = rep_reduce(
+            spot, lambda g: down_parts.at[g], p_sums, p_others, p_send, p_recv
+        )
+
+        def each(*steps):
+            for step in steps:
+                next(step)
+
+        def deal_out():
+            o_quarter[...] = next(out_reduce).astype(o_quarter.dtype)
+            next(out_exchange)
+            down_sum[...] = next(down_reduce)
+
+        def own_out():
+            finish(out_exchange)
+            summed = o_from[0].astype(jnp.float32)
+            for mate in range(1, HEADS):
+                summed = summed + o_from[mate].astype(jnp.float32)
+            o_own[...] = summed.astype(o_own.dtype)
+            next(out_copies)
+
+        plan = {
+            (0, 1): lambda: each(*reduces, out_reduce, down_reduce),
+            (0, 4): lambda: each(out_reduce, down_reduce),
+            (1, 0): deal_out,
+            (1, 1): lambda: each(*reduces),
+            (1, 3): lambda: each(*reduces),
+            (1, 4): own_out,
+            (1, 5): lambda: each(*reduces, out_copies),
+            (1, 7): lambda: each(*reduces),
+        }
+
+    def staged(phase, body, carried):
+        reached, turns = 0, blocks // together
+        for at, step in sorted(plan.items()):
+            if at[0] == phase:
+                carried = lax.fori_loop(reached, at[1], body, carried)
+                reached = at[1]
+                step()
+        return lax.fori_loop(reached, turns, body, carried)
     all_conv = pl.ds(0, 5 * dim)
 
     def spots(step):
@@ -1076,7 +1159,7 @@
             )
         return gain_sum
 
-    d_gain[...] = lax.fori_loop(0, blocks // together, first, jnp.zeros((1, dim), jnp.float32))
+    d_gain[...] = staged(0, first, jnp.zeros((1, dim), jnp.float32))
 
     def chain(step, carried):
         block = blocks - 1 - step
@@ -1237,9 +1320,8 @@
             d_proj[seq, pl.ds(base, STRETCH), all_conv] = low(total)
         return conv_sum, small_sum, *rims
 
-    conv_sum, small_sum, *rims = lax.fori_loop(
-        0,
-        blocks // together,
+    conv_sum, small_sum, *rims = staged(
+        1,
         last,
         (jnp.zeros((CONV, 5 * dim), jnp.float32), jnp.zeros((2, dim), jnp.float32))
         + (jnp.zeros((8, 5 * dim), jnp.float32),) * seqs,
@@ -1250,11 +1332,21 @@
     d_conv[...] = conv_sum
     d_small_sums[...] = small_sum
     if groups:
+        finish(*reduces, out_copies)
+        gate_up_own[...] = low(g_total[0])
+        down_own[...] = low(w_total[0])
         for k in range(1, HEADS):
             from_mate(spot.mate_off(k), k).wait_send()
 
 
-def mixer_backward(proj, conv, decay, gain, kept, d_mixer, groups=0, link=()):
+def team_scratch(seqs, span, width):
+    sums = pltpu.VMEM((seqs, COLS, span, width), jnp.bfloat16)
+    passing = pltpu.VMEM((seqs, COLS + 1, span, width), jnp.bfloat16)
+    total = pltpu.VMEM((seqs, span, width), jnp.float32)
+    return [sums, passing, total, dma(3, seqs, COLS), dma(3, seqs, COLS)]
+
+
+def mixer_backward(proj, conv, decay, gain, kept, d_mixer, parts=(), groups=0, link=()):
     seqs, length, width = proj.shape
     dim = gain.shape[1]
     units = seqs * (length // STRETCH)
@@ -1269,20 +1361,34 @@
             jax.ShapeDtypeStruct((seqs, dim, dim), jnp.float32),
             jax.ShapeDtypeStruct((seqs, 8, 5 * dim), jnp.float32),
         )
+    scratch = [
+        pltpu.VMEM((units, STRETCH, dim), jnp.float32),
+        pltpu.VMEM((units, dim, dim), jnp.float32),
+    ]
+    if groups:
+        gate_up_grad, down_grad, out_grad, down_parts = parts
+        low_, half = jnp.bfloat16, groups // 2
+        out_block = pltpu.VMEM((half, HEADS) + out_grad.shape[2:], low_)
+        down_block = pltpu.VMEM((half,) + down_parts.shape[1:], low_)
+        out_team = pltpu.VMEM((HEADS,) + out_grad.shape[2:], low_)
+        shapes += (
+            jax.ShapeDtypeStruct(gate_up_grad.shape[1:], low_),
+            jax.ShapeDtypeStruct(down_grad.shape[1:], low_),
+            jax.ShapeDtypeStruct(out_grad.shape[1:], low_),
+            jax.ShapeDtypeStruct(down_parts.shape[1:], jnp.float32),
+        )
+        scratch += [pltpu.VMEM((seqs, length, dim), low_), dma(HEADS), dma(HEADS), dma(3)]
+        scratch += team_scratch(1, *gate_up_grad.shape[1:]) + team_scratch(1, *down_grad.shape[1:])
+        scratch += [out_block] * 2 + [dma(groups), dma(groups), out_team, out_team]
+        scratch += [pltpu.VMEM(out_grad.shape[2:], low_), dma(HEADS), dma(HEADS)]
+        scratch += [dma(groups), dma(groups)]
+        scratch += [down_block] * 2 + [dma(groups), dma(groups)]
     return pl.pallas_call(
         functools.partial(backward_kernel, bool(link), groups),
         out_shape=shapes,
-        in_specs=[IN_VMEM] * (11 + len(link)),
+        in_specs=[IN_VMEM] * (11 + len(link) + len(parts)),
         out_specs=[IN_VMEM] * len(shapes),
-        scratch_shapes=[
-            pltpu.VMEM((units, STRETCH, dim), jnp.float32),
-            pltpu.VMEM((units, dim, dim), jnp.float32),
-        ]
-        + (
-            [pltpu.VMEM((seqs, length, dim), jnp.bfloat16), dma(HEADS), dma(HEADS), dma(1)]
-            if groups
-            else []
-        ),
+        scratch_shapes=scratch,
         compiler_params=pltpu.CompilerParams(
             vmem_limit_bytes=60 * 2**20,
             collective_id=5 if groups else None,
@@ -1294,7 +1400,7 @@
             transcendentals=units * WIDE * WIDE * 8,
         ),
         name="mixer_backward",
-    )(proj, conv, decay, gain, *kept, d_mixer, *link)
+    )(proj, conv, decay, gain, *kept, d_mixer, *link, *parts)
 
 
 def matmul(left, right):
@@ -1463,11 +1569,7 @@
     open_gate = jax.nn.sigmoid(gate)
     silu = gate * open_gate
     hidden = (silu * up).astype(bf16)
-    down = lax.psum_scatter(
-        matmul(hidden, down_part).astype(bf16), "rep", scatter_dimension=0, tiled=True
-    )
-    result = (valid * (resid + down.astype(f32))).astype(bf16)
-
+    down_parts = matmul(hidden, down_part).astype(bf16).reshape(groups, rows, width)
     d_hidden = times_transposed(grad_all, down_part)
     d_gate_up = jnp.concatenate(
         [d_hidden * up * (open_gate * (1.0 + gate * (1.0 - open_gate))), d_hidden * silu], axis=1
@@ -1484,6 +1586,22 @@
     d_mixer = times_transposed(d_branch, w_out_full)
 
     d_mixer = d_mixer.astype(bf16)
+
+    def team_share(grad):
+        grad = grad.astype(bf16)
+        if teams == 1:
+            return grad
+        return lax.psum_scatter(
+            grad, "ctx", scatter_dimension=0, tiled=True, axis_index_groups=peers
+        )
+
+    grad_parts = (
+        team_share(grad_gate_up).reshape(HEADS, own, -1),
+        team_share(grad_down).reshape(HEADS, hidden_own, width),
+        team_share(grad_out_proj).reshape(HEADS, groups, piece, width),
+        down_parts,
+    )
+    link = ()
     if teams > 1:
         def to_heads(array):
             split = array.reshape(rows, HEADS, dim).transpose(1, 0, 2)
@@ -1492,9 +1610,9 @@
                 seqs, length, dim
             )
 
-        d_mixer = to_heads(d_mixer)
+        heads_own = to_heads(d_mixer)
         later = jnp.zeros((seqs, dim, dim), f32)
-        local = mixer_backward(proj, conv_head, decay, gain, kept, d_mixer, link=(halo, later))[4]
+        local = mixer_backward(proj, conv_head, decay, gain, kept, heads_own, link=(halo, later))[4]
         locals_ = lax.all_gather(local, "ctx", axis_index_groups=peers)
         for turn in range(teams - 1, 0, -1):
             later = jnp.where(
@@ -1502,9 +1620,22 @@
                 batched(spans[0][turn].transpose(0, 2, 1), later) + locals_[turn],
                 later,
             )
-        d_proj, grad_conv, small_sums, grad_gain, _, rim = mixer_backward(
-            proj, conv_head, decay, gain, kept, d_mixer, link=(halo, later)
-        )
+        link = (halo, later)
+    d_proj, grad_conv, small_sums, grad_gain, *rims, grad_gate_up, grad_down, grad_out_proj, down = (
+        mixer_backward(
+            proj,
+            conv_head,
+            decay,
+            gain,
+            kept,
+            d_mixer.reshape(seqs, tokens, width),
+            grad_parts,
+            groups,
+            link,
+        )
+    )
+    if teams > 1:
+        rim = rims[1]
         rim = lax.ppermute(rim, "ctx", [(c, c - HEADS) for c in range(HEADS, count)])
         spill = jnp.zeros((seqs, CONV - 1, kinds * dim - dim), f32)
         for ahead in range(1, CONV):
@@ -1515,10 +1646,7 @@
         d_proj = d_proj.at[:, length - CONV + 1 :, : (kinds - 1) * dim].set(
             (last.astype(f32) + spill).astype(bf16)
         )
-    else:
-        d_proj, grad_conv, small_sums, grad_gain = mixer_backward(
-            proj, conv_head, decay, gain, kept, d_mixer.reshape(seqs, tokens, width), groups
-        )
+    result = (valid * (resid + down)).astype(bf16)
     d_proj = d_proj.reshape(seqs * length, -1)
     h_flat = h_first.reshape(seqs * length, width)
     grad_head = transposed_times(h_flat, d_proj[:, : kinds * dim]).astype(bf16)
@@ -1538,33 +1666,25 @@
         ]
     )
     packed = jnp.pad(packed, ((0, -packed.shape[0] % 8), (0, 0)))
+    grad_head = team_share(grad_head)
     if teams > 1:
-        grad_head = lax.psum_scatter(
-            grad_head, "ctx", scatter_dimension=0, tiled=True, axis_index_groups=peers
-        )
         packed = lax.psum(packed, "ctx", axis_index_groups=peers)
-    d_first, grad_in, packed = epilogue(
+    d_first, grad_in, packed, grad_gate_up, grad_down = epilogue(
         d_first.astype(bf16).reshape(seqs, length, width),
         grad_head.reshape(HEADS, groups, piece, kinds * dim),
         packed,
+        grad_gate_up,
+        grad_down,
     )
     d_inputs, _ = norm_back(inputs, gains[0], d_first.reshape(rows, width))
     in_grad = (d_resid + d_inputs).astype(bf16)
     grad_in = grad_in.reshape(groups, HEADS, piece, kinds, dim).transpose(0, 2, 3, 1, 4)
     grad_in = grad_in.reshape(own, -1)
 
-    grad_gate_up = lax.psum_scatter(
-        grad_gate_up.astype(bf16), "ctx", scatter_dimension=0, tiled=True
-    )
-    grad_gate_up = lax.all_gather(
-        grad_gate_up.reshape(own, 2, count, hidden_own), "rep", axis=3
-    ).reshape(own, -1)
-    grad_down = lax.psum_scatter(grad_down.astype(bf16), "ctx", scatter_dimension=0, tiled=True)
-    grad_down = lax.all_gather(grad_down, "rep", axis=0, tiled=True)
-    grad_out_proj = lax.psum_scatter(
-        grad_out_proj.astype(bf16), "ctx", scatter_dimension=0, tiled=True
-    )
-    grad_out_proj = lax.psum(grad_out_proj, "rep")
+    grad_gate_up = grad_gate_up.reshape(groups, own, 2, count, hidden_own)
+    grad_gate_up = grad_gate_up.transpose(1, 2, 3, 0, 4).reshape(own, -1)
+    grad_down = grad_down.reshape(groups * hidden_own, width)
+    grad_out_proj = grad_out_proj.reshape(own, width)
 
     def take(size):
         nonlocal packed

time: 649 us -> 501 us (0.77)
  waiting for transfers between devices: 154 us -> 0 us
  Pallas kernels: 327 us -> 368 us
  between operations: 15.1 us -> 1.63 us
  blocking collectives: 8.44 us -> 0 us
  matrix products: 66.3 us -> 59.4 us
  other arithmetic: 24.8 us -> 18.2 us
    reduce_scatter x4 -> x0, waiting for transfers between devices: 129 us -> none  [the longest x1 64.9 us: per_device(): lax.psum_scatter(grad_gate_up.astype(bf16), 'ctx', scatter_dimension=0, t...]
    pallas_call x1, Pallas kernels: 69.8 us -> 116 us  [mixer_backward(): pl.pallas_call(functools.partial(backward_kernel, bool(link), groups), ou...]
    psum x1 -> x0, waiting for transfers between devices: 25.2 us -> none  [per_device(): grad_out_proj = lax.psum(grad_out_proj, 'rep')]
    all_gather x1 -> x0, blocking collectives: 8.44 us -> none  [per_device(): grad_down = lax.all_gather(grad_down, 'rep', axis=0, tiled=True)]
  transfers between devices with their start and end apart: 6 -> 0, of which waited for: 4 -> 0; matrix products, arithmetic and copies ran while one was open for 12% -> 0% of each run, Pallas kernels for 28% -> 0%
where the time goes in v3:
time: 501 us; the launch traced here: 492 us
  Pallas kernels  368 us (73%)
  matrix products  59.4 us (12%)
  local copies, waits for them, and re-layouts  45 us (9%)
  other arithmetic  18.2 us (4%)
    pallas_call x1, Pallas kernels, mixer_backward(): pl.pallas_call(functools.partial(backward_kernel, bool(link), groups), ou...  116 us
    pallas_call x1, Pallas kernels, epilogue(): pl.pallas_call(functools.partial(epilogue_kernel, groups), out_shape=(jax...  84.1 us
    pallas_call x1, Pallas kernels, mixer_forward(): pl.pallas_call(functools.partial(forward_kernel, bool(link), groups), out...  77.5 us
    pallas_call x1, Pallas kernels, prologue(): pl.pallas_call(functools.partial(prologue_kernel, groups), out_shape=(jax...  56 us
    dot_general x4, matrix products, matmul(): return jnp.dot(left, right, preferred_element_type=jnp.float32)  21.9 us
    dot_general x4, matrix products, times_transposed(): lax.dot_general(left, right, (((1,), (1,)), ((), ())), preferred_element_...  20 us
    dot_general x5, matrix products, transposed_times(): lax.dot_general(left, right, (((0,), (0,)), ((), ())), preferred_element_...  17.6 us
    pallas_call x1, Pallas kernels, reduce_copies(): pl.pallas_call(functools.partial(reduce_kernel, groups), out_shape=jax.Sh...  17.2 us

profile of v3, /device:TPU:8, one launch (start us, length us, event | category | flops | bytes accessed | tf_op | source)
XLA Modules:
  0.0 492.1 jit_solution(8356202531056352070)
XLA Ops:
  3.1 2.7 reshape.293.pieces
  7.7 56.0 %prologue.1 = (bf16[2,1024,1024]{2,1,0:T(8,128)(2,1)}, bf16[8,4,32,768]{3,2,1,0:T(8,128)(2,1)}, bf16[8,46,128]{2,1,0:T(8,128)(2,1)}, bf16[4,256,1024]{2,1,0:T(8,128)(2,1)}) custom-call(bf16[2,128,1024]{2,1,0:T(8,128)(2,1)} %bitcast.162, bf16[8,4,32,768]{3,2,1,0:T(8,128)(2,1)} %reshape.293.pieces, bf16[46,128]{1,0:T(8,128)(2,1)} %maximum_bitcast_fusion.smalls, ...), custom_call_target="tpu_custom_call" | custom-call | tf_op jit(solution)/shard_map/prologue/pallas_call | solution.py:282
  63.7 3.2 fusion
  67.9 5.1 %convert_multiply_fusion = (f32[2,1024,1024]{2,1,0:T(8,128)}, bf16[2,1024,1024]{2,1,0:T(8,128)(2,1)}) fusion(bf16[2,1024,1024]{2,1,0:T(8,128)(2,1)S(1)} %copy-done.7, f32[2,1024]{1,0:T(2,128)S(1)} %add_rsqrt_fusion, f32[1024]{0:T(1024)S(1)} %get-tuple-element.112), kind=kLoop, calls=%fused_computation | loop fusion | flops 8388608 | bytes 16789504 | tf_op jit(solution)/shard_map/mul | solution.py:1530
  75.6 10.2 %fusion.5.refs_0_ = f32[2,1024,896]{2,1,0:T(8,128)} fusion(bf16[2,1024,1024]{2,1,0:T(8,128)(2,1)} %get-tuple-element.110, bf16[1024,3]{1,0:T(8,128)(2,1)S(1)} %copy.53, bf16[1024,768]{1,0:T(8,128)(2,1)} %bitcast.212, bf16[896]{0:T(1024)(128)(2,1)S(1)} %pad.12.clone), kind=kOutput, calls=%fused_computation.20 | convolution fusion | flops 3763601408 | bytes 13115136 | tf_op jit(solution)/shard_map/dot_general | solution.py:1407
  94.6 77.5 %mixer_forward.1 = (f32[2,1024,128]{2,1,0:T(8,128)}, f32[32,128,128]{2,1,0:T(8,128)}, f32[32,128,128]{2,1,0:T(8,128)}, f32[32,128,128]{2,1,0:T(8,128)}, f32[32,1...) custom-call(f32[2,1024,896]{2,1,0:T(8,128)} %fusion.5.refs_0_, ...), custom_call_target="tpu_custom_call" | custom-call | flops 4026531840 | bytes 15728640 | tf_op jit(solution)/shard_map/mixer_forward/pallas_call | solution.py:978
  175.7 17.1 %gather_copies.1 = bf16[4,256,1024]{2,1,0:T(8,128)(2,1)} custom-call(bf16[256,1024]{1,0:T(8,128)(2,1)} %multiply_convert_fusion.5.block), custom_call_target="tpu_custom_call" | custom-call | tf_op jit(solution)/shard_map/gather_copies/pallas_call | solution.py:309
  192.8 5.9 %fusion.29 = f32[1024,1408]{0,1:T(8,128)S(1)} fusion(bf16[1024,1024]{1,0:T(8,128)(2,1)} %bitcast.178, bf16[1024,1408]{1,0:T(8,128)(2,1)} %bitcast.214), kind=kOutput, calls=%fused_computation.88 | convolution fusion | flops 2952790016 | bytes 10747904 | tf_op jit(solution)/shard_map/dot_general | solution.py:1407
  198.8 3.0 multiply_convert_fusion.3
  201.8 3.8 convolution_convert_fusion.2
  205.6 17.2 %reduce_copies.1 = f32[256,1024]{1,0:T(8,128)S(1)} custom-call(bf16[4,256,1024]{2,1,0:T(8,128)(2,1)S(1)} %bitcast.158), custom_call_target="tpu_custom_call" | custom-call | tf_op jit(solution)/shard_map/reduce_copies/pallas_call | solution.py:369
  226.0 5.0 %convolution_convert_fusion = bf16[1024,1408]{1,0:T(8,128)(2,1)} fusion(bf16[1024,1024]{1,0:T(8,128)(2,1)S(1)} %bitcast.179, bf16[1024,704]{0,1:T(8,128)(2,1)S(1)} %get-tuple-element.105, bf16[1024,704]{0,1:T(8,128)(2,1)S(1)} %get-tuple-element.104), kind=kOutput, calls=%fused_computation.6 | convolution fusion | flops 2959998976 | bytes 7864320 | tf_op jit(solution)/shard_map/dot_general | solution.py:1417
  231.0 2.8 convolution_convert_fusion.4
  235.8 3.2 convolution_convert_fusion.3
  239.0 115.9 %mixer_backward.1 = (bf16[2,1024,896]{2,1,0:T(8,128)(2,1)}, f32[4,640]{1,0:T(4,128)}, f32[2,128]{1,0:T(2,128)}, f32[1,128]{1,0:T(1,128)}, bf16[128,1408]{1,0:T(8...) custom-call(f32[2,1024,896]{2,1,0:T(8,128)} %fusion.5.refs_0_, ...), custom_call_target="tpu_custom_call" | custom-call | flops 4026531840 | bytes 15728640 | tf_op jit(solution)/shard_map/mixer_backward/pallas_call | solution.py:1386
  357.1 11.6 %fusion.1 = (f32[1024]{0:T(1024)S(1)}, bf16[2048,1024]{1,0:T(8,128)(2,1)}) fusion(f32[2,1024,1024]{2,1,0:T(8,128)} %get-tuple-element.109, bf16[2048,896]{1,0:T(8,128)(2,1)} %bitcast.195, bf16[1024,3]{1,0:T(8,128)(2,1)S(1)} %copy.53, bf16[1024,768]{1,0:T(8,128)(2,1)} %bitcast.213, bf16[896]{0:T(1024)(128)(2,1)S(1)} %pad.12.clone), kind=kOutput, calls=%fused_computation.4 | convolution fusion | flops 3769891840 | bytes 17837824 | tf_op jit(solution)/shard_map/dot_general | solution.py:1411
  368.7 4.6 fusion.7
  373.4 3.1 fusion.19
  376.9 84.1 %epilogue.1 = (f32[2,128,1024]{2,1,0:T(8,128)S(1)}, bf16[4,8,32,768]{3,2,1,0:T(8,128)(2,1)}, f32[8,64,128]{2,1,0:T(8,128)S(1)}, bf16[4,128,1408]{2,1,0:T(8,128)(2,1)S(1)}, bf16[4,88,1024]{2,1,0:T(8,128)(2,1)S(1)}) custom-call(bf16[2,1024,1024]{2,1,0:T(8,128)(2,1)} %bitcast.171, bf16[8,4,32,768]{3,2,1,0:T(8,128)(2,1)} %bitcast.181, f32[64,128]{1,0:T(8,128)S(1)} %pad.5.smalls, ...), custom_call_target="tpu_custom_call" | custom-call | tf_op jit(solution)/shard_map/epilogue/pallas_call | solution.py:551
  463.2 4.6 reshape.345
  467.8 5.7 %copy.58 = f32[4,32,6,8,128]{4,3,2,1,0:T(8,128)} copy(f32[4,32,6,8,128]{4,2,1,3,0:T(8,128)} %bitcast.159) | data formatting | bytes 6291456 | tf_op jit(solution)/shard_map/convert_element_type | solution.py:1712
  473.5 4.3 reshape.340
  483.2 3.7 copy.63
  486.9 3.4 copy.66
  (129 shorter events, 36.7 us)
Async XLA Ops:
  0.6 93.3 %copy-start = (bf16[352,1024]{1,0:T(8,128)(2,1)S(1)}, bf16[352,1024]{1,0:T(8,128)(2,1)}, u32[]{:S(2)}) copy-start(bf16[352,1024]{1,0:T(8,128)(2,1)} %param.24) | copy-start | bytes 2162692
  2.5 3.3 copy-start.18
  2.5 3.3 copy-start.17
  2.5 3.6 copy-start.20
  2.5 4.2 copy-start.21
  2.5 4.2 copy-start.13
  63.7 4.2 copy-start.7
  75.6 10.9 %copy-start.24 = (f32[8]{0:T(128)S(1)}, f32[8]{0:T(128)}, u32[]{:S(2)}) copy-start(f32[8]{0:T(128)} %param.19) | copy-start | bytes 100
  75.6 11.5 %copy-start.25 = (f32[8]{0:T(128)S(1)}, f32[8]{0:T(128)}, u32[]{:S(2)}) copy-start(f32[8]{0:T(128)} %param.20) | copy-start | bytes 100
  94.6 77.5 %copy-start.8 = (bf16[2,1,128,1024]{3,2,1,0:T(8,128)(2,1)S(1)}, bf16[2,1,128,1024]{3,2,1,0:T(8,128)(2,1)}, u32[]{:S(2)}) copy-start(bf16[2,1,128,1024]{3,2,1,0:T(8,128)(2,1)} %param.13) | copy-start | bytes 1572868
  192.8 6.0 %copy-start.22 = (bf16[4,256,1024]{2,1,0:T(8,128)(2,1)S(1)}, bf16[4,256,1024]{2,1,0:T(8,128)(2,1)}, u32[]{:S(2)}) copy-start(bf16[4,256,1024]{2,1,0:T(8,128)(2,1)} %get-tuple-element.50) | copy-start | bytes 6291460
  192.8 6.0 %copy-start.27 = (bf16[8,88,1024]{2,1,0:T(8,128)(2,1)S(1)}, bf16[8,88,1024]{2,1,0:T(8,128)(2,1)}, u32[]{:S(2)}) copy-start(bf16[8,88,1024]{2,1,0:T(8,128)(2,1)} %get-tuple-element.51) | copy-start | bytes 4325380
  224.4 9.3 %copy-start.4 = (f32[256,1024]{1,0:T(8,128)}, f32[256,1024]{1,0:T(8,128)S(1)}, u32[]{:S(2)}) copy-start(f32[256,1024]{1,0:T(8,128)S(1)} %multiply_add_fusion) | copy-start | bytes 3145732
  357.1 11.6 %copy-start.6 = (bf16[2,1024,1024]{2,1,0:T(8,128)(2,1)S(1)}, bf16[2,1024,1024]{2,1,0:T(8,128)(2,1)}, u32[]{:S(2)}) copy-start(bf16[2,1024,1024]{2,1,0:T(8,128)(2,1)} %get-tuple-element.110) | copy-start | bytes 12582916
  357.1 11.6 %copy-start.15 = (bf16[2,1024,896]{2,1,0:T(8,128)(2,1)S(1)}, bf16[2,1024,896]{2,1,0:T(8,128)(2,1)}, u32[]{:S(2)}) copy-start(bf16[2,1024,896]{2,1,0:T(8,128)(2,1)} %get-tuple-element.54) | copy-start | bytes 11010052
  373.4 3.2 copy-start.16
  373.4 3.2 copy-start.23
  373.4 3.5 copy-start.19
  373.4 3.5 copy-start.2
  373.4 3.5 copy-start.3
  376.9 84.1 %copy-start.9 = (bf16[2,1,128,1024]{3,2,1,0:T(8,128)(2,1)S(1)}, bf16[2,1,128,1024]{3,2,1,0:T(8,128)(2,1)}, u32[]{:S(2)}) copy-start(bf16[2,1,128,1024]{3,2,1,0:T(8,128)(2,1)} %param.13) | copy-start | bytes 1572868
  376.9 84.6 %copy-start.5 = (f32[256,1024]{1,0:T(8,128)S(1)}, f32[256,1024]{1,0:T(8,128)}, u32[]{:S(2)}) copy-start(f32[256,1024]{1,0:T(8,128)} %copy-done.4) | copy-start | bytes 3145732
  473.5 6.9 %copy-start.14 = (bf16[4,32,1024]{2,1,0:T(8,128)(2,1)S(1)}, bf16[4,32,1024]{2,1,0:T(8,128)(2,1)}, u32[]{:S(2)}) copy-start(bf16[4,32,1024]{2,1,0:T(8,128)(2,1)} %get-tuple-element.63) | copy-start | bytes 786436
  486.9 4.8 copy-start.1
  (4 other events, 10.1 us)

commit v4 on v1

v4 whole, which is shorter than its diff:
```python
import functools
import jax
import jax.numpy as jnp
from jax import lax
from jax.experimental import pallas as pl
from jax.experimental.pallas import tpu as pltpu
from jax.sharding import PartitionSpec as P

STEPS = 2
CONV = 4
STRETCH = 64
HEADS = 8
EPS = 1e-06
WIDE = 2 * STRETCH


MESH = pl.DeviceIdType.MESH
ROWS = 2
COLS = HEADS // ROWS


class Spot:
    def __init__(self, groups):
        place = lax.axis_index("ctx")
        self.mate = lax.rem(place, HEADS)
        self.base = place - self.mate
        self.col = lax.div(self.mate, ROWS)
        self.row = lax.rem(self.mate, ROWS)
        self.groups = groups
        self.group = lax.axis_index("rep")
        self.side = lax.rem(self.group, 2)
        self.pair = lax.div(self.group, 2)
        self.twin = self.group + 1 - 2 * self.side

    def to_mate(self, mate):
        return {"ctx": self.base + mate}

    def to_group(self, group):
        return {"rep": group}

    def mate_off(self, k):
        return lax.rem(self.mate + k, HEADS)

    def group_off(self, k):
        return lax.rem(self.group + 2 * k, self.groups)

    def barrier(self, team=True, copies=True):
        sem = pltpu.get_barrier_semaphore()
        others = []
        if team:
            others += [self.to_mate(self.mate_off(k)) for k in range(1, HEADS)]
        if copies:
            others += [self.to_group(self.twin)]
            others += [self.to_group(self.group_off(k)) for k in range(1, self.groups // 2)]
        for other in others:
            pl.semaphore_signal(sem, inc=1, device_id=other, device_id_type=MESH)
        pl.semaphore_wait(sem, len(others))


def remote(src, dst, send, recv, where):
    return pltpu.make_async_remote_copy(
        src_ref=src,
        dst_ref=dst,
        send_sem=send,
        recv_sem=recv,
        device_id=where,
        device_id_type=MESH,
    )


TEAM_SEMS = 3 * COLS + 1


def team_gather(spot, src, out, send, recv, own):
    mate, col = spot.mate, spot.col
    up, down = spot.to_mate(mate + ROWS), spot.to_mate(mate - ROWS)
    across = spot.to_mate(mate + 1 - 2 * spot.row)
    other = mate + 1 - 2 * spot.row
    local = pltpu.make_async_copy(src, out(mate), own)

    def hop(block, origin, slot, where):
        return remote(block, out(origin), send.at[slot], recv.at[slot], where)

    rise, fall, cross_low, cross_high = 0, COLS - 1, 2 * COLS - 2, 3 * COLS - 3
    last = COLS - 1
    local.start()

    @pl.when(col < last)
    def _():
        hop(src, mate, rise, up).start()

    @pl.when(col > 0)
    def _():
        hop(src, mate, fall, down).start()

    hop(src, mate, cross_low, across).start()
    yield
    for k in range(1, COLS):
        below, above = mate - ROWS * k, mate + ROWS * k

        @pl.when(col >= k)
        def _():
            hop(out(below), below, rise + k - 1, up).wait_recv()
            if k < last:

                @pl.when(col < last)
                def _():
                    hop(out(below), below, rise + k, up).start()

            hop(out(below), below, cross_low + k, across).start()

        @pl.when(col + k <= last)
        def _():
            hop(out(above), above, fall + k - 1, down).wait_recv()
            if k < last:

                @pl.when(col > 0)
                def _():
                    hop(out(above), above, fall + k, down).start()

            hop(out(above), above, cross_high + k, across).start()

        yield
    hop(src, other, cross_low, across).wait_recv()
    for k in range(1, COLS):

        @pl.when(col >= k)
        def _():
            hop(src, other - ROWS * k, cross_low + k, across).wait_recv()

        @pl.when(col + k <= last)
        def _():
            hop(src, other + ROWS * k, cross_high + k, across).wait_recv()

    @pl.when(col < last)
    def _():
        hop(src, mate, rise, up).wait_send()

    @pl.when(col > 0)
    def _():
        hop(src, mate, fall, down).wait_send()

    hop(src, mate, cross_low, across).wait_send()
    for k in range(1, COLS):

        @pl.when(col >= k)
        def _():
            if k < last:

                @pl.when(col < last)
                def _():
                    hop(src, mate, rise + k, up).wait_send()

            hop(src, mate, cross_low + k, across).wait_send()

        @pl.when(col + k <= last)
        def _():
            if k < last:

                @pl.when(col > 0)
                def _():
                    hop(src, mate, fall + k, down).wait_send()

            hop(src, mate, cross_high + k, across).wait_send()

    local.wait()
    yield


def rep_gather(spot, src, out, send, recv, own):
    group, twin, half = spot.group, spot.twin, spot.groups // 2
    local = None
    if own is not None:
        local = pltpu.make_async_copy(src, out(group), own)
        local.start()

    def hop(block, origin, slot, where):
        return remote(block, out(origin), send.at[slot], recv.at[slot], spot.to_group(where))

    hop(src, group, 0, twin).start()
    for k in range(1, half):
        hop(src, group, k, spot.group_off(k)).start()
    yield
    for k in range(1, half):
        origin = spot.group_off(half - k)
        hop(out(origin), origin, k, twin).wait_recv()
        hop(out(origin), origin, half + k, twin).start()
    yield
    hop(src, twin, 0, twin).wait_recv()
    for k in range(1, half):
        origin = lax.rem(twin + 2 * (half - k), spot.groups)
        hop(src, origin, half + k, twin).wait_recv()
    hop(src, group, 0, twin).wait_send()
    for k in range(1, half):
        hop(src, group, k, twin).wait_send()
        hop(src, group, half + k, twin).wait_send()
    if local is not None:
        local.wait()
    yield


def team_exchange(spot, src, dst, send, recv, own):
    local = pltpu.make_async_copy(src(spot.mate), dst(spot.mate), own)
    local.start()

    def hop(k):
        to = spot.mate_off(k)
        return remote(src(to), dst(spot.mate), send.at[k], recv.at[k], spot.to_mate(to))

    for k in range(1, HEADS):
        hop(k).start()
    yield
    for k in range(1, HEADS):
        hop(k).wait_recv()
    for k in range(1, HEADS):
        hop(k).wait_send()
    local.wait()
    yield


def dma(*shape):
    return pltpu.SemaphoreType.DMA(shape)


ANY = pl.BlockSpec(memory_space=pl.ANY)
IN_VMEM = pl.BlockSpec(memory_space=pltpu.VMEM)


def finish(*steps):
    for step in steps:
        for _ in step:
            pass


def rep_reduce(spot, part, sums, others, send, recv):
    half, side = spot.groups // 2, spot.side

    def to_twin(k):
        return remote(
            part(2 * k + 1 - side), sums.at[k], send.at[k], recv.at[k], spot.to_group(spot.twin)
        )

    def onward(k):
        slot = half + k
        return remote(
            sums.at[lax.rem(spot.pair + k, half)], others.at[k], send.at[slot], recv.at[slot], spot.to_group(spot.group_off(k))
        )

    for k in range(half):
        to_twin(k).start()
    yield
    for k in range(half):
        to_twin(k).wait_recv()

    def both(pair):
        return part(2 * pair + side)[...].astype(jnp.float32) + sums[pair].astype(jnp.float32)

    for k in range(1, half):
        pair = lax.rem(spot.pair + k, half)
        sums[pair] = both(pair).astype(sums.dtype)
        onward(k).start()
    yield
    total = both(spot.pair)
    for k in range(1, half):
        onward(k).wait_recv()
        total = total + others[k].astype(jnp.float32)
    for k in range(half):
        to_twin(k).wait_send()
    for k in range(1, half):
        onward(k).wait_send()
    yield total


class Lane:
    def __init__(self, part, sums, passing, total, send, recv):
        self.part, self.sums, self.passing = part, sums, passing
        self.total, self.send, self.recv = total, send, recv


def team_reduce(spot, lanes, window):
    mate, col, row = spot.mate, spot.col, spot.row
    up, down = spot.to_mate(mate + ROWS), spot.to_mate(mate - ROWS)
    across = spot.to_mate(mate + 1 - 2 * row)
    last = COLS - 1
    f32 = jnp.float32

    def hop(lane, d, way):
        src = lane.part(ROWS * d + 1 - row) if way == 0 else lane.sums.at[d]
        dst = (lane.sums.at[d], lane.passing.at[d + 1], lane.passing.at[d])[way]
        return remote(
            src, dst, lane.send.at[way, d], lane.recv.at[way, d], (across, up, down)[way]
        )

    def both(lane, d):
        return lane.part(ROWS * d + row)[...].astype(f32) + lane.sums[d].astype(f32)

    def crossed(lane, d):
        hop(lane, d, 0).wait_recv()

        @pl.when(col == d)
        def _():
            lane.total[...] = both(lane, d)

        for end, way in ((0, 1), (last, 2)):
            if d != end:

                @pl.when(col == end)
                def _():
                    lane.sums[d] = both(lane, d).astype(lane.sums.dtype)
                    hop(lane, d, way).start()

    def passed(lane, d, c, way):
        @pl.when(col == c)
        def _():
            hop(lane, d, way).wait_recv()
            got = lane.passing[d + 2 - way].astype(f32)
            if c == d:
                lane.total[...] += got
            else:
                lane.sums[d] = (both(lane, d) + got).astype(lane.sums.dtype)
                hop(lane, d, way).start()

    order_out = [d for pair in zip(range(last, -1, -1), range(COLS)) for d in pair][:COLS]
    rounds = {}
    for i, d in enumerate(order_out):
        for k, lane in enumerate(lanes):
            time = i * len(lanes) + k
            rounds.setdefault(time, []).append(functools.partial(crossed, lane, d))
            for c in range(1, d + 1):
                step = functools.partial(passed, lane, d, c, 1)
                rounds.setdefault(time + c, []).append(step)
            for c in range(d, last):
                step = functools.partial(passed, lane, d, c, 2)
                rounds.setdefault(time + last - c, []).append(step)
    ahead = [(lane, d) for d in order_out for lane in lanes]
    for lane, d in ahead[:window]:
        hop(lane, d, 0).start()
    yield
    for time in sorted(rounds):
        for k, step in enumerate(rounds[time]):
            step()
            if k == 0 and time + window < len(ahead):
                lane, d = ahead[time + window]
                hop(lane, d, 0).start()
        yield
    for d in range(COLS):
        for lane in lanes:
            hop(lane, d, 0).wait_send()

            @pl.when(col < d)
            def _():
                hop(lane, d, 1).wait_send()

            @pl.when(col > d)
            def _():
                hop(lane, d, 2).wait_send()

    yield


def advance(step, count):
    for _ in range(count):
        next(step, None)


def lane_scratch(count, rows, width):
    return [
        pltpu.VMEM((count, COLS, rows, width), jnp.bfloat16),
        pltpu.VMEM((count, COLS + 1, rows, width), jnp.bfloat16),
        dma(count, 3, COLS),
        dma(count, 3, COLS),
    ]


class Job:
    def __init__(self, make, ins=(), outs=(), scratch=(), spaces=None):
        self.make, self.ins, self.outs, self.scratch = make, list(ins), list(outs), list(scratch)
        self.in_space, self.out_space = spaces or (ANY, ANY)


def fused_call(body, ins, outs, scratch, jobs, groups, number, name, vmem, cost=None, copies=True):
    def kernel(*refs):
        refs = list(refs)

        def take(count):
            part = refs[:count]
            del refs[:count]
            return part

        own_in = take(len(ins))
        jobs_in = [take(len(job.ins)) for job in jobs]
        own_out = take(len(outs))
        jobs_out = [take(len(job.outs)) for job in jobs]
        own_scratch = take(len(scratch))
        jobs_scratch = [take(len(job.scratch)) for job in jobs]
        spot = None
        if number:
            spot = Spot(groups)
            spot.barrier(copies=copies)
        steps = [
            job.make(spot, a, b, c)
            for job, a, b, c in zip(jobs, jobs_in, jobs_out, jobs_scratch)
        ]
        body(spot, own_in, own_out, own_scratch, steps)
        finish(*steps)

    results = pl.pallas_call(
        kernel,
        out_shape=[s for s, _ in outs] + [s for job in jobs for s in job.outs],
        in_specs=[spec for _, spec in ins] + [job.in_space for job in jobs for _ in job.ins],
        out_specs=[spec for _, spec in outs] + [job.out_space for job in jobs for _ in job.outs],
        scratch_shapes=list(scratch) + [s for job in jobs for s in job.scratch],
        compiler_params=pltpu.CompilerParams(
            collective_id=number, has_side_effects=bool(number), vmem_limit_bytes=vmem * 2**20
        ),
        cost_estimate=cost,
        name=name,
    )(*[a for a, _ in ins], *[a for job in jobs for a in job.ins])
    results = list(results)
    own, rest = results[: len(outs)], results[len(outs) :]
    given = []
    for job in jobs:
        given.append(rest[: len(job.outs)])
        rest = rest[len(job.outs) :]
    return own, given


def staged(turns, body, carried, marks):
    reached = 0
    for at in sorted(marks):
        if at > reached:
            carried = lax.fori_loop(reached, at, body, carried)
            reached = at
        marks[at]()
    if reached < turns:
        carried = lax.fori_loop(reached, turns, body, carried)
    return carried


def marks_of(plan, phase, steps):
    def mark(moves):
        def go():
            for job, count in moves:
                advance(steps[job], count)

        return go

    return {turn: mark(moves) for (at, turn), moves in plan.items() if at == phase}


def shape(dims, kind):
    return jax.ShapeDtypeStruct(tuple(dims), kind)


def team_gather_job(block, groups=None, twofold=False):
    low_ = block.dtype
    if not twofold:

        def make(spot, ins, outs, scratch):
            return team_gather(spot, ins[0], lambda m: outs[0].at[m], *scratch[:2], scratch[2].at[0])

        return Job(
            make, [block], [shape((HEADS,) + block.shape, low_)],
            [dma(TEAM_SEMS), dma(TEAM_SEMS), dma(1)],
        )

    def make(spot, ins, outs, scratch):
        whole = outs[0]
        yield from team_gather(
            spot, ins[0], lambda m: whole.at[m, spot.group], *scratch[:2], scratch[4].at[0]
        )
        yield from rep_gather(
            spot, whole.at[:, spot.group], lambda g: whole.at[:, g], *scratch[2:4], None
        )

    return Job(
        make, [block], [shape((HEADS, groups) + block.shape, low_)],
        [dma(TEAM_SEMS), dma(TEAM_SEMS), dma(groups), dma(groups), dma(1)],
    )


def sequences_job(block):
    seqs = block.shape[0]

    def make(spot, ins, outs, scratch):
        gathers = [
            team_gather(
                spot, ins[0].at[seq], lambda m, seq=seq: outs[0].at[seq, m],
                scratch[0].at[seq], scratch[1].at[seq], scratch[2].at[seq],
            )
            for seq in range(seqs)
        ]
        for _ in zip(*gathers):
            yield

    return Job(
        make, [block], [shape((seqs, HEADS) + block.shape[1:], block.dtype)],
        [dma(seqs, TEAM_SEMS), dma(seqs, TEAM_SEMS), dma(seqs)],
    )


def rep_gather_job(block, groups, space=ANY):
    def make(spot, ins, outs, scratch):
        return rep_gather(spot, ins[0], lambda g: outs[0].at[g], *scratch[:2], scratch[2].at[0])

    return Job(
        make, [block], [shape((groups,) + block.shape, block.dtype)],
        [dma(groups), dma(groups), dma(1)], (space, space),
    )


def rep_reduce_job(parts, groups):
    block = pltpu.VMEM((groups // 2,) + parts.shape[1:], parts.dtype)

    def make(spot, ins, outs, scratch):
        for total in rep_reduce(spot, lambda g: ins[0].at[g], *scratch):
            if total is not None:
                outs[0][...] = total
            yield

    return Job(
        make, [parts], [shape(parts.shape[1:], jnp.float32)],
        [block, block, dma(groups), dma(groups)], (IN_VMEM, IN_VMEM),
    )


def tokens_job(parts, halves):
    seqs, _, rows, width = parts.shape
    rows_of = rows // halves

    def make(spot, ins, outs, scratch):
        sums, passing, send, recv = scratch
        lanes = []
        for seq in range(seqs):
            for half in range(halves):
                k, own = seq * halves + half, pl.ds(half * rows_of, rows_of)
                lanes.append(
                    Lane(
                        lambda mate, seq=seq, own=own: ins[0].at[seq, mate, own],
                        sums.at[k], passing.at[k], outs[0].at[seq, own], send.at[k], recv.at[k],
                    )
                )
        return team_reduce(spot, lanes, 2 * halves)

    return Job(
        make, [parts], [shape((seqs, rows, width), jnp.float32)],
        lane_scratch(seqs * halves, rows_of, width), (IN_VMEM, IN_VMEM),
    )


def team_reduce_job(parts, pieces, window, kind):
    _, rows, width = parts.shape
    rows_of = rows // pieces

    def make(spot, ins, outs, scratch):
        sums, passing, send, recv, *total = scratch
        total = total[0] if total else outs[0]
        lanes = []
        for k in range(pieces):
            own = pl.ds(k * rows_of, rows_of)
            lanes.append(
                Lane(
                    lambda mate, own=own: ins[0].at[mate, own],
                    sums.at[k], passing.at[k], total.at[own], send.at[k], recv.at[k],
                )
            )
        yield from team_reduce(spot, lanes, window)
        if kind != jnp.float32:
            outs[0][...] = total[...].astype(kind)
        yield

    scratch = lane_scratch(pieces, rows_of, width)
    if kind != jnp.float32:
        scratch.append(pltpu.VMEM((rows, width), jnp.float32))
    return Job(make, [parts], [shape((rows, width), kind)], scratch, (IN_VMEM, IN_VMEM))


def both_reduce_job(parts, groups):
    heads, _, rows, width = parts.shape
    low_ = parts.dtype
    block = pltpu.VMEM((groups // 2, heads, rows, width), low_)
    team = pltpu.VMEM((heads, rows, width), low_)

    def make(spot, ins, outs, scratch):
        sums, others, quarter, arrived, r_send, r_recv, e_send, e_recv, own = scratch
        for total in rep_reduce(
            spot, lambda g: ins[0].at[:, g], sums, others, r_send, r_recv
        ):
            if total is None:
                yield
        quarter[...] = total.astype(low_)
        exchange = team_exchange(
            spot, lambda m: quarter.at[m], lambda m: arrived.at[m], e_send, e_recv, own.at[0]
        )
        next(exchange)
        yield
        finish(exchange)
        outs[0][...] = sum(arrived[m].astype(jnp.float32) for m in range(heads)).astype(low_)
        yield

    return Job(
        make, [parts], [shape((rows, width), low_)],
        [block, block, team, team]
        + [dma(groups), dma(groups), dma(HEADS), dma(HEADS), dma(1)],
        (IN_VMEM, IN_VMEM),
    )


def deal_job(parts, groups):
    heads, _, piece, cols = parts.shape
    low_, f32 = parts.dtype, jnp.float32
    kinds = 2 + 2 * STEPS
    dim = cols // kinds
    block = pltpu.VMEM((groups // 2, heads, piece, cols), low_)

    def make(spot, ins, outs, scratch):
        sums, others, quarter, dealt, r_send, r_recv, e_send, e_recv, g_send, g_recv, own = scratch
        for total in rep_reduce(
            spot, lambda g: ins[0].at[:, g], sums, others, r_send, r_recv
        ):
            if total is None:
                yield
        quarter[...] = total.astype(low_)
        exchange = team_exchange(
            spot, lambda m: quarter.at[m], lambda m: dealt.at[spot.group, m],
            e_send, e_recv, own.at[0],
        )
        next(exchange)
        yield
        finish(exchange)
        yield from rep_gather(
            spot, dealt.at[spot.group], lambda g: dealt.at[g], g_send, g_recv, None
        )
        for g in range(groups):
            for h in range(heads):
                rows = dealt[g, h].astype(f32)
                for k in range(kinds):
                    at = (k * heads + h) * dim
                    outs[0][g, :, at : at + dim] = rows[:, k * dim : (k + 1) * dim]
        yield

    return Job(
        make, [parts], [shape((groups, piece, heads * cols), f32)],
        [block, block, pltpu.VMEM((heads, piece, cols), low_)]
        + [pltpu.VMEM((groups, heads, piece, cols), low_)]
        + [dma(groups), dma(groups), dma(HEADS), dma(HEADS), dma(groups), dma(groups), dma(1)],
        (IN_VMEM, IN_VMEM),
    )


def small_job(smalls, groups):
    def make(spot, ins, outs, scratch):
        copies, total, s_send, s_recv, x_send, x_recv, own = scratch
        yield from rep_gather(spot, ins[0], lambda g: copies.at[g], s_send, s_recv, own.at[0])
        total[...] = sum(copies[g] for g in range(groups))
        yield from team_exchange(
            spot, lambda m: total, lambda m: outs[0].at[m], x_send, x_recv, own.at[1]
        )

    return Job(
        make, [smalls], [shape((HEADS,) + smalls.shape, jnp.float32)],
        [pltpu.VMEM((groups,) + smalls.shape, jnp.float32), pltpu.VMEM(smalls.shape, jnp.float32)]
        + [dma(groups), dma(groups), dma(HEADS), dma(HEADS), dma(2)],
        (IN_VMEM, IN_VMEM),
    )


def head_job(pieces, groups):
    def make(spot, ins, outs, scratch):
        e_send, e_recv, w_send, w_recv, own = scratch
        yield from team_exchange(
            spot, lambda m: ins[0].at[m, spot.group], lambda m: outs[0].at[m, spot.group],
            e_send, e_recv, own.at[0],
        )
        yield from rep_gather(
            spot, outs[0].at[:, spot.group], lambda g: outs[0].at[:, g], w_send, w_recv, None
        )

    return Job(
        make, [pieces], [shape(pieces.shape, pieces.dtype)],
        [dma(HEADS), dma(HEADS), dma(groups), dma(groups), dma(1)],
    )


def spread_job(block):
    def make(spot, ins, outs, scratch):
        return team_exchange(
            spot, lambda m: ins[0], lambda m: outs[0].at[m], *scratch[:2], scratch[2].at[0]
        )

    return Job(
        make, [block], [shape((HEADS,) + block.shape, block.dtype)], [dma(HEADS), dma(HEADS), dma(1)]
    )


def carry(jobs, plan, groups, number, name, vmem=40):
    def body(spot, ins, outs, scratch, steps):
        for job in plan:
            advance(steps[job], 1)

    return fused_call(body, [], [], [], jobs, groups, number, name, vmem)[1]


def low(a):
    return a.astype(jnp.bfloat16)


def halves(a):
    high = low(a)
    return high, low(a - high.astype(jnp.float32))


def dot(a, b, dims):
    return lax.dot_general(a, b, (dims, ((), ())), preferred_element_type=jnp.float32)


def fold(out):
    half = out.shape[1] // 2
    return out[:, :half] + out[:, half:]


def left_nn(parts):
    return jnp.concatenate(parts, axis=1)


def right_nn(parts):
    row = jnp.concatenate(parts, axis=1)
    return jnp.concatenate([row, row], axis=0)


def right_nt(parts):
    high, rest = parts
    return jnp.concatenate(
        [jnp.concatenate([high, high], axis=1), jnp.concatenate([rest, rest], axis=1)], axis=0
    )


def mul(a, b):
    return fold(dot(left_nn(halves(a)), right_nn(halves(b)), ((1,), (0,))))


def mul_nt(a, b):
    return fold(dot(left_nn(halves(a)), right_nt(halves(b)), ((1,), (1,))))


def mul_tn(a, b):
    left = jnp.concatenate(halves(a), axis=0)
    return fold(dot(left, right_nn(halves(b)), ((0,), (0,))))


def iotas(rows, cols):
    return (
        lax.broadcasted_iota(jnp.int32, (rows, cols), 0),
        lax.broadcasted_iota(jnp.int32, (rows, cols), 1),
    )


def order(index):
    return STEPS * lax.rem(index, STRETCH) + lax.div(index, STRETCH)


def sigmoid(a):
    return 1.0 / (1.0 + jnp.exp(-a))


def softplus(a):
    return jnp.maximum(a, 0.0) + jnp.log1p(jnp.exp(-jnp.abs(a)))


def window(ref, halo, length, base, columns):
    before = ref[pl.ds(pl.multiple_of(jnp.maximum(base - 8, 0), 8), 8), columns]
    ahead = 0.0
    if halo is not None:
        ahead = halo[pl.ds(pl.multiple_of(lax.div(base, length) * 8, 8), 8), columns]
    first = lax.rem(base, length) == 0
    return jnp.concatenate(
        [jnp.where(first, ahead, before), ref[pl.ds(base, STRETCH), columns]], axis=0
    )


def stack(act, at, dim):
    return jnp.concatenate(
        [act[:, at * dim : (at + 1) * dim], act[:, (at + 1) * dim : (at + 2) * dim]], axis=0
    )


def convolve(rows, conv):
    total = None
    for tap in range(CONV):
        start = 8 - (CONV - 1) + tap
        term = conv[tap : tap + 1] * rows[start : start + STRETCH]
        total = term if total is None else total + term
    return total


def rates(small, decay):
    beta = jnp.concatenate([sigmoid(small[:, 0:1]), sigmoid(small[:, 1:2])], axis=0)
    gamma = -jnp.exp(decay[0:1]) * softplus(small + decay[1:2])
    row, col = iotas(STRETCH, STRETCH)
    tri = low(jnp.where(row >= col, 1.0, 0.0))
    high = low(gamma)
    rest = gamma - high.astype(jnp.float32)
    middle = low(rest)
    last = low(rest - middle.astype(jnp.float32))
    running = (
        dot(tri, high, ((1,), (0,))) + dot(tri, middle, ((1,), (0,))) + dot(tri, last, ((1,), (0,)))
    )
    return beta, running


def decays(running):
    column = running[:, 2:3]
    across = jnp.transpose(running)[2:3, :]
    row, col = iotas(STRETCH, STRETCH)
    gap = jnp.broadcast_to(column, (STRETCH, STRETCH)) - across
    upto = jnp.where(row >= col, jnp.exp(jnp.where(row >= col, gap, 0.0)), 0.0)
    before = jnp.where(row > col, upto, 0.0)
    strict = jnp.concatenate(
        [
            jnp.concatenate([before, before], axis=1),
            jnp.concatenate([upto, before], axis=1),
        ],
        axis=0,
    )
    return strict, jnp.concatenate([upto, upto], axis=1)


def level_masks():
    row, col = iotas(WIDE, WIDE)
    row, col = order(row), order(col)
    masks, size = [], 1
    while size < WIDE:
        inside = (lax.div(row, 2 * size) == lax.div(col, 2 * size)) & (
            lax.div(row, size) != lax.div(col, size)
        )
        masks.append(jnp.where(inside, 1.0, 0.0))
        size *= 2
    return [masks[0]] + [low(mask) for mask in masks[1:]]


def inverses(systems, masks):
    row, col = iotas(WIDE, WIDE)
    eye = jnp.where(row == col, 1.0, 0.0)
    solved = [eye - masks[0] * system for system in systems]
    split = [halves(system) for system in systems]
    for mask in masks[1:]:
        parts = [halves(a) for a in solved]
        steps = [
            fold(
                dot(
                    jnp.concatenate([high * mask, rest * mask], axis=1),
                    right_nn(part),
                    ((1,), (0,)),
                )
            )
            for (high, rest), part in zip(split, parts)
        ]
        solved = [
            a - fold(dot(left_nn(part), right_nn(halves(step)), ((1,), (0,))))
            for a, part, step in zip(solved, parts, steps)
        ]
    return solved


def unit_rows(stacked):
    return lax.rsqrt(jnp.sum(stacked * stacked, axis=1, keepdims=True) + EPS)


def twice(column):
    return jnp.concatenate([column, column], axis=0)


TOGETHER = 4


def forward_body(linked, seqs, spot, ins, outs, scratch, steps, plan):
    tokens, norm_gain, head, conv, decay, gain, *link = ins
    proj, normed, out, fresh, inv, weights, trans, states, *more = outs
    local, offset, mixer, *sems = scratch
    halo = None
    if linked:
        halo, start = link
        final, product, *more = more
    length = proj.shape[0] // seqs
    dim = gain.shape[1]
    blocks = length // STRETCH
    each = TOGETHER // seqs
    turns = blocks // each
    masks = level_masks()
    row, col = iotas(dim, dim)
    diagonal = row == col

    def project(step, _):
        at = pl.ds(pl.multiple_of(step * TOGETHER * STRETCH, STRETCH), TOGETHER * STRETCH)
        rows = tokens[at].astype(jnp.float32)
        scale = lax.rsqrt(jnp.mean(rows * rows, axis=1, keepdims=True) + EPS)
        rows = low(rows * scale * norm_gain[...])
        normed[at] = rows
        proj[at] = dot(rows, head[...], ((1,), (0,)))
        return 0

    staged(seqs * blocks // TOGETHER, project, 0, marks_of(plan, 0, steps))

    def spots(step):
        return [seq * blocks + step * each + k for k in range(each) for seq in range(seqs)]

    def first(step, _):
        units = spots(step)
        kept = []
        for block in units:
            base = pl.multiple_of(block * STRETCH, STRETCH)
            rows = window(proj, halo, length, base, pl.ds(0, 5 * dim))
            pre = convolve(rows, conv)
            act = pre * sigmoid(pre)
            raw = stack(act, 1, dim)
            key = raw * unit_rows(raw)
            beta, running = rates(proj[pl.ds(base, STRETCH), pl.ds(6 * dim, dim)], decay)
            kept.append((act[:, :dim], key, stack(act, 3, dim), beta, running))
        systems = []
        for block, (query, key, value, beta, running) in zip(units, kept):
            at = block
            strict, upto = decays(running)
            key_halves = halves(key)
            both = fold(
                dot(
                    jnp.concatenate([left_nn(key_halves), left_nn(halves(query))], axis=0),
                    right_nt(key_halves),
                    ((1,), (1,)),
                )
            )
            systems.append(beta * both[:WIDE] * strict)
            local[at] = both[WIDE:] * upto
            offset[at] = query * jnp.exp(running[:, 2:3])
        for block, (query, key, value, beta, running), solved in zip(
            units, kept, inverses(systems, masks)
        ):
            at = block
            inv[at] = solved
            grown = twice(jnp.exp(running[:, 2:3]))
            end = running[STRETCH - 1 :, 2:3]
            solved_left = left_nn(halves(solved))
            weight = fold(dot(solved_left, right_nn(halves(beta * key * grown)), ((1,), (0,))))
            value = fold(dot(solved_left, right_nn(halves(beta * value)), ((1,), (0,))))
            weights[at] = weight
            fresh[at] = value
            to_end = jnp.concatenate(halves(key * twice(jnp.exp(end - running[:, 2:3]))), axis=0)
            trans[at] = jnp.where(diagonal, jnp.exp(end), 0.0) - fold(
                dot(to_end, right_nn(halves(weight)), ((0,), (0,)))
            )
            states[at] = fold(dot(to_end, right_nn(halves(value)), ((0,), (0,))))
        return 0

    staged(turns, first, 0, marks_of(plan, 1, steps))

    def chain(step, carried):
        new = []
        for seq, state in enumerate(carried):
            block = seq * blocks + step
            added = states[block]
            states[block] = state
            if linked:
                product[seq] = mul(trans[block], product[seq])
            new.append(mul(trans[block], state) + added)
        return tuple(new)

    begin = (jnp.zeros((dim, dim), jnp.float32),) * seqs
    if linked:
        for seq in range(seqs):
            product[seq] = jnp.where(diagonal, 1.0, 0.0)
        begin = tuple(start[seq] for seq in range(seqs))
    ended = lax.fori_loop(0, blocks, chain, begin)
    if linked:
        for seq in range(seqs):
            final[seq] = ended[seq]
    if spot is not None:
        (mixed,), (x_send, x_recv, own) = more, sems
        span = length // HEADS

        def block_of(seq, mate):
            return mixer.at[pl.ds(pl.multiple_of(seq * length + mate * span, span), span)]

        def columns_of(seq, mate):
            return mixed.at[seq, :, pl.ds(pl.multiple_of(mate * dim, dim), dim)]

        def to_mate(seq, mate, slot):
            return remote(
                block_of(seq, mate), columns_of(seq, spot.mate), x_send.at[seq, slot],
                x_recv.at[seq, slot], spot.to_mate(mate),
            )

        def to_self(seq):
            return pltpu.make_async_copy(
                block_of(seq, spot.mate), columns_of(seq, spot.mate), own.at[seq]
            )

    def last(step, _):
        units = spots(step)
        reads = [
            mul(
                jnp.concatenate([weights[block], offset[block]], axis=0),
                states[block],
            )
            for block in units
        ]
        for block, read in zip(units, reads):
            at = block
            base = pl.multiple_of(block * STRETCH, STRETCH)
            new = fresh[at] - read[:WIDE]
            fresh[at] = new
            result = read[WIDE:] + mul(local[at], new)
            out[pl.ds(base, STRETCH)] = result
            gate = proj[pl.ds(base, STRETCH), pl.ds(5 * dim, dim)]
            scale = lax.rsqrt(jnp.mean(result * result, axis=1, keepdims=True) + EPS)
            mixer[pl.ds(base, STRETCH)] = low(
                result * scale * gain[...] * (gate * sigmoid(gate))
            )
        if spot is not None:
            mates = each * STRETCH // span
            for k in range(mates):
                to = step * mates + k
                slot = lax.rem(to - spot.mate + HEADS, HEADS)

                @pl.when(slot == 0)
                def _():
                    for seq in range(seqs):
                        to_self(seq).start()

                @pl.when(slot != 0)
                def _():
                    for seq in range(seqs):
                        to_mate(seq, to, slot).start()

        return 0

    staged(turns, last, 0, marks_of(plan, 2, steps))
    if spot is not None:
        for seq in range(seqs):
            for k in range(1, HEADS):
                to_mate(seq, spot.mate_off(k), k).wait_recv()
            for k in range(1, HEADS):
                to_mate(seq, spot.mate_off(k), k).wait_send()
            to_self(seq).wait()


def mixer_cost(units):
    return pl.CostEstimate(
        flops=units * 60 * WIDE * WIDE * WIDE,
        bytes_accessed=units * WIDE * WIDE * 30,
        transcendentals=units * WIDE * WIDE * 8,
    )


def mixer_forward(
    tokens, norm_gain, head, conv, decay, gain, groups=0, number=None, link=(), jobs=(), plan=None
):
    seqs, length, width = tokens.shape
    tokens = tokens.reshape(seqs * length, width)
    dim = gain.shape[1]
    units = seqs * length // STRETCH
    f32, low_ = jnp.float32, jnp.bfloat16
    outs = [
        (shape((seqs * length, head.shape[1]), f32), IN_VMEM),
        (shape((seqs * length, width), low_), IN_VMEM),
        (shape((seqs * length, dim), f32), IN_VMEM),
    ]
    outs += [(shape((units, WIDE, dim), f32), IN_VMEM)] * 5
    if link:
        outs += [(shape((seqs, dim, dim), f32), IN_VMEM)] * 2
    scratch = [
        pltpu.VMEM((units, STRETCH, WIDE), f32),
        pltpu.VMEM((units, STRETCH, dim), f32),
        pltpu.VMEM((seqs * length, dim), low_),
    ]
    if number:
        outs += [(shape((seqs, length // HEADS, HEADS * dim), low_), ANY)]
        scratch += [dma(seqs, HEADS), dma(seqs, HEADS), dma(seqs)]

    def body(spot, ins, outs, scratch, steps):
        forward_body(bool(link), seqs, spot, ins, outs, scratch, steps, plan or {})

    return fused_call(
        body, [(a, IN_VMEM) for a in (tokens, norm_gain, head, conv, decay, gain, *link)], outs, scratch, jobs,
        groups, number, "mixer_forward", 56, mixer_cost(units),
    )


def backward_body(linked, seqs, spot, ins, outs, scratch, steps, plan):
    proj, conv, decay, gain, out, fresh, inv, weights, trans, states, d_mixer, tokens, head, *link = ins
    d_proj, d_conv, d_small_sums, d_gain, d_normed, d_norm_gain, *more = outs
    d_out, chained, *arrived = scratch
    halo = None
    if linked:
        halo, end_state = link
        d_start, d_first = more
    length = proj.shape[0] // seqs
    dim = gain.shape[1]
    blocks = length // STRETCH
    each = TOGETHER // seqs
    turns = blocks // each
    span = length // HEADS
    all_conv = pl.ds(0, 5 * dim)
    if spot is not None:
        d_tokens = d_mixer
        d_mixer, x_send, x_recv, own = arrived

        def block_of(seq, mate):
            return d_mixer.at[pl.ds(pl.multiple_of(seq * length + mate * span, span), span)]

        def columns_of(seq, mate):
            return d_tokens.at[seq, :, pl.ds(pl.multiple_of(mate * dim, dim), dim)]

        def from_mate(seq, mate, slot):
            return remote(
                columns_of(seq, mate), block_of(seq, mate), x_send.at[seq, slot],
                x_recv.at[seq, slot], spot.to_mate(mate),
            )

        def from_self(seq):
            return pltpu.make_async_copy(
                columns_of(seq, spot.mate), block_of(seq, spot.mate), own.at[seq]
            )

        for seq in range(seqs):
            next(
                team_exchange(
                    spot, functools.partial(columns_of, seq), functools.partial(block_of, seq),
                    x_send.at[seq], x_recv.at[seq], own.at[seq],
                )
            )

    def spots(step):
        return [
            seq * blocks + blocks - 1 - step * each - k for k in range(each) for seq in range(seqs)
        ]

    def first(step, gain_sum):
        units = spots(step)
        kept = []
        if spot is not None:
            mates = each * STRETCH // span
            for k in range(mates):
                origin = HEADS - 1 - step * mates - k
                slot = lax.rem(spot.mate - origin + HEADS, HEADS)

                @pl.when(slot == 0)
                def _():
                    for seq in range(seqs):
                        from_self(seq).wait()

                @pl.when(slot != 0)
                def _():
                    for seq in range(seqs):
                        from_mate(seq, origin, slot).wait_recv()

        for block in units:
            at = block
            base = pl.multiple_of(block * STRETCH, STRETCH)
            result = out[pl.ds(base, STRETCH)]
            gate = proj[pl.ds(base, STRETCH), pl.ds(5 * dim, dim)]
            given = d_mixer[pl.ds(base, STRETCH)].astype(jnp.float32)
            scale = lax.rsqrt(jnp.mean(result * result, axis=1, keepdims=True) + EPS)
            normal = result * scale
            open_ = sigmoid(gate)
            silu = gate * open_
            gain_sum = gain_sum + jnp.sum(given * normal * silu, axis=0, keepdims=True)
            d_proj[pl.ds(base, STRETCH), pl.ds(5 * dim, dim)] = low(
                given * normal * gain[...] * (open_ * (1.0 + gate * (1.0 - open_)))
            )
            inner = given * gain[...] * silu
            d_result = scale * (inner - normal * jnp.mean(inner * normal, axis=1, keepdims=True))
            d_out[at] = d_result
            pre = convolve(window(proj, halo, length, base, pl.ds(0, 3 * dim)), conv[:, : 3 * dim])
            act = pre * sigmoid(pre)
            raw = stack(act, 1, dim)
            _, running = rates(proj[pl.ds(base, STRETCH), pl.ds(6 * dim, dim)], decay)
            kept.append((act[:, :dim], raw * unit_rows(raw), running, d_result))
        scores = [
            mul_nt(query, key) * decays(running)[1] for query, key, running, _ in kept
        ]
        d_freshes = [mul_tn(score, unit[3]) for score, unit in zip(scores, kept)]
        for block, (query, _, running, d_result), d_fresh in zip(units, kept, d_freshes):
            at = block
            chained[at] = mul_tn(
                jnp.concatenate([query * jnp.exp(running[:, 2:3]), -weights[at]], axis=0),
                jnp.concatenate([d_result, d_fresh], axis=0),
            )
        return gain_sum

    d_gain[...] = staged(
        turns, first, jnp.zeros((1, dim), jnp.float32), marks_of(plan, 0, steps)
    )

    def chain(step, carried):
        new = []
        for seq, later in enumerate(carried):
            block = seq * blocks + blocks - 1 - step
            added = chained[block]
            chained[block] = later
            new.append(mul_tn(trans[block], later) + added)
        return tuple(new)

    begin = (jnp.zeros((dim, dim), jnp.float32),) * seqs
    if linked:
        begin = tuple(end_state[seq] for seq in range(seqs))
    ended = lax.fori_loop(0, blocks, chain, begin)
    if linked:
        for seq in range(seqs):
            d_start[seq] = ended[seq]

    def last(step, sums):
        conv_sum, small_sum, *rims = sums
        units = spots(step)
        ats = units
        bases = [pl.multiple_of(block * STRETCH, STRETCH) for block in units]
        acts, keys, rate_sets = [], [], []
        for base in bases:
            pre = convolve(window(proj, halo, length, base, all_conv), conv)
            gate = sigmoid(pre)
            act = pre * gate
            raw = stack(act, 1, dim)
            unit = unit_rows(raw)
            acts.append((act, gate * (1.0 + pre * (1.0 - gate)), unit))
            keys.append(raw * unit)
            rate_sets.append(rates(proj[pl.ds(base, STRETCH), pl.ds(6 * dim, dim)], decay))
        nears = [
            mul_nt(jnp.concatenate([key, act[:, :dim]], axis=0), key)
            for (act, _, _), key in zip(acts, keys)
        ]
        masks = [decays(running) for _, running in rate_sets]
        d_freshes = [
            mul_tn(near[WIDE:] * upto, d_out[at])
            + mul(key * twice(jnp.exp(running[STRETCH - 1 :, 2:3] - running[:, 2:3])), chained[at])
            for near, (_, upto), at, key, (_, running) in zip(nears, masks, ats, keys, rate_sets)
        ]
        backs = [mul_tn(inv[at], d_fresh) for at, d_fresh in zip(ats, d_freshes)]
        reads = [
            stack(act, 3, dim) - mul(key * twice(jnp.exp(running[:, 2:3])), states[at])
            for (act, _, _), key, (_, running), at in zip(acts, keys, rate_sets, ats)
        ]
        to_state = [
            mul_nt(jnp.concatenate([beta * back, d_out[at]], axis=0), states[at])
            for (beta, _), back, at in zip(rate_sets, backs, ats)
        ]
        to_new = [
            mul_nt(jnp.concatenate([back, d_out[at]], axis=0), fresh[at])
            for back, at in zip(backs, ats)
        ]
        d_ends = [mul_nt(fresh[at], chained[at]) for at in ats]
        shaped = [-cross[:WIDE] * strict for cross, (strict, _) in zip(to_new, masks)]
        insides = [beta * a for (beta, _), a in zip(rate_sets, shaped)]
        d_nears = [cross[WIDE:] * upto for cross, (_, upto) in zip(to_new, masks)]
        towards = [
            mul(jnp.concatenate([inside, d_near], axis=0), key)
            for inside, d_near, key in zip(insides, d_nears, keys)
        ]
        away = [
            mul_tn(
                jnp.concatenate([inside, d_near], axis=0),
                jnp.concatenate([key, act[:, :dim]], axis=0),
            )
            for inside, d_near, key, (act, _, _) in zip(insides, d_nears, keys, acts)
        ]
        d_heres = []
        for k, (at, base) in enumerate(zip(ats, bases)):
            act, slope, unit = acts[k]
            query, key = act[:, :dim], keys[k]
            beta, running = rate_sets[k]
            small = proj[pl.ds(base, STRETCH), pl.ds(6 * dim, dim)]
            g = running[:, 2:3]
            end = g[STRETCH - 1 :]
            grown, to_go = jnp.exp(g), jnp.exp(end - g)
            back = backs[k]
            d_scaled, d_query_scaled = -to_state[k][:WIDE], to_state[k][WIDE:]
            with_inside = shaped[k] * nears[k][:WIDE]
            d_beta = jnp.sum(back * reads[k] + with_inside, axis=1, keepdims=True)
            gaps = beta * with_inside
            score_gaps = d_nears[k] * nears[k][WIDE:]
            d_query = towards[k][WIDE:] + d_query_scaled * grown
            from_start, from_end = d_scaled * twice(grown), d_ends[k] * twice(to_go)
            d_key = towards[k][:WIDE] + away[k] + from_start + from_end
            ended = jnp.sum(from_end * key, axis=1, keepdims=True)
            row_terms = jnp.sum(gaps + from_start * key, axis=1, keepdims=True) - ended
            col_terms = jnp.sum(gaps, axis=0, keepdims=True) + jnp.sum(
                score_gaps, axis=0, keepdims=True
            )
            col_terms = jnp.transpose(jnp.broadcast_to(col_terms, (8, WIDE)))[:, 0:1]
            row_terms = row_terms - col_terms
            d_g = (
                row_terms[:STRETCH]
                + row_terms[STRETCH:]
                + jnp.sum(score_gaps + d_query_scaled * grown * query, axis=1, keepdims=True)
            )
            d_end = jnp.sum(ended, axis=0, keepdims=True) + jnp.exp(end) * jnp.sum(
                jnp.sum(states[at] * chained[at], axis=0, keepdims=True), axis=1, keepdims=True
            )
            row, col = iotas(STRETCH, STRETCH)
            across = jnp.transpose(jnp.broadcast_to(d_g, (STRETCH, WIDE)))[:STRETCH]
            d_gamma = jnp.sum(jnp.where(row <= col, across, 0.0), axis=1, keepdims=True) + d_end
            lane = iotas(STRETCH, dim)[1]
            shifted = small + decay[1:2]
            d_soft = -jnp.exp(decay[0:1]) * d_gamma
            d_logit = d_soft * sigmoid(shifted)
            d_rate = jnp.where(lane == 0, d_beta[:STRETCH], d_beta[STRETCH:])
            open_beta = sigmoid(small)
            d_small = jnp.where(
                lane < 2,
                d_rate * open_beta * (1.0 - open_beta),
                jnp.where(lane == 2, d_logit, 0.0),
            )
            d_proj[pl.ds(base, STRETCH), pl.ds(6 * dim, dim)] = low(d_small)
            small_sum = small_sum + jnp.concatenate(
                [
                    jnp.sum(d_soft * softplus(shifted), axis=0, keepdims=True),
                    jnp.sum(d_logit, axis=0, keepdims=True),
                ],
                axis=0,
            )
            d_raw = unit * (d_key - key * jnp.sum(d_key * key, axis=1, keepdims=True))
            d_value = beta * back
            d_act = jnp.concatenate(
                [d_query, d_raw[:STRETCH], d_raw[STRETCH:], d_value[:STRETCH], d_value[STRETCH:]],
                axis=1,
            )
            d_heres.append(d_act * slope)
        for k, (base, d_here) in enumerate(zip(bases, d_heres)):
            rows = window(proj, halo, length, base, all_conv)
            first_row = 8 - (CONV - 1)
            conv_sum = conv_sum + jnp.concatenate(
                [
                    jnp.sum(
                        d_here * rows[first_row + tap : first_row + tap + STRETCH],
                        axis=0,
                        keepdims=True,
                    )
                    for tap in range(CONV)
                ],
                axis=0,
            )
            ahead = jnp.concatenate([d_here, rims[k % seqs]], axis=0)
            rims[k % seqs] = d_here[:8]
            total = None
            for tap in range(CONV):
                start = CONV - 1 - tap
                term = conv[tap : tap + 1] * ahead[start : start + STRETCH]
                total = term if total is None else total + term
            d_proj[pl.ds(base, STRETCH), all_conv] = low(total)
        return conv_sum, small_sum, *rims

    conv_sum, small_sum, *rims = staged(
        turns,
        last,
        (
            jnp.zeros((CONV, 5 * dim), jnp.float32),
            jnp.zeros((2, dim), jnp.float32),
        )
        + (jnp.zeros((8, 5 * dim), jnp.float32),) * seqs,
        marks_of(plan, 1, steps),
    )
    def unproject(step, total):
        at = pl.ds(pl.multiple_of(step * TOGETHER * STRETCH, STRETCH), TOGETHER * STRETCH)
        given = dot(d_proj[at], head[...], ((1,), (1,)))
        d_normed[at] = low(given)
        rows = tokens[at].astype(jnp.float32)
        scale = lax.rsqrt(jnp.mean(rows * rows, axis=1, keepdims=True) + EPS)
        return total + jnp.sum(given * (rows * scale), axis=0, keepdims=True)

    d_norm_gain[...] = staged(
        seqs * blocks // TOGETHER,
        unproject,
        jnp.zeros((1, tokens.shape[1]), jnp.float32),
        marks_of(plan, 2, steps),
    )
    if linked:
        for seq in range(seqs):
            d_first[seq] = rims[seq]
    d_conv[...] = conv_sum
    d_small_sums[...] = small_sum
    if spot is not None:
        for seq in range(seqs):
            for k in range(1, HEADS):
                from_mate(seq, spot.mate_off(k), k).wait_send()


def mixer_backward(
    proj, conv, decay, gain, kept, d_mixer, tokens, head, groups=0, number=None, link=(), jobs=(), plan=None
):
    seqs, length, _ = tokens.shape
    width = proj.shape[1]
    tokens = tokens.reshape(seqs * length, -1)
    dim = gain.shape[1]
    units = seqs * length // STRETCH
    f32, low_ = jnp.float32, jnp.bfloat16
    outs = [
        shape((seqs * length, width), low_),
        shape((CONV, 5 * dim), f32),
        shape((2, dim), f32),
        shape((1, dim), f32),
        shape(tokens.shape, low_),
        shape((1, tokens.shape[1]), f32),
    ]
    if link:
        outs += [shape((seqs, dim, dim), f32), shape((seqs, 8, 5 * dim), f32)]
    scratch = [pltpu.VMEM((units, STRETCH, dim), f32), pltpu.VMEM((units, dim, dim), f32)]
    if number:
        scratch += [pltpu.VMEM((seqs * length, dim), low_)]
        scratch += [dma(seqs, HEADS), dma(seqs, HEADS), dma(seqs)]

    def body(spot, ins, outs, scratch, steps):
        backward_body(bool(link), seqs, spot, ins, outs, scratch, steps, plan or {})

    return fused_call(
        body,
        [(a, IN_VMEM) for a in (proj, conv, decay, gain, *kept, d_mixer, tokens, head, *link)],
        [(a, IN_VMEM) for a in outs], scratch, jobs, groups, number, "mixer_backward", 60,
        mixer_cost(units),
    )


PROLOGUE_PLAN = (1, 0, 3, 1, 2, 3, 2, 0, 2, 0, 2, 0, 3, 0, 2)
EPILOGUE_PLAN = (2, 2, 2, 4, 2, 1, 1, 4, 5, 6, 2, 2, 2, 1, 3, 2, 0, 5, 2, 0, 0, 6, 2, 1, 2, 0, 5, 2, 2, 0, 6, 3, 2, 2, 0, 2, 2, 2, 4, 1, 0, 2, 3, 2)
FORWARD_PLAN = {
    (0, 0): ((0, 1), (1, 1)),
    (0, 6): ((1, 1), (0, 1), (2, 1)),
    (1, 3): ((0, 1), (1, 1)),
    (1, 4): ((1, 1),),
    (1, 5): ((0, 1),),
    (1, 6): ((0, 1), (2, 1), (0, 1)),
    (1, 7): ((2, 1),),
    (1, 8): ((2, 1),),
    (2, 0): ((0, 1),),
    (2, 4): ((2, 1),),
}
BACKWARD_PLAN = {
    (0, 0): ((1, 1), (0, 1)),
    (0, 2): ((0, 1),),
    (0, 6): ((0, 1),),
    (0, 8): ((1, 1), (0, 1)),
    (1, 0): ((0, 1),),
    (1, 1): ((0, 1),),
    (1, 2): ((0, 1),),
    (1, 4): ((0, 1),),
    (1, 5): ((1, 1),),
    (1, 6): ((0, 1),),
    (2, 2): ((0, 1),),
    (2, 6): ((0, 1), (0, 1), (1, 1)),
    (2, 7): ((0, 1),),
}
REDUCE_PLAN = (1, 0, 1, 0, 1, 1, 1, 0, 1, 1, 1, 1)
def matmul(left, right):
    return jnp.dot(left, right, preferred_element_type=jnp.float32)


def times_transposed(left, right):
    return lax.dot_general(
        left, right, (((1,), (1,)), ((), ())), preferred_element_type=jnp.float32
    )


def transposed_times(left, right):
    return lax.dot_general(
        left, right, (((0,), (0,)), ((), ())), preferred_element_type=jnp.float32
    )


def exact(left, right):
    return jnp.einsum("sij,sjk->sik", left, right, precision=lax.Precision.HIGHEST)


def norm_scale(values):
    return lax.rsqrt(jnp.mean(values * values, axis=-1, keepdims=True) + EPS)


def norm_back(values, gain, given):
    scale = norm_scale(values)
    normal = values * scale
    inner = given * gain
    return scale * (inner - normal * jnp.mean(inner * normal, axis=-1, keepdims=True)), (
        given * normal
    )


def per_device(
    block_in,
    lengths,
    norm_gains,
    w_in,
    w_small,
    conv_weight,
    decay_log,
    decay_bias,
    out_norm_gain,
    w_out,
    gate_up_weight,
    w_down,
    out_cotangent,
):
    micro, seq_count, tokens, width = block_in.shape
    seqs = micro * seq_count
    count = lax.axis_size("ctx")
    groups = lax.axis_size("rep")
    place = lax.axis_index("ctx")
    group = lax.axis_index("rep")
    teams = count // HEADS
    head = lax.rem(place, HEADS)
    team = lax.div(place, HEADS)
    mates = peers = None
    if teams > 1:
        mates = [[t * HEADS + h for h in range(HEADS)] for t in range(teams)]
        peers = [[t * HEADS + h for t in range(teams)] for h in range(HEADS)]
    dim = width // HEADS
    length = HEADS * tokens
    rows = seqs * tokens
    kinds = 2 + 2 * STEPS
    rates_of = STEPS + 1
    f32, bf16 = jnp.float32, jnp.bfloat16

    def over_teams(array):
        if teams == 1:
            return array
        return lax.all_gather(array, "ctx", axis=0, tiled=True, axis_index_groups=peers)

    places = place * tokens + lax.broadcasted_iota(jnp.int32, (seqs, tokens), 1)
    valid = (places < lengths.reshape(seqs, 1)).astype(f32).reshape(rows, 1)
    grad_out = (out_cotangent.reshape(rows, width).astype(f32) * valid).astype(bf16)

    own = width // count
    piece = own // groups
    small_block = jnp.concatenate(
        [norm_gains.reshape(-1), conv_weight.reshape(-1)]
    )
    small_block = jnp.pad(small_block, (0, -small_block.size % 128)).reshape(-1, 128)
    pieces = w_in.reshape(groups, piece, kinds, HEADS, dim).transpose(3, 0, 1, 2, 4)
    small_pieces = lax.optimization_barrier(
        jnp.stack([w_small[:, h::HEADS] for h in range(HEADS)]).reshape(HEADS, groups, piece, rates_of)
    )
    pieces = jnp.concatenate(
        [
            pieces.reshape(HEADS, groups, piece, kinds * dim),
            jnp.pad(small_pieces, ((0, 0), (0, 0), (0, 0), (0, dim - rates_of))),
        ],
        axis=3,
    )
    (w_head,), (smalls,), (sequences,), (grad_all,) = carry(
        [
            head_job(pieces, groups),
            spread_job(small_block),
            sequences_job(block_in.reshape(seqs, tokens, width)),
            rep_gather_job(grad_out, groups),
        ],
        PROLOGUE_PLAN,
        groups,
        1,
        "prologue",
    )
    sequences = sequences.reshape(seqs, length, width)
    grad_all = grad_all.reshape(groups * rows, width)
    smalls = over_teams(smalls).reshape(count, -1)
    gains = smalls[:, : 2 * own].reshape(count, 2, own).transpose(1, 0, 2).reshape(2, width)
    gains = gains.astype(f32)
    taps_at = 2 * own
    conv_all = smalls[:, taps_at : taps_at + conv_weight.size].reshape(count, CONV, -1)
    conv_all = conv_all.transpose(1, 0, 2).reshape(CONV, kinds - 1, HEADS, dim)
    conv_head = lax.dynamic_index_in_dim(conv_all, head, 2, keepdims=False)
    conv_head = conv_head.reshape(CONV, -1).astype(f32)
    w_head = over_teams(w_head).reshape(width, -1)
    hidden_own = w_down.shape[0] // groups
    hidden_units = count * hidden_own
    out_piece = lax.dynamic_index_in_dim(
        w_out.reshape(groups, piece, width), group, 0, keepdims=False
    )
    gate_up_part = lax.dynamic_index_in_dim(
        gate_up_weight.reshape(own, 2, count, groups, hidden_own), group, 3, keepdims=False
    ).reshape(own, -1)
    down_part = lax.dynamic_index_in_dim(
        w_down.reshape(groups, hidden_own, width), group, 0, keepdims=False
    )

    decay = jnp.stack(
        [
            jnp.broadcast_to(lax.dynamic_index_in_dim(decay_log, head, 0), (dim,)),
            jnp.broadcast_to(lax.dynamic_index_in_dim(decay_bias, head, 0), (dim,)),
        ]
    )
    gain = out_norm_gain.reshape(1, dim)
    head_args = (sequences, gains[:1], w_head, conv_head, decay, gain)
    link = ()
    if teams > 1:
        onward = [(c, c + HEADS) for c in range(count - HEADS)]
        tail = sequences[:, length - 8 :].reshape(seqs * 8, width).astype(f32)
        tail = (tail * norm_scale(tail) * gains[0]).astype(bf16)
        halo = lax.ppermute(matmul(tail, w_head), "ctx", onward)
        start = jnp.zeros((seqs, dim, dim), f32)
        (*_, offset, transfer), _ = mixer_forward(*head_args, link=(halo, start))
        spans = lax.all_gather((transfer, offset), "ctx", axis_index_groups=peers)
        for turn in range(teams - 1):
            start = jnp.where(turn < team, exact(spans[0][turn], start) + spans[1][turn], start)
        link = (halo, start)
    (proj, h_flat, *kept), given = mixer_forward(
        *head_args, groups, 2, link,
        [
            team_gather_job(out_piece, groups, twofold=True),
            team_gather_job(gate_up_part),
            team_gather_job(down_part),
        ],
        FORWARD_PLAN,
    )
    (w_out_full,), (gate_up_part,), (down_part,) = given
    mixer = kept[-1].reshape(rows, width)
    kept = kept[:6]
    w_out_full = over_teams(w_out_full).reshape(width, width)
    gate_up_part = over_teams(gate_up_part).reshape(width, 2 * hidden_units)
    inputs = block_in.reshape(rows, width).astype(f32)
    resid = inputs + matmul(mixer, w_out_full)

    def team_share(grad):
        grad = grad.astype(bf16)
        if teams == 1:
            return grad
        return lax.psum_scatter(
            grad, "ctx", scatter_dimension=0, tiled=True, axis_index_groups=peers
        )

    h_second = (resid * norm_scale(resid) * gains[1]).astype(bf16)
    ((h_all,),) = carry([rep_gather_job(h_second, groups)], (), groups, 3, "gather_copies")
    h_all = h_all.reshape(groups * rows, width)
    down_part = over_teams(down_part).reshape(hidden_units, width)
    gate_up = matmul(h_all, gate_up_part)
    gate, up = gate_up[:, :hidden_units], gate_up[:, hidden_units:]
    open_gate = jax.nn.sigmoid(gate)
    silu = gate * open_gate
    hidden = (silu * up).astype(bf16)
    d_hidden = times_transposed(grad_all, down_part)
    d_gate_up = jnp.concatenate(
        [d_hidden * up * (open_gate * (1.0 + gate * (1.0 - open_gate))), d_hidden * silu], axis=1
    ).astype(bf16)
    d_second = times_transposed(d_gate_up, gate_up_part).astype(bf16)
    grad_down = team_share(transposed_times(hidden, grad_all)).reshape(HEADS, hidden_own, width)
    (d_second,), (grad_down,) = carry(
        [
            rep_reduce_job(d_second.reshape(groups, rows, width), groups),
            team_reduce_job(grad_down, 1, 2, bf16),
        ],
        REDUCE_PLAN,
        groups,
        4,
        "reduce_copies",
    )
    down_parts = matmul(hidden, down_part).astype(bf16).reshape(groups, rows, width)
    grad_gate_up = transposed_times(h_all, d_gate_up)
    d_norm, gain_terms_second = norm_back(resid, gains[1], d_second)
    d_resid = grad_out.astype(f32) + d_norm
    d_branch = d_resid.astype(bf16)
    grad_out_proj = transposed_times(mixer, d_branch)
    d_mixer = times_transposed(d_branch, w_out_full).astype(bf16).reshape(seqs, tokens, width)

    grad_gate_up = team_share(grad_gate_up).reshape(HEADS, own, -1)
    grad_out_proj = team_share(grad_out_proj).reshape(HEADS, groups, piece, width)

    link = ()
    if teams > 1:
        later = jnp.zeros((seqs, dim, dim), f32)
        heads_own = lax.all_to_all(
            d_mixer.reshape(rows, HEADS, dim).transpose(1, 0, 2),
            "ctx", 0, 0, tiled=True, axis_index_groups=mates,
        )
        heads_own = heads_own.reshape(HEADS, seqs, tokens, dim).transpose(1, 0, 2, 3)
        local = mixer_backward(
            proj, conv_head, decay, gain, kept, heads_own.reshape(seqs * length, dim), sequences,
            w_head, link=(halo, later),
        )[0][6]
        locals_ = lax.all_gather(local, "ctx", axis_index_groups=peers)
        for turn in range(teams - 1, 0, -1):
            later = jnp.where(
                turn > team,
                exact(spans[0][turn].transpose(0, 2, 1), later) + locals_[turn],
                later,
            )
        link = (halo, later)
    (d_proj, grad_conv, small_sums, grad_gain, d_first, gain_sum, *rims), given = mixer_backward(
        proj, conv_head, decay, gain, kept, d_mixer, sequences, w_head, groups, 5, link,
        [
            team_reduce_job(grad_gate_up, 2, 3, bf16),
            both_reduce_job(grad_out_proj, groups),
        ],
        BACKWARD_PLAN,
    )
    (grad_gate_up,), (grad_out_proj,) = given
    if teams > 1:
        rim = lax.ppermute(rims[1], "ctx", [(c, c - HEADS) for c in range(HEADS, count)])
        spill = jnp.zeros((seqs, CONV - 1, kinds * dim - dim), f32)
        for ahead in range(1, CONV):
            spill = spill.at[:, CONV - 1 - ahead :].add(
                conv_head[CONV - 1 - ahead] * rim[:, :ahead]
            )
        d_proj = d_proj.reshape(seqs, length, -1)
        end = d_proj[:, length - CONV + 1 :, : (kinds - 1) * dim]
        d_proj = d_proj.at[:, length - CONV + 1 :, : (kinds - 1) * dim].set(
            (end.astype(f32) + spill).astype(bf16)
        )
        d_proj = d_proj.reshape(seqs * length, -1)
        d_first = times_transposed(d_proj, w_head)
        normal = sequences.reshape(seqs * length, width).astype(f32)
        gain_sum = (d_first * (normal * norm_scale(normal))).sum(axis=0)
        d_first = d_first.astype(bf16)

    grad_head = transposed_times(h_flat, d_proj[:, : kinds * dim])
    grad_small = transposed_times(d_proj[:, kinds * dim : kinds * dim + 8], h_flat)
    packed = jnp.concatenate(
        [
            jnp.stack([gain_sum.reshape(width), gain_terms_second.sum(axis=0)]).reshape(-1, dim),
            grad_small[:rates_of].reshape(-1, dim),
            grad_conv.reshape(-1, dim),
            grad_gain,
            small_sums[:, STEPS : STEPS + 1] + jnp.zeros((1, dim), f32),
        ]
    )
    packed = jnp.pad(packed, ((0, -packed.shape[0] % 8), (0, 0)))
    grad_head = team_share(grad_head)
    if teams > 1:
        packed = lax.psum(packed, "ctx", axis_index_groups=peers)
    (grad_in,), (packed,), (d_first,), (grad_gate_up,), (grad_down,), (grad_out_proj,), (down,) = carry(
        [
            deal_job(grad_head.reshape(HEADS, groups, piece, kinds * dim), groups),
            small_job(packed, groups),
            tokens_job(d_first.reshape(seqs, HEADS, tokens, width), 2),
            rep_gather_job(grad_gate_up, groups, IN_VMEM),
            rep_gather_job(grad_down, groups, IN_VMEM),
            rep_gather_job(grad_out_proj, groups, IN_VMEM),
            rep_reduce_job(down_parts, groups),
        ],
        EPILOGUE_PLAN,
        groups,
        6,
        "epilogue",
    )
    d_inputs, _ = norm_back(inputs, gains[0], d_first.reshape(rows, width))
    in_grad = (d_resid + d_inputs).astype(bf16)
    result = (valid * (resid + down)).astype(bf16)
    grad_in = grad_in.reshape(own, -1)
    grad_gate_up = grad_gate_up.reshape(groups, own, 2, count, hidden_own)
    grad_gate_up = grad_gate_up.transpose(1, 2, 3, 0, 4).reshape(own, -1)
    grad_down = grad_down.reshape(groups * hidden_own, width)
    grad_out_proj = grad_out_proj.reshape(own, width)

    def take(size):
        nonlocal packed
        part, packed = packed[:, :size], packed[:, size:]
        return part

    grad_gains = take(2 * HEADS).sum(axis=0).reshape(2, width)
    grad_small = take(rates_of * HEADS).reshape(HEADS, rates_of, width)
    grad_small = grad_small.transpose(2, 1, 0).reshape(width, rates_of * HEADS)
    grad_conv = take(CONV * (kinds - 1)).reshape(HEADS, CONV, kinds - 1, dim)
    grad_conv = grad_conv.transpose(1, 2, 0, 3).reshape(CONV, (kinds - 1) * width)
    grad_gain = take(1).sum(axis=0).reshape(dim)
    decays_sum = take(2)[:, :, 0].transpose(1, 0)

    def mine(array, axis, size):
        return lax.dynamic_slice_in_dim(array, place * size, size, axis)

    grad_gains = mine(grad_gains, 1, own)
    grad_small = mine(grad_small, 0, own)
    grad_conv = mine(grad_conv, 1, conv_weight.shape[1])
    return (
        result.reshape(block_in.shape),
        in_grad.reshape(block_in.shape),
        grad_gains,
        grad_in.astype(f32),
        grad_small,
        grad_conv,
        decays_sum[0],
        decays_sum[1],
        grad_gain,
        grad_out_proj.astype(f32),
        grad_gate_up.astype(f32),
        grad_down.astype(f32),
    )


def solution(mesh):
    placed = (
        P(None, "rep", "ctx", None),
        P(None, "rep"),
        P(None, "ctx"),
        P("ctx", None),
        P("ctx", None),
        P(None, "ctx"),
        P(),
        P(),
        P(),
        P("ctx", None),
        P("ctx", None),
        P("ctx", None),
        P(None, "rep", "ctx", None),
    )
    return jax.shard_map(
        per_device,
        mesh=mesh,
        in_specs=placed,
        out_specs=(
            P(None, "rep", "ctx", None),
            P(None, "rep", "ctx", None),
            P(None, "ctx"),
            P("ctx", None),
            P("ctx", None),
            P(None, "ctx"),
            P(),
            P(),
            P(),
            P("ctx", None),
            P("ctx", None),
            P("ctx", None),
        ),
        check_vma=False,
    )
```

time: 953 us -> 468 us (0.49)
  waiting for transfers between devices: 532 us -> 0 us
  Pallas kernels: 107 us -> 367 us
  blocking collectives: 134 us -> 0 us
  matrix products: 68.4 us -> 36.2 us
  starting transfers between devices: 14.8 us -> 0 us
  between operations: 14.7 us -> 1.68 us
    pallas_call x2 -> x6, Pallas kernels: 107 us -> 367 us  [fused_call(): pl.pallas_call(kernel, out_shape=[s for s, _ in outs] + [s for job in job...]
    reduce_scatter x6 -> x0, waiting for transfers between devices: 207 us -> none  [the longest x1 87.9 us: per_device(): lax.psum_scatter(d_first.reshape(HEADS * rows, width), 'ctx', scatter_dim...]
    psum x2 -> x0, waiting for transfers between devices: 169 us -> none  [the longest x1 126 us: per_device(): packed = lax.psum(packed, ('rep', 'ctx')).reshape(-1)]
    all_gather x7 -> x0, waiting for transfers between devices: 123 us -> none  [the longest x1 37.4 us: per_device(): down_part = lax.all_gather(down_part, 'ctx', axis=0, tiled=True)]
    all_gather x2 -> x0, blocking collectives: 78.2 us -> none  [the longest x1 69.8 us: per_device(): smalls = lax.all_gather(small_block, 'ctx', axis=0).reshape(count, -1)]
    all_to_all x2 -> x0, blocking collectives: 56.1 us -> none  [the longest x1 30.6 us: to_heads(): lax.all_to_all(split, 'ctx', 0, 0, tiled=True, axis_index_groups=mates)]
    all_to_all x2 -> x0, waiting for transfers between devices: 31.4 us -> none  [the longest x1 31.4 us: per_device(): lax.all_to_all(grad_in.reshape(HEADS, own, kinds * dim), 'ctx', 0, 0, til...]
    dot_general x4 -> x3, matrix products: 24.2 us -> 9.16 us  [matmul(): return jnp.dot(left, right, preferred_element_type=jnp.float32)]
  transfers between devices with their start and end apart: 17 -> 0, of which waited for: 14 -> 0; matrix products, arithmetic and copies ran while one was open for 12% -> 0% of each run, Pallas kernels for 11% -> 0%
where the time goes in v4:
time: 468 us; the launch traced here: 460 us
  Pallas kernels  367 us (78%)
  local copies, waits for them, and re-layouts  44.7 us (10%)
  matrix products  36.2 us (8%)
  other arithmetic  10.7 us (2%)
    pallas_call x6, Pallas kernels, fused_call(): pl.pallas_call(kernel, out_shape=[s for s, _ in outs] + [s for job in job...  367 us
    unnamed x73, local copies, waits for them, and re-layouts  22.2 us
    dot_general x5, matrix products, transposed_times(): lax.dot_general(left, right, (((0,), (0,)), ((), ())), preferred_element_...  18.4 us

profile of v4, /device:TPU:8, one launch (start us, length us, event | category | flops | bytes accessed | tf_op | source)
XLA Modules:
  0.0 460.1 jit_solution(682877989223537918)
XLA Ops:
  5.9 2.0 fusion.8.refs_3_
  7.9 1.7 copy.121
  10.2 2.7 reshape.278
  17.1 58.8 %prologue.1 = (bf16[8,4,32,896]{3,2,1,0:T(8,128)(2,1)S(1)}, bf16[8,22,128]{2,1,0:T(8,128)(2,1)S(1)}, bf16[2,8,128,1024]{3,2,1,0:T(8,128)(2,1)S(1)}, bf16[4,256,1024]{2,1,0:T(8,128)(2,1)S(1)}) custom-call(bf16[8,4,32,896]{3,2,1,0:T(8,128)(2,1)S(1)} %fusion.4.refs_0_, bf16[22,128]{1,0:T(8,128)(2,1)S(1)} %maximum_bitcast_fusion.refs_1_, ...), custom_call_target="tpu_custom_call" | custom-call | tf_op jit(solution)/shard_map/prologue/pallas_call | solution.py:407
  75.8 2.1 copy-done.3
  81.8 1.8 copy.108
  86.8 77.3 %mixer_forward.1 = (f32[2048,896]{1,0:T(8,128)}, bf16[2048,1024]{1,0:T(8,128)(2,1)}, f32[2048,128]{1,0:T(8,128)}, f32[32,128,128]{2,1,0:T(8,128)}, f32[32,128,12...) custom-call(bf16[2048,1024]{1,0:T(8,128)(2,1)} %bitcast.161, ...), custom_call_target="tpu_custom_call" | custom-call | flops 4026531840 | bytes 15728640 | tf_op jit(solution)/shard_map/mixer_forward/pallas_call | solution.py:407
  164.1 2.6 multiply_reduce_fusion.4
  166.9 20.6 %gather_copies.1 = bf16[4,256,1024]{2,1,0:T(8,128)(2,1)S(1)} custom-call(bf16[256,1024]{1,0:T(8,128)(2,1)S(1)} %multiply_convert_fusion.4.refs_0_), custom_call_target="tpu_custom_call" | custom-call | tf_op jit(solution)/shard_map/gather_copies/pallas_call | solution.py:407
  187.5 3.3 fusion.22
  190.9 3.3 multiply_convert_fusion.2
  194.2 3.2 convolution_convert_fusion.3
  199.1 3.7 convolution_convert_fusion.2
  202.8 33.3 %reduce_copies.1 = (f32[256,1024]{1,0:T(8,128)S(1)}, bf16[88,1024]{1,0:T(8,128)(2,1)S(1)}) custom-call(bf16[4,256,1024]{2,1,0:T(8,128)(2,1)S(1)} %bitcast.166, bf16[8,88,1024]{2,1,0:T(8,128)(2,1)S(1)} %bitcast.171), custom_call_target="tpu_custom_call" | custom-call | tf_op jit(solution)/shard_map/reduce_copies/pallas_call | solution.py:407
  237.6 2.1 convolution_convert_fusion.1
  239.6 4.8 %convolution_convert_fusion = bf16[1024,1408]{1,0:T(8,128)(2,1)} fusion(bf16[1024,1024]{1,0:T(8,128)(2,1)S(1)} %bitcast.165, bf16[1024,704]{0,1:T(8,128)(2,1)S(1)} %get-tuple-element.141, bf16[1024,704]{0,1:T(8,128)(2,1)S(1)} %get-tuple-element.140), kind=kOutput, calls=%fused_computation | convolution fusion | flops 2959998976 | bytes 7864320 | tf_op jit(solution)/shard_map/dot_general | solution.py:1460
  246.0 88.0 %mixer_backward.1 = (bf16[2048,896]{1,0:T(8,128)(2,1)}, f32[4,640]{1,0:T(4,128)}, f32[2,128]{1,0:T(2,128)}, f32[1,128]{1,0:T(1,128)}, bf16[2048,1024]{1,0:T(8,12...) custom-call(f32[2048,896]{1,0:T(8,128)} %get-tuple-element.51.refs_0_, ...), custom_call_target="tpu_custom_call" | custom-call | flops 4026531840 | bytes 15728640 | tf_op jit(solution)/shard_map/mixer_backward/pallas_call | solution.py:407
  334.0 3.1 fusion.14
  337.5 6.8 %fusion.5 = bf16[1024,768]{1,0:T(8,128)(2,1)S(1)} fusion(bf16[2048,1024]{1,0:T(8,128)(2,1)} %get-tuple-element.50, bf16[2048,896]{1,0:T(8,128)(2,1)} %get-tuple-element.62), kind=kOutput, calls=%fused_computation.16 | convolution fusion | flops 3222011904 | bytes 8912896 | tf_op jit(solution)/shard_map/dot_general | solution.py:1460
  344.4 88.9 %epilogue.1 = (f32[4,32,6144]{2,1,0:T(8,128)S(1)}, f32[8,64,128]{2,1,0:T(8,128)S(1)}, f32[2,128,1024]{2,1,0:T(8,128)S(1)}, bf16[4,128,1408]{2,1,0:T(8,128)(2,1)S...) custom-call(bf16[8,4,32,768]{3,2,1,0:T(8,128)(2,1)S(1)} %bitcast.170, ...), custom_call_target="tpu_custom_call" | custom-call | tf_op jit(solution)/shard_map/epilogue/pallas_call | solution.py:407
  437.4 3.0 copy.115
  440.4 3.7 copy.116
  444.1 3.4 copy.119
  455.8 3.9 copy.136
  (149 shorter events, 34.4 us)
Async XLA Ops:
  0.6 84.0 %copy-start = (bf16[352,1024]{1,0:T(8,128)(2,1)S(1)}, bf16[352,1024]{1,0:T(8,128)(2,1)}, u32[]{:S(2)}) copy-start(bf16[352,1024]{1,0:T(8,128)(2,1)} %param.24) | copy-start | bytes 2162692
  10.2 2.7 copy-start.24
  12.9 3.0 copy-start.26
  12.9 3.1 copy-start.29
  12.9 3.1 copy-start.2
  75.8 2.1 copy-start.3
  166.7 69.9 %copy-start.17 = (f32[256,1024]{1,0:T(8,128)}, f32[256,1024]{1,0:T(8,128)S(1)}, u32[]{:S(2)}) copy-start(f32[256,1024]{1,0:T(8,128)S(1)} %get-tuple-element.151) | copy-start | bytes 3145732
  166.7 20.8 %copy-start.31 = (bf16[8,128,1408]{2,1,0:T(8,128)(2,1)S(1)}, bf16[8,128,1408]{2,1,0:T(8,128)(2,1)}, u32[]{:S(2)}) copy-start(bf16[8,128,1408]{2,1,0:T(8,128)(2,1)} %get-tuple-element.60) | copy-start | bytes 8650756
  187.5 3.4 copy-start.16
  187.5 3.4 copy-start.32
  202.8 33.8 %copy-start.23 = (bf16[2,1,128,1024]{3,2,1,0:T(8,128)(2,1)S(1)}, bf16[2,1,128,1024]{3,2,1,0:T(8,128)(2,1)}, u32[]{:S(2)}) copy-start(bf16[2,1,128,1024]{3,2,1,0:T(8,128)(2,1)} %param.25) | copy-start | bytes 1572868
  237.6 6.9 %copy-start.19 = (f32[256,1024]{1,0:T(8,128)}, f32[256,1024]{1,0:T(8,128)S(1)}, u32[]{:S(2)}) copy-start(f32[256,1024]{1,0:T(8,128)S(1)} %multiply_add_fusion) | copy-start | bytes 3145732
  239.6 4.8 %copy-start.21 = (bf16[8,4,32,1024]{3,2,1,0:T(8,128)(2,1)S(1)}, bf16[8,4,32,1024]{3,2,1,0:T(8,128)(2,1)}, u32[]{:S(2)}) copy-start(bf16[8,4,32,1024]{3,2,1,0:T(8,128)(2,1)} %get-tuple-element.49) | copy-start | bytes 6291460
  334.0 3.1 copy-start.27
  334.0 3.2 copy-start.25
  334.0 3.2 copy-start.30
  334.0 3.4 copy-start.28
  337.5 6.9 %copy-start.6 = (bf16[1024,1024]{1,0:T(8,128)(2,1)S(1)}, bf16[1024,1024]{1,0:T(8,128)(2,1)}, u32[]{:S(2)}) copy-start(bf16[1024,1024]{1,0:T(8,128)(2,1)} %convolution_convert_fusion.3) | copy-start | bytes 6291460
  337.5 6.9 %copy-start.9 = (bf16[128,1408]{1,0:T(8,128)(2,1)S(1)}, bf16[128,1408]{1,0:T(8,128)(2,1)}, u32[]{:S(2)}) copy-start(bf16[128,1408]{1,0:T(8,128)(2,1)} %get-tuple-element.68.refs_3_) | copy-start | bytes 1081348
  337.5 6.9 %copy-start.14 = (bf16[32,1024]{1,0:T(8,128)(2,1)S(1)}, bf16[32,1024]{1,0:T(8,128)(2,1)}, u32[]{:S(2)}) copy-start(bf16[32,1024]{1,0:T(8,128)(2,1)} %get-tuple-element.70.refs_5_) | copy-start | bytes 196612
  447.5 1.8 copy-start.18
  447.5 2.1 copy-start.20
  449.5 2.2 copy-start.11
  454.4 5.2 %copy-start.1 = (bf16[352,1024]{1,0:T(8,128)(2,1)S(1)}, bf16[352,1024]{1,0:T(8,128)(2,1)}, u32[]{:S(2)}) copy-start(bf16[352,1024]{1,0:T(8,128)(2,1)} %param.24) | copy-start | bytes 2162692
  (9 other events, 10.2 us)

commit v5 on v4

--- a/solution.py
+++ b/solution.py
@@ -606,17 +606,44 @@
     )
 
 
-def deal_job(parts, groups):
-    heads, _, piece, cols = parts.shape
-    low_, f32 = parts.dtype, jnp.float32
+def tile_product(left, right, tile, width):
+    return low(dot(left[:, tile * 128 : (tile + 1) * 128], right[:, :width], ((0,), (0,))))
+
+
+def product_job(left, right):
+    rows, width = left.shape[1], right.shape[1]
+
+    def make(spot, ins, outs, scratch):
+        for tile in range(rows // 128):
+            outs[0][tile * 128 : (tile + 1) * 128] = tile_product(ins[0], ins[1], tile, width)
+            yield
+
+    return Job(
+        make, [left, right], [shape((rows, width), jnp.bfloat16)], (), (IN_VMEM, IN_VMEM)
+    )
+
+
+def deal_job(ins, dims, groups):
+    heads, _, piece, cols = dims
+    low_ = jnp.bfloat16
     kinds = 2 + 2 * STEPS
     dim = cols // kinds
     block = pltpu.VMEM((groups // 2, heads, piece, cols), low_)
+    made = len(ins) == 2
 
     def make(spot, ins, outs, scratch):
-        sums, others, quarter, dealt, r_send, r_recv, e_send, e_recv, g_send, g_recv, own = scratch
+        sums, others, quarter, dealt, r_send, r_recv, e_send, e_recv, g_send, g_recv, own = scratch[:11]
+        parts = ins[0]
+        if made:
+            parts = scratch[11]
+            for mate in range(heads):
+                tile = tile_product(ins[0], ins[1], mate, cols)
+                for g in range(groups):
+                    parts[mate, g] = tile[g * piece : (g + 1) * piece]
+                if mate % 2:
+                    yield
         for total in rep_reduce(
-            spot, lambda g: ins[0].at[:, g], sums, others, r_send, r_recv
+            spot, lambda g: parts.at[:, g], sums, others, r_send, r_recv
         ):
             if total is None:
                 yield
@@ -633,17 +660,18 @@
         )
         for g in range(groups):
             for h in range(heads):
-                rows = dealt[g, h].astype(f32)
+                rows = dealt[g, h]
                 for k in range(kinds):
                     at = (k * heads + h) * dim
                     outs[0][g, :, at : at + dim] = rows[:, k * dim : (k + 1) * dim]
         yield
 
     return Job(
-        make, [parts], [shape((groups, piece, heads * cols), f32)],
+        make, ins, [shape((groups, piece, heads * cols), low_)],
         [block, block, pltpu.VMEM((heads, piece, cols), low_)]
         + [pltpu.VMEM((groups, heads, piece, cols), low_)]
-        + [dma(groups), dma(groups), dma(HEADS), dma(HEADS), dma(groups), dma(groups), dma(1)],
+        + [dma(groups), dma(groups), dma(HEADS), dma(HEADS), dma(groups), dma(groups), dma(1)]
+        + ([pltpu.VMEM(dims, low_)] if made else []),
         (IN_VMEM, IN_VMEM),
     )
 
@@ -665,20 +693,39 @@
     )
 
 
-def head_job(pieces, groups):
+def head_job(w_in, w_small, groups):
+    own, width = w_in.shape
+    kinds, piece = 2 + 2 * STEPS, own // groups
+    dim = width // (kinds * HEADS)
+    rates_of = w_small.shape[1] // HEADS
+    dims = (HEADS, groups, piece, (kinds + 1) * dim)
+
     def make(spot, ins, outs, scratch):
-        e_send, e_recv, w_send, w_recv, own = scratch
+        pieces, e_send, e_recv, w_send, w_recv, local = scratch
+        row, col = iotas(w_small.shape[1], dim)
+        for h in range(HEADS):
+            chosen = low(jnp.where((row == col * HEADS + h) & (col < rates_of), 1.0, 0.0))
+            blocks = [ins[0][:, (k * HEADS + h) * dim : (k * HEADS + h + 1) * dim] for k in range(kinds)]
+            blocks.append(low(dot(ins[1][...], chosen, ((1,), (0,)))))
+            for k, block in enumerate(blocks):
+                block = block.astype(jnp.float32)
+                for g in range(groups):
+                    pieces[h, g, :, k * dim : (k + 1) * dim] = low(
+                        block[g * piece : (g + 1) * piece]
+                    )
         yield from team_exchange(
-            spot, lambda m: ins[0].at[m, spot.group], lambda m: outs[0].at[m, spot.group],
-            e_send, e_recv, own.at[0],
+            spot, lambda m: pieces.at[m, spot.group], lambda m: outs[0].at[m, spot.group],
+            e_send, e_recv, local.at[0],
         )
         yield from rep_gather(
             spot, outs[0].at[:, spot.group], lambda g: outs[0].at[:, g], w_send, w_recv, None
         )
 
     return Job(
-        make, [pieces], [shape(pieces.shape, pieces.dtype)],
-        [dma(HEADS), dma(HEADS), dma(groups), dma(groups), dma(1)],
+        make, [w_in, w_small], [shape(dims, w_in.dtype)],
+        [pltpu.VMEM(dims, w_in.dtype)]
+        + [dma(HEADS), dma(HEADS), dma(groups), dma(groups), dma(1)],
+        (IN_VMEM, ANY),
     )
 
 
@@ -1417,7 +1464,10 @@
 
 
 PROLOGUE_PLAN = (1, 0, 3, 1, 2, 3, 2, 0, 2, 0, 2, 0, 3, 0, 2)
-EPILOGUE_PLAN = (2, 2, 2, 4, 2, 1, 1, 4, 5, 6, 2, 2, 2, 1, 3, 2, 0, 5, 2, 0, 0, 6, 2, 1, 2, 0, 5, 2, 2, 0, 6, 3, 2, 2, 0, 2, 2, 2, 4, 1, 0, 2, 3, 2)
+EPILOGUE_PLAN = (
+    2, 0, 2, 2, 0, 4, 2, 2, 4, 6, 5, 2, 5, 2, 2, 1, 3, 0, 2, 1, 4, 2, 6, 2, 0, 2, 0, 1, 3, 2, 2, 2, 0, 2,
+    0, 2, 5, 0, 2, 1, 0, 6, 2, 2, 0, 3, 0, 1,
+)
 FORWARD_PLAN = {
     (0, 0): ((0, 1), (1, 1)),
     (0, 6): ((1, 1), (0, 1), (2, 1)),
@@ -1445,7 +1495,9 @@
     (2, 6): ((0, 1), (0, 1), (1, 1)),
     (2, 7): ((0, 1),),
 }
-REDUCE_PLAN = (1, 0, 1, 0, 1, 1, 1, 0, 1, 1, 1, 1)
+REDUCE_PLAN = (
+    1, 2, 0, 2, 2, 2, 1, 2, 2, 0, 1, 2, 1, 1, 2, 1, 1, 1, 1, 0,
+)
 def matmul(left, right):
     return jnp.dot(left, right, preferred_element_type=jnp.float32)
 
@@ -1529,20 +1581,9 @@
         [norm_gains.reshape(-1), conv_weight.reshape(-1)]
     )
     small_block = jnp.pad(small_block, (0, -small_block.size % 128)).reshape(-1, 128)
-    pieces = w_in.reshape(groups, piece, kinds, HEADS, dim).transpose(3, 0, 1, 2, 4)
-    small_pieces = lax.optimization_barrier(
-        jnp.stack([w_small[:, h::HEADS] for h in range(HEADS)]).reshape(HEADS, groups, piece, rates_of)
-    )
-    pieces = jnp.concatenate(
-        [
-            pieces.reshape(HEADS, groups, piece, kinds * dim),
-            jnp.pad(small_pieces, ((0, 0), (0, 0), (0, 0), (0, dim - rates_of))),
-        ],
-        axis=3,
-    )
     (w_head,), (smalls,), (sequences,), (grad_all,) = carry(
         [
-            head_job(pieces, groups),
+            head_job(w_in, w_small, groups),
             spread_job(small_block),
             sequences_job(block_in.reshape(seqs, tokens, width)),
             rep_gather_job(grad_out, groups),
@@ -1575,12 +1616,9 @@
         w_down.reshape(groups, hidden_own, width), group, 0, keepdims=False
     )
 
-    decay = jnp.stack(
-        [
-            jnp.broadcast_to(lax.dynamic_index_in_dim(decay_log, head, 0), (dim,)),
-            jnp.broadcast_to(lax.dynamic_index_in_dim(decay_bias, head, 0), (dim,)),
-        ]
-    )
+    mine_only = lax.broadcasted_iota(jnp.int32, (2, HEADS), 1) == head
+    decay = jnp.where(mine_only, jnp.stack([decay_log, decay_bias]), 0.0).sum(axis=1, keepdims=True)
+    decay = jnp.broadcast_to(decay, (2, dim))
     gain = out_norm_gain.reshape(1, dim)
     head_args = (sequences, gains[:1], w_head, conv_head, decay, gain)
     link = ()
@@ -1635,10 +1673,11 @@
     ).astype(bf16)
     d_second = times_transposed(d_gate_up, gate_up_part).astype(bf16)
     grad_down = team_share(transposed_times(hidden, grad_all)).reshape(HEADS, hidden_own, width)
-    (d_second,), (grad_down,) = carry(
+    (d_second,), (grad_down,), (grad_gate_up,) = carry(
         [
             rep_reduce_job(d_second.reshape(groups, rows, width), groups),
             team_reduce_job(grad_down, 1, 2, bf16),
+            product_job(h_all, d_gate_up),
         ],
         REDUCE_PLAN,
         groups,
@@ -1646,7 +1685,6 @@
         "reduce_copies",
     )
     down_parts = matmul(hidden, down_part).astype(bf16).reshape(groups, rows, width)
-    grad_gate_up = transposed_times(h_all, d_gate_up)
     d_norm, gain_terms_second = norm_back(resid, gains[1], d_second)
     d_resid = grad_out.astype(f32) + d_norm
     d_branch = d_resid.astype(bf16)
@@ -1703,7 +1741,6 @@
         gain_sum = (d_first * (normal * norm_scale(normal))).sum(axis=0)
         d_first = d_first.astype(bf16)
 
-    grad_head = transposed_times(h_flat, d_proj[:, : kinds * dim])
     grad_small = transposed_times(d_proj[:, kinds * dim : kinds * dim + 8], h_flat)
     packed = jnp.concatenate(
         [
@@ -1715,12 +1752,15 @@
         ]
     )
     packed = jnp.pad(packed, ((0, -packed.shape[0] % 8), (0, 0)))
-    grad_head = team_share(grad_head)
+    factors = [h_flat, d_proj]
+    if teams > 1:
+        grad_head = team_share(transposed_times(h_flat, d_proj[:, : kinds * dim]))
+        factors = [grad_head.reshape(HEADS, groups, piece, kinds * dim)]
     if teams > 1:
         packed = lax.psum(packed, "ctx", axis_index_groups=peers)
     (grad_in,), (packed,), (d_first,), (grad_gate_up,), (grad_down,), (grad_out_proj,), (down,) = carry(
         [
-            deal_job(grad_head.reshape(HEADS, groups, piece, kinds * dim), groups),
+            deal_job(factors, (HEADS, groups, piece, kinds * dim), groups),
             small_job(packed, groups),
             tokens_job(d_first.reshape(seqs, HEADS, tokens, width), 2),
             rep_gather_job(grad_gate_up, groups, IN_VMEM),
@@ -1738,7 +1778,9 @@
     result = (valid * (resid + down)).astype(bf16)
     grad_in = grad_in.reshape(own, -1)
     grad_gate_up = grad_gate_up.reshape(groups, own, 2, count, hidden_own)
-    grad_gate_up = grad_gate_up.transpose(1, 2, 3, 0, 4).reshape(own, -1)
+    grad_gate_up = lax.optimization_barrier(
+        grad_gate_up.transpose(1, 2, 3, 0, 4).reshape(own, -1)
+    )
     grad_down = grad_down.reshape(groups * hidden_own, width)
     grad_out_proj = grad_out_proj.reshape(own, width)
 

time: 468 us -> 449 us (0.959)
  matrix products: 36.2 us -> 24.3 us
  Pallas kernels: 367 us -> 359 us
    dot_general x5 -> x3, matrix products: 18.4 us -> 6.83 us  [transposed_times(): lax.dot_general(left, right, (((0,), (0,)), ((), ())), preferred_element_...]
    pallas_call x6, Pallas kernels: 367 us -> 359 us  [fused_call(): pl.pallas_call(kernel, out_shape=[s for s, _ in outs] + [s for job in job...]
    convert_element_type x2 -> x0, local copies, waits for them, and re-layouts: 6.68 us -> none  [per_device(): grad_gate_up.astype(f32)]
    unnamed x73 -> x70, local copies, waits for them, and re-layouts: 22.2 us -> 23.8 us
where the time goes in v5:
time: 449 us; the launch traced here: 440 us
  Pallas kernels  359 us (80%)
  local copies, waits for them, and re-layouts  40.4 us (9%)
  matrix products  24.3 us (5%)
  other arithmetic  14.2 us (3%)
    pallas_call x6, Pallas kernels, fused_call(): pl.pallas_call(kernel, out_shape=[s for s, _ in outs] + [s for job in job...  359 us
    unnamed x70, local copies, waits for them, and re-layouts  23.8 us
    dot_general x3, matrix products, matmul(): return jnp.dot(left, right, preferred_element_type=jnp.float32)  9.17 us

profile of v5, /device:TPU:8, one launch (start us, length us, event | category | flops | bytes accessed | tf_op | source)
XLA Modules:
  0.0 439.8 jit_solution(7671112956943568295)
XLA Ops:
  7.3 56.5 %prologue.1 = (bf16[8,4,32,896]{3,2,1,0:T(8,128)(2,1)S(1)}, bf16[8,22,128]{2,1,0:T(8,128)(2,1)S(1)}, bf16[2,8,128,1024]{3,2,1,0:T(8,128)(2,1)S(1)}, bf16[4,256,1024]{2,1,0:T(8,128)(2,1)S(1)}) custom-call(bf16[128,6144]{1,0:T(8,128)(2,1)S(1)} %copy-done.9, bf16[128,24]{1,0:T(8,128)(2,1)S(1)} %copy.47.refs_1_, ...), custom_call_target="tpu_custom_call" | custom-call | tf_op jit(solution)/shard_map/prologue/pallas_call | solution.py:407
  63.9 2.0 copy-done.5
  69.3 2.5 copy.48
  74.4 1.5 dynamic-slice_bitcast_fusion.1.refs_6_
  75.9 77.1 %mixer_forward.1 = (f32[2048,896]{1,0:T(8,128)}, bf16[2048,1024]{1,0:T(8,128)(2,1)}, f32[2048,128]{1,0:T(8,128)}, f32[32,128,128]{2,1,0:T(8,128)}, f32[32,128,12...) custom-call(bf16[2048,1024]{1,0:T(8,128)(2,1)} %bitcast.142, ...), custom_call_target="tpu_custom_call" | custom-call | flops 4026531840 | bytes 15728640 | tf_op jit(solution)/shard_map/mixer_forward/pallas_call | solution.py:407
  153.0 2.6 multiply_reduce_fusion.4
  155.7 21.1 %gather_copies.1 = bf16[4,256,1024]{2,1,0:T(8,128)(2,1)S(1)} custom-call(bf16[256,1024]{1,0:T(8,128)(2,1)S(1)} %multiply_convert_fusion.4.refs_0_), custom_call_target="tpu_custom_call" | custom-call | tf_op jit(solution)/shard_map/gather_copies/pallas_call | solution.py:407
  176.9 3.4 fusion.14
  180.3 3.0 multiply_convert_fusion.2
  183.4 3.2 convolution_convert_fusion.2
  186.6 1.7 convolution_convert_fusion.3
  189.1 3.7 convolution_convert_fusion.1
  192.8 34.2 %reduce_copies.1 = (f32[256,1024]{1,0:T(8,128)S(1)}, bf16[88,1024]{1,0:T(8,128)(2,1)S(1)}, bf16[1024,1408]{1,0:T(8,128)(2,1)S(1)}) custom-call(bf16[4,256,1024]{2,1,0:T(8,128)(2,1)S(1)} %bitcast.146, bf16[8,88,1024]{2,1,0:T(8,128)(2,1)S(1)} %bitcast.149, bf16[1024,1024]{1,0:T(8,128)(2,1)S(1)} %bitcast.141, bf16[1024,1408]{1,0:T(8,128)(2,1)S(1)} %pad_maximum_fusion.refs_3_), custom_call_target="tpu_custom_call" | custom-call | tf_op jit(solution)/shard_map/reduce_copies/pallas_call | solution.py:407
  229.0 2.1 convolution_convert_fusion
  231.6 1.5 convolution_convert_fusion.4
  233.1 87.4 %mixer_backward.1 = (bf16[2048,896]{1,0:T(8,128)(2,1)}, f32[4,640]{1,0:T(4,128)}, f32[2,128]{1,0:T(2,128)}, f32[1,128]{1,0:T(1,128)}, bf16[2048,1024]{1,0:T(8,12...) custom-call(f32[2048,896]{1,0:T(8,128)} %get-tuple-element.52.refs_0_, ...), custom_call_target="tpu_custom_call" | custom-call | flops 4026531840 | bytes 15728640 | tf_op jit(solution)/shard_map/mixer_backward/pallas_call | solution.py:407
  320.5 3.1 fusion.7
  324.0 2.0 copy-done.4
  326.0 1.6 copy-done.7
  329.5 83.1 %epilogue.1 = (bf16[4,32,6144]{2,1,0:T(8,128)(2,1)S(1)}, f32[8,64,128]{2,1,0:T(8,128)S(1)}, f32[2,128,1024]{2,1,0:T(8,128)S(1)}, bf16[4,128,1408]{2,1,0:T(8,128)...) custom-call(bf16[2048,1024]{1,0:T(8,128)(2,1)} %get-tuple-element.51.refs_0_,, ...), custom_call_target="tpu_custom_call" | custom-call | tf_op jit(solution)/shard_map/epilogue/pallas_call | solution.py:407
  416.3 2.5 copy.55
  418.8 2.6 copy.56
  421.4 3.0 copy.59
  424.3 3.4 bitcast_convert_fusion
  (116 shorter events, 33.5 us)
Async XLA Ops:
  0.6 73.1 %copy-start = (bf16[352,1024]{1,0:T(8,128)(2,1)S(1)}, bf16[352,1024]{1,0:T(8,128)(2,1)}, u32[]{:S(2)}) copy-start(bf16[352,1024]{1,0:T(8,128)(2,1)} %param.24) | copy-start | bytes 2162692
  0.7 67.2 %copy-start.28 = (f32[8]{0:T(128)S(1)}, f32[8]{0:T(128)}, u32[]{:S(2)}) copy-start(f32[8]{0:T(128)} %param.19) | copy-start | bytes 100
  0.7 67.2 %copy-start.27 = (f32[8]{0:T(128)S(1)}, f32[8]{0:T(128)}, u32[]{:S(2)}) copy-start(f32[8]{0:T(128)} %param.20) | copy-start | bytes 100
  5.9 1.4 copy-start.9
  63.9 2.0 copy-start.5
  75.9 77.1 %copy-start.3 = (bf16[2,1,128,1024]{3,2,1,0:T(8,128)(2,1)S(1)}, bf16[2,1,128,1024]{3,2,1,0:T(8,128)(2,1)}, u32[]{:S(2)}) copy-start(bf16[2,1,128,1024]{3,2,1,0:T(8,128)(2,1)} %param.13) | copy-start | bytes 1572868
  155.6 71.9 %copy-start.17 = (f32[256,1024]{1,0:T(8,128)}, f32[256,1024]{1,0:T(8,128)S(1)}, u32[]{:S(2)}) copy-start(f32[256,1024]{1,0:T(8,128)S(1)} %get-tuple-element.129) | copy-start | bytes 3145732
  155.6 21.3 %copy-start.30 = (bf16[8,128,1408]{2,1,0:T(8,128)(2,1)S(1)}, bf16[8,128,1408]{2,1,0:T(8,128)(2,1)}, u32[]{:S(2)}) copy-start(bf16[8,128,1408]{2,1,0:T(8,128)(2,1)} %get-tuple-element.61) | copy-start | bytes 8650756
  176.9 3.4 copy-start.31
  227.0 1.8 copy-start.6
  227.0 1.4 copy-start.23
  227.4 1.6 copy-start.22
  229.0 4.1 copy-start.19
  229.0 2.6 copy-start.21
  320.5 3.1 copy-start.25
  320.5 3.2 copy-start.24
  320.5 3.2 copy-start.29
  320.5 3.4 copy-start.26
  324.0 2.0 copy-start.4
  326.0 1.6 copy-start.7
  427.7 1.8 copy-start.18
  427.7 2.1 copy-start.20
  429.8 1.4 copy-start.15
  429.8 9.5 %copy-start.1 = (bf16[352,1024]{1,0:T(8,128)(2,1)S(1)}, bf16[352,1024]{1,0:T(8,128)(2,1)}, u32[]{:S(2)}) copy-start(bf16[352,1024]{1,0:T(8,128)(2,1)} %param.24) | copy-start | bytes 2162692
  (8 other events, 7.8 us)

commit v6 on v5

--- a/solution.py
+++ b/solution.py
@@ -738,6 +738,27 @@
     return Job(
         make, [block], [shape((HEADS,) + block.shape, block.dtype)], [dma(HEADS), dma(HEADS), dma(1)]
     )
+
+
+def weave(parts, piece):
+    groups, rows, width = parts.shape
+
+    def kernel(parts_ref, out):
+        for k in range(width // piece):
+            blocks = [
+                parts_ref[g, :, k * piece : (k + 1) * piece].astype(jnp.float32)
+                for g in range(groups)
+            ]
+            at = k * groups * piece
+            out[:, at : at + groups * piece] = jnp.concatenate(blocks, axis=1)
+
+    return pl.pallas_call(
+        kernel,
+        out_shape=shape((rows, groups * width), jnp.float32),
+        in_specs=[IN_VMEM],
+        out_specs=IN_VMEM,
+        name="weave",
+    )(parts)
 
 
 def carry(jobs, plan, groups, number, name, vmem=40):
@@ -1777,10 +1798,7 @@
     in_grad = (d_resid + d_inputs).astype(bf16)
     result = (valid * (resid + down)).astype(bf16)
     grad_in = grad_in.reshape(own, -1)
-    grad_gate_up = grad_gate_up.reshape(groups, own, 2, count, hidden_own)
-    grad_gate_up = lax.optimization_barrier(
-        grad_gate_up.transpose(1, 2, 3, 0, 4).reshape(own, -1)
-    )
+    grad_gate_up = weave(grad_gate_up, hidden_own)
     grad_down = grad_down.reshape(groups * hidden_own, width)
     grad_out_proj = grad_out_proj.reshape(own, width)
 

time: 449 us -> 441 us (0.982)
  local copies, waits for them, and re-layouts: 40.4 us -> 28.7 us
  Pallas kernels: 359 us -> 364 us
    unnamed x70 -> x67, local copies, waits for them, and re-layouts: 23.8 us -> 17.2 us
    pallas_call x0 -> x1, Pallas kernels: none -> 4.82 us  [weave(): pl.pallas_call(kernel, out_shape=shape((rows, groups * width), jnp.float3...]
where the time goes in v6:
time: 441 us; the launch traced here: 432 us
  Pallas kernels  364 us (83%)
  local copies, waits for them, and re-layouts  28.7 us (7%)
  matrix products  24.3 us (6%)
  other arithmetic  13.1 us (3%)
    pallas_call x6, Pallas kernels, fused_call(): pl.pallas_call(kernel, out_shape=[s for s, _ in outs] + [s for job in job...  359 us
    unnamed x67, local copies, waits for them, and re-layouts  17.2 us
    dot_general x3, matrix products, matmul(): return jnp.dot(left, right, preferred_element_type=jnp.float32)  9.18 us

profile of v6, /device:TPU:8, one launch (start us, length us, event | category | flops | bytes accessed | tf_op | source)
XLA Modules:
  0.0 431.8 jit_solution(10157207305016057780)
XLA Ops:
  5.9 1.4 copy-done.9
  7.3 56.5 %prologue.1 = (bf16[8,4,32,896]{3,2,1,0:T(8,128)(2,1)S(1)}, bf16[8,22,128]{2,1,0:T(8,128)(2,1)S(1)}, bf16[2,8,128,1024]{3,2,1,0:T(8,128)(2,1)S(1)}, bf16[4,256,1024]{2,1,0:T(8,128)(2,1)S(1)}) custom-call(bf16[128,6144]{1,0:T(8,128)(2,1)S(1)} %copy-done.9, bf16[128,24]{1,0:T(8,128)(2,1)S(1)} %copy.43.refs_1_, ...), custom_call_target="tpu_custom_call" | custom-call | tf_op jit(solution)/shard_map/prologue/pallas_call | solution.py:407
  63.9 2.0 copy-done.5
  69.3 2.5 copy.44
  74.4 1.5 dynamic-slice_bitcast_fusion.1.refs_6_
  75.9 77.1 %mixer_forward.1 = (f32[2048,896]{1,0:T(8,128)}, bf16[2048,1024]{1,0:T(8,128)(2,1)}, f32[2048,128]{1,0:T(8,128)}, f32[32,128,128]{2,1,0:T(8,128)}, f32[32,128,12...) custom-call(bf16[2048,1024]{1,0:T(8,128)(2,1)} %bitcast.138, ...), custom_call_target="tpu_custom_call" | custom-call | flops 4026531840 | bytes 15728640 | tf_op jit(solution)/shard_map/mixer_forward/pallas_call | solution.py:407
  153.0 2.6 multiply_reduce_fusion.4
  155.7 21.2 %gather_copies.1 = bf16[4,256,1024]{2,1,0:T(8,128)(2,1)S(1)} custom-call(bf16[256,1024]{1,0:T(8,128)(2,1)S(1)} %multiply_convert_fusion.4.refs_0_), custom_call_target="tpu_custom_call" | custom-call | tf_op jit(solution)/shard_map/gather_copies/pallas_call | solution.py:407
  176.9 3.4 fusion.14
  180.3 3.0 multiply_convert_fusion.2
  183.4 3.2 convolution_convert_fusion.2
  186.6 1.7 convolution_convert_fusion.3
  189.2 3.7 convolution_convert_fusion.1
  192.8 34.1 %reduce_copies.1 = (f32[256,1024]{1,0:T(8,128)S(1)}, bf16[88,1024]{1,0:T(8,128)(2,1)S(1)}, bf16[1024,1408]{1,0:T(8,128)(2,1)S(1)}) custom-call(bf16[4,256,1024]{2,1,0:T(8,128)(2,1)S(1)} %bitcast.142, bf16[8,88,1024]{2,1,0:T(8,128)(2,1)S(1)} %bitcast.145, bf16[1024,1024]{1,0:T(8,128)(2,1)S(1)} %bitcast.137, bf16[1024,1408]{1,0:T(8,128)(2,1)S(1)} %pad_maximum_fusion.refs_3_), custom_call_target="tpu_custom_call" | custom-call | tf_op jit(solution)/shard_map/reduce_copies/pallas_call | solution.py:407
  229.0 2.1 convolution_convert_fusion
  231.6 1.5 convolution_convert_fusion.4
  233.1 87.4 %mixer_backward.1 = (bf16[2048,896]{1,0:T(8,128)(2,1)}, f32[4,640]{1,0:T(4,128)}, f32[2,128]{1,0:T(2,128)}, f32[1,128]{1,0:T(1,128)}, bf16[2048,1024]{1,0:T(8,12...) custom-call(f32[2048,896]{1,0:T(8,128)} %get-tuple-element.52.refs_0_, ...), custom_call_target="tpu_custom_call" | custom-call | flops 4026531840 | bytes 15728640 | tf_op jit(solution)/shard_map/mixer_backward/pallas_call | solution.py:407
  320.6 3.1 fusion.7
  324.0 2.0 copy-done.4
  326.1 1.6 copy-done.7
  329.5 83.1 %epilogue.1 = (bf16[4,32,6144]{2,1,0:T(8,128)(2,1)S(1)}, f32[8,64,128]{2,1,0:T(8,128)S(1)}, f32[2,128,1024]{2,1,0:T(8,128)S(1)}, bf16[4,128,1408]{2,1,0:T(8,128)...) custom-call(bf16[2048,1024]{1,0:T(8,128)(2,1)} %get-tuple-element.51.refs_0_,, ...), custom_call_target="tpu_custom_call" | custom-call | tf_op jit(solution)/shard_map/epilogue/pallas_call | solution.py:407
  412.7 2.3 bitcast_convert_fusion
  414.9 4.8 %weave.1 = f32[128,5632]{1,0:T(8,128)} custom-call(bf16[4,128,1408]{2,1,0:T(8,128)(2,1)} %copy-done.10), custom_call_target="tpu_custom_call" | custom-call | tf_op jit(solution)/shard_map/weave/pallas_call | solution.py:755
  421.8 1.4 fusion.5
  (112 shorter events, 27.0 us)
Async XLA Ops:
  0.6 73.1 %copy-start = (bf16[352,1024]{1,0:T(8,128)(2,1)S(1)}, bf16[352,1024]{1,0:T(8,128)(2,1)}, u32[]{:S(2)}) copy-start(bf16[352,1024]{1,0:T(8,128)(2,1)} %param.24) | copy-start | bytes 2162692
  0.7 67.2 %copy-start.27 = (f32[8]{0:T(128)S(1)}, f32[8]{0:T(128)}, u32[]{:S(2)}) copy-start(f32[8]{0:T(128)} %param.19) | copy-start | bytes 100
  0.7 67.2 %copy-start.26 = (f32[8]{0:T(128)S(1)}, f32[8]{0:T(128)}, u32[]{:S(2)}) copy-start(f32[8]{0:T(128)} %param.20) | copy-start | bytes 100
  63.9 2.0 copy-start.5
  75.9 77.1 %copy-start.3 = (bf16[2,1,128,1024]{3,2,1,0:T(8,128)(2,1)S(1)}, bf16[2,1,128,1024]{3,2,1,0:T(8,128)(2,1)}, u32[]{:S(2)}) copy-start(bf16[2,1,128,1024]{3,2,1,0:T(8,128)(2,1)} %param.13) | copy-start | bytes 1572868
  155.5 71.9 %copy-start.16 = (f32[256,1024]{1,0:T(8,128)}, f32[256,1024]{1,0:T(8,128)S(1)}, u32[]{:S(2)}) copy-start(f32[256,1024]{1,0:T(8,128)S(1)} %get-tuple-element.129) | copy-start | bytes 3145732
  155.6 21.3 %copy-start.29 = (bf16[8,128,1408]{2,1,0:T(8,128)(2,1)S(1)}, bf16[8,128,1408]{2,1,0:T(8,128)(2,1)}, u32[]{:S(2)}) copy-start(bf16[8,128,1408]{2,1,0:T(8,128)(2,1)} %get-tuple-element.61) | copy-start | bytes 8650756
  176.9 3.4 copy-start.30
  227.0 1.8 copy-start.6
  227.4 1.6 copy-start.21
  229.0 4.1 copy-start.18
  229.0 2.6 copy-start.20
  320.5 3.1 copy-start.24
  320.5 3.2 copy-start.23
  320.5 3.2 copy-start.28
  320.6 3.4 copy-start.25
  324.0 2.0 copy-start.4
  326.1 1.6 copy-start.7
  412.6 2.3 copy-start.10
  412.6 2.3 copy-start.12
  412.6 2.3 copy-start.13
  419.8 1.8 copy-start.17
  419.8 2.1 copy-start.19
  421.8 9.5 %copy-start.1 = (bf16[352,1024]{1,0:T(8,128)(2,1)S(1)}, bf16[352,1024]{1,0:T(8,128)(2,1)}, u32[]{:S(2)}) copy-start(bf16[352,1024]{1,0:T(8,128)(2,1)} %param.24) | copy-start | bytes 2162692
  (7 other events, 8.4 us)
